TPU v7x, 128 devices: a whole 4x4x4 slice. The times are simulated.
128 devices in a mesh: docs: 16 (over y, x_lo, core), vocab: 8 (over z, x_hi).
Axes of the slice: x: 4 (x_hi: 2, x_lo: 2; x = x_hi * 2 + x_lo), y: 4, z: 4, core: 2. Of those that a mesh axis runs over, the one named last changes fastest.
Arguments:
- doc_topics: bfloat16 [32768, 256], P('docs'), may hold values from 0.099609375 to 10
- word_topics: bfloat16 [65536, 256], P('vocab'), may hold values from 0.099609375 to 10
- word_weights: float32 [65536], P('vocab'), may hold values from 1 to 10
- tile_pairs: int32 [16, 8, 96], P('docs', 'vocab'), may hold values from 0 to 255, as said below
- tile_counts: bfloat16 [16, 8, 96, 512, 128], P('docs', 'vocab'), may hold values from 0 to 3
- tile_load: int32 [16, 8], P('docs', 'vocab'), may hold values from 1 to 96, as said below
Outputs:
- doc_next: float32 [32768, 256], P('docs')
- word_next: float32 [65536, 256], P(('vocab', 'docs'))
Inputs may be any that keep to these rules, and one draw needn't show every extreme that they name: `tile_pairs`: A device's entries are distinct; entry p names document block p // 64 and word block p % 64 of the device's own documents and words. Only the first tile_load slots of a device's list hold its tiles; later slots hold entries and frequencies that are no tiles. Some device has exactly 96 tiles.
All inputs are finite; a program needn't handle non-finite values.
Results may differ from a plain program's by a relative error of at most 0.00095.
Values may be sent and summed in bfloat16 or wider, within the bound.
No kernel may reach another device: no remote copies, remote signals or barrier semaphores. Data moves between devices by JAX's collectives and lax.ppermute only.
A program may use at most 128 MiB of HBM per device.

v0:
```python
import jax
import jax.numpy as jnp
from jax import lax
from jax.sharding import PartitionSpec as P

prior_doc = 0.5
prior_word = 0.01


def tile_terms(weighted, doc_rows, word_rows):
    predicted = lax.dot_general(
        doc_rows, word_rows, (((1,), (1,)), ((), ())), preferred_element_type=jnp.float32
    )
    count_ratio = (weighted.astype(jnp.float32) / predicted).astype(jnp.bfloat16)
    doc_terms = jnp.dot(count_ratio, word_rows, preferred_element_type=jnp.float32)
    word_terms = lax.dot_general(
        count_ratio, doc_rows, (((0,), (0,)), ((), ())), preferred_element_type=jnp.float32
    )
    return (doc_terms, word_terms)


def add_rows(total, start, addend):
    current = lax.dynamic_slice_in_dim(total, start, addend.shape[0], 0)
    return lax.dynamic_update_slice_in_dim(total, current + addend, start, 0)


def weigh_tile(frequencies, weight_table, tile_pair, blocks):
    weight_rows = lax.dynamic_index_in_dim(weight_table, tile_pair % blocks, 0, keepdims=False)
    return (frequencies.astype(jnp.float32) * weight_rows[None, :]).astype(jnp.bfloat16)


def run_tiles(tile_total, fetch_tile, doc_source, word_topics, doc_part, word_part, blocks):

    def tile_step(tile_slot, running):
        doc_acc, word_acc = running
        tile_pair, weighted = fetch_tile(tile_slot)
        tile_docs, tile_words = weighted.shape
        doc_start = tile_pair // blocks * tile_docs
        word_start = tile_pair % blocks * tile_words
        doc_rows = lax.dynamic_slice_in_dim(doc_source, doc_start, tile_docs, 0)
        word_rows = lax.dynamic_slice_in_dim(word_topics, word_start, tile_words, 0)
        doc_terms, word_terms = tile_terms(weighted, doc_rows, word_rows)
        return (add_rows(doc_acc, doc_start, doc_terms), add_rows(word_acc, word_start, word_terms))

    return lax.fori_loop(0, tile_total, tile_step, (doc_part, word_part))


def on_device(doc_topics, word_topics, word_weights, tile_pairs, tile_counts, tile_load):
    pair_list = tile_pairs[0, 0]
    counts_all = tile_counts[0, 0]
    own_load = tile_load[0, 0]
    tile_words = counts_all.shape[2]
    blocks = word_topics.shape[0] // tile_words
    weight_table = word_weights.reshape(blocks, tile_words)
    doc_zero = jnp.zeros(doc_topics.shape, jnp.float32)
    word_part = jnp.zeros(word_topics.shape, jnp.float32)

    def own_tile(tile_slot):
        tile_pair = pair_list[tile_slot]
        return (tile_pair, weigh_tile(counts_all[tile_slot], weight_table, tile_pair, blocks))

    doc_part, word_part = run_tiles(
        own_load, own_tile, doc_topics, word_topics, doc_zero, word_part, blocks
    )
    doc_sums = lax.psum(doc_part, "vocab")
    doc_scaled = doc_topics.astype(jnp.float32) * doc_sums + prior_doc
    doc_next = doc_topics.shape[1] * doc_scaled / jnp.sum(doc_scaled, axis=1, keepdims=True)
    row_count = word_topics.shape[0] // lax.axis_size("docs")
    docs_index = lax.axis_index("docs")
    word_sums = lax.psum_scatter(word_part, "docs", scatter_dimension=0, tiled=True)
    own_words = lax.dynamic_slice_in_dim(word_topics, docs_index * row_count, row_count, 0)
    word_scaled = own_words.astype(jnp.float32) * word_sums + prior_word
    column = lax.psum(jnp.sum(word_scaled, axis=0), ("docs", "vocab"))
    vocab_total = word_topics.shape[0] * lax.axis_size("vocab")
    word_next = vocab_total * word_scaled / column[None, :]
    return (doc_next, word_next)


def solution(mesh):
    placed = (
        P("docs", None),
        P("vocab", None),
        P("vocab"),
        P("docs", "vocab", None),
        P("docs", "vocab", None, None, None),
        P("docs", "vocab"),
    )
    return jax.shard_map(
        on_device,
        mesh=mesh,
        in_specs=placed,
        out_specs=(P("docs", None), P(("vocab", "docs"), None)),
        check_vma=False,
    )
```

profile of v0, /device:TPU:0, one launch (start us, length us, event | category | flops | bytes accessed | tf_op | source)
XLA Modules:
  0.0 1095.6 jit_solution(4643388116260689129)
XLA Ops:
  8.2 3.8 broadcast_in_dim.10
  12.0 826.7 %while.14 = (s32[]{:T(128)}, f32[2048,256]{1,0:T(8,128)S(1)}, f32[8192,256]{1,0:T(8,128)}, s32[]{:T(128)}, s32[96]{0:T(128)S(1)}, /*index=5*/bf16[96,512,128]{2,...) while((s32[]{:T(128)}, f32[2048,256]{1,0:T(8,128)S(1)}, ...), condition=%wide.region_1.2_spmd, body=%wide.region_0.1_spmd.sunk | while | flops 101220384 | bytes 2492484 | solution.py:45
  27.4 1.8 fusion.35
  53.2 1.8 fusion.35
  61.8 1.8 fusion.35
  70.4 1.8 fusion.35
  87.6 1.8 fusion.35
  96.2 1.8 fusion.35
  104.8 1.8 fusion.35
  113.4 1.8 fusion.35
  122.1 1.8 fusion.35
  139.3 1.8 fusion.35
  156.5 1.8 fusion.35
  182.3 1.8 fusion.35
  190.9 1.8 fusion.35
  208.1 1.8 fusion.35
  216.7 1.8 fusion.35
  225.3 1.8 fusion.35
  233.9 1.8 fusion.35
  259.7 1.8 fusion.35
  268.3 1.8 fusion.35
  276.9 1.8 fusion.35
  285.5 1.8 fusion.35
  302.7 1.8 fusion.35
  328.6 1.8 fusion.35
  337.2 1.8 fusion.35
  345.8 1.8 fusion.35
  354.4 1.8 fusion.35
  380.2 1.8 fusion.35
  388.8 1.8 fusion.35
  397.4 1.8 fusion.35
  406.0 1.8 fusion.35
  423.2 1.8 fusion.35
  431.8 1.8 fusion.35
  483.4 1.8 fusion.35
  492.0 1.8 fusion.35
  500.6 1.8 fusion.35
  526.4 1.8 fusion.35
  535.1 1.8 fusion.35
  552.3 1.8 fusion.35
  560.9 1.8 fusion.35
  569.5 1.8 fusion.35
  578.1 1.8 fusion.35
  586.7 1.8 fusion.35
  595.3 1.8 fusion.35
  621.1 1.8 fusion.35
  629.7 1.8 fusion.35
  638.3 1.8 fusion.35
  646.9 1.8 fusion.35
  672.7 1.8 fusion.35
  689.9 1.8 fusion.35
  707.2 1.8 fusion.35
  715.8 1.8 fusion.35
  741.6 1.8 fusion.35
  758.8 1.8 fusion.35
  801.8 1.8 fusion.35
  810.4 1.8 fusion.35
  819.0 1.8 fusion.35
  827.7 1.8 fusion.35
  836.3 1.8 fusion.35
  840.6 176.0 %all-reduce.2.cloned.1.call-done = f32[2048,256]{1,0:T(8,128)} async-done(((f32[2048,256]{1,0:T(8,128)}), f32[2048,256]{1,0:T(8,128)}) %all-reduce.2.cloned.1.call-update) | async-done | bytes 2097168 | tf_op jit(solution)/shard_map/psum | solution.py:65
  1016.7 2.1 fusion.12
  1021.8 64.4 %psum.15 = f32[256]{0:T(256)S(1)} all-reduce(f32[256]{0:T(256)S(1)} %fusion.13), channel_id=1, replica_groups=mesh['docs'=16,'vocab'=8] {'docs','vocab'}, use_global_device_ids=true, to_apply=%region_6.7 | all-reduce | flops 256 | bytes 2048 | tf_op jit(solution)/shard_map/psum | solution.py:73
  1086.2 2.0 multiply_divide_fusion.1
  (438 shorter events, 410.1 us)
Async XLA Ops:
  8.0 1008.7 %all-reduce.2.cloned.1.call-start = ((), (), s32[]{:S(2)}) async-start(), calls=%async_computation.1 | async-start | bytes 4194304 | tf_op jit(solution)/shard_map/psum | solution.py:65
  8.2 3.8 copy-start.1
  8.2 3.8 copy-start.3
  838.7 1.3 copy-start
  840.1 180.5 %reduce-scatter.2.cloned.1.call-start = ((), (), s32[]{:S(2)}) async-start(), calls=%async_computation.2 | async-start | bytes 8912896 | tf_op jit(solution)/shard_map/reduce_scatter | solution.py:70
  1016.6 2.2 copy-start.2
Sparse Core Ops, SparseCore 0:
  840.2 176.4 all-reduce.1
Sparse Core Ops, SparseCore 1:
  842.9 162.7 reduce-scatter.1
where the time goes:
time: 1110 us; the launch traced here: 1100 us
  matrix products  386 us (35%)
  loops' own time  318 us (29%)
  waiting for transfers between devices  177 us (16%)
  local copies, waits for them, and re-layouts  129 us (12%)
  blocking collectives  64.4 us (6%)
  between operations  15.5 us (1%)
    another operation x1, loops' own time, run_tiles(): return lax.fori_loop(0, tile_total, tile_step, (doc_part, word_part))  318 us
    psum x1, waiting for transfers between devices, on_device(): doc_sums = lax.psum(doc_part, 'vocab')  176 us
    dot_general x96, matrix products, tile_terms(): lax.dot_general(count_ratio, doc_rows, (((0,), (0,)), ((), ())), preferre...  172 us
    dot_general x96, matrix products, tile_terms(): lax.dot_general(doc_rows, word_rows, (((1,), (1,)), ((), ())), preferred_...  113 us
    dot_general x96, matrix products, tile_terms(): jnp.dot(count_ratio, word_rows, preferred_element_type=jnp.float32)  101 us
    mul x96, local copies, waits for them, and re-layouts, weigh_tile(): frequencies.astype(jnp.float32) * weight_rows[None, :]  66.8 us
    psum x1, blocking collectives, on_device(): column = lax.psum(jnp.sum(word_scaled, axis=0), ('docs', 'vocab'))  64.4 us
    dynamic_slice x96, local copies, waits for them, and re-layouts, own_tile(): tile_pair = pair_list[tile_slot]  56.3 us
  transfers between devices with their start and end apart: 2, of which 1 were waited for; matrix products, arithmetic and copies ran while one was open for 0% of the time, Pallas kernels for 0%

commit v1 on v0

v1 whole, which is shorter than its diff:
```python
import functools

import jax
import jax.numpy as jnp
from jax import lax
from jax.experimental import pallas as pl
from jax.experimental.pallas import tpu as pltpu
from jax.sharding import PartitionSpec as P

prior_doc = 0.5
prior_word = 0.01
SLOTS = 4


def tiles_kernel(
    pairs_ref,
    load_ref,
    doc_hbm,
    word_hbm,
    weights_ref,
    counts_hbm,
    doc_out,
    word_out,
    doc_rows,
    word_rows,
    counts_buf,
    first_slot,
    second_slot,
    item_doc,
    pending,
    topics_sem,
    counts_sem,
):
    tile_docs, tile_words = counts_hbm.shape[1:]
    blocks = word_hbm.shape[0] // tile_words
    doc_blocks = doc_hbm.shape[0] // tile_docs
    load = load_ref[0]

    doc_copy = pltpu.make_async_copy(doc_hbm, doc_rows, topics_sem.at[0])
    word_copy = pltpu.make_async_copy(word_hbm, word_rows, topics_sem.at[1])
    doc_copy.start()
    word_copy.start()

    for b in range(doc_blocks):
        pending[b] = -1

    def sort_slot(s, made):
        b = pairs_ref[s] // blocks
        waiting = pending[b]
        first_slot[made] = waiting
        second_slot[made] = s
        item_doc[made] = b
        pending[b] = jnp.where(waiting >= 0, -1, s)
        return made + jnp.where(waiting >= 0, 1, 0)

    made = lax.fori_loop(0, load, sort_slot, 0)
    for b in range(doc_blocks):
        waiting = pending[b]
        first_slot[made] = waiting
        second_slot[made] = -1
        item_doc[made] = b
        made = made + jnp.where(waiting >= 0, 1, 0)

    def copies(item):
        ring = lax.rem(item, SLOTS)
        first = first_slot[item]
        second = second_slot[item]
        second = jnp.where(second >= 0, second, first)
        return (
            pltpu.make_async_copy(
                counts_hbm.at[first], counts_buf.at[ring, 0], counts_sem.at[ring, 0]
            ),
            pltpu.make_async_copy(
                counts_hbm.at[second], counts_buf.at[ring, 1], counts_sem.at[ring, 1]
            ),
        )

    def start(item):
        for copy in copies(item):
            copy.start()

    for ahead in range(SLOTS - 1):

        @pl.when(ahead < made)
        def _():
            start(ahead)

    doc_out[...] = jnp.zeros_like(doc_out)
    word_out[...] = jnp.zeros_like(word_out)
    doc_copy.wait()
    word_copy.wait()

    def run_item(item, carry):
        @pl.when(item + SLOTS - 1 < made)
        def _():
            start(item + SLOTS - 1)

        ring = lax.rem(item, SLOTS)
        first = first_slot[item]
        second = second_slot[item]
        paired = second >= 0
        first_block = lax.rem(pairs_ref[first], blocks)
        second_block = lax.rem(pairs_ref[jnp.where(paired, second, first)], blocks)
        doc_at = pl.ds(pl.multiple_of(item_doc[item] * tile_docs, tile_docs), tile_docs)
        first_at = pl.ds(pl.multiple_of(first_block * tile_words, tile_words), tile_words)
        second_at = pl.ds(pl.multiple_of(second_block * tile_words, tile_words), tile_words)
        words = jnp.concatenate([word_rows[first_at, :], word_rows[second_at, :]], axis=0)
        docs = doc_rows[doc_at, :]
        weight = jnp.concatenate(
            [
                weights_ref[pl.ds(first_block, 1), :],
                weights_ref[pl.ds(second_block, 1), :] * jnp.where(paired, 1.0, 0.0),
            ],
            axis=1,
        )
        for copy in copies(item):
            copy.wait()
        predicted = lax.dot_general(
            docs, words, (((1,), (1,)), ((), ())), preferred_element_type=jnp.float32
        )
        counts = jnp.concatenate([counts_buf[ring, 0], counts_buf[ring, 1]], axis=1)
        weighted = (counts.astype(jnp.float32) * weight).astype(jnp.bfloat16)
        ratio = (weighted.astype(jnp.float32) / predicted).astype(jnp.bfloat16)
        doc_out[doc_at, :] += jnp.dot(ratio, words, preferred_element_type=jnp.float32)
        terms = lax.dot_general(
            ratio, docs, (((0,), (0,)), ((), ())), preferred_element_type=jnp.float32
        )
        word_out[first_at, :] += terms[:tile_words]
        word_out[second_at, :] += terms[tile_words:]
        return carry

    lax.fori_loop(0, made, run_item, 0)


def run_tiles(pair_list, own_load, doc_topics, word_topics, weight_table, counts_all):
    slots = pair_list.shape[0]
    tile_docs, tile_words = counts_all.shape[1:]
    doc_blocks = doc_topics.shape[0] // tile_docs
    items = slots + doc_blocks + 8
    return pl.pallas_call(
        tiles_kernel,
        out_shape=(
            jax.ShapeDtypeStruct(doc_topics.shape, jnp.float32),
            jax.ShapeDtypeStruct(word_topics.shape, jnp.float32),
        ),
        in_specs=[
            pl.BlockSpec(memory_space=pltpu.SMEM),
            pl.BlockSpec(memory_space=pltpu.SMEM),
            pl.BlockSpec(memory_space=pl.ANY),
            pl.BlockSpec(memory_space=pl.ANY),
            pl.BlockSpec(memory_space=pltpu.VMEM),
            pl.BlockSpec(memory_space=pl.ANY),
        ],
        out_specs=(
            pl.BlockSpec(memory_space=pltpu.VMEM),
            pl.BlockSpec(memory_space=pltpu.VMEM),
        ),
        scratch_shapes=[
            pltpu.VMEM(doc_topics.shape, doc_topics.dtype),
            pltpu.VMEM(word_topics.shape, word_topics.dtype),
            pltpu.VMEM((SLOTS, 2, tile_docs, tile_words), counts_all.dtype),
            pltpu.SMEM((items,), jnp.int32),
            pltpu.SMEM((items,), jnp.int32),
            pltpu.SMEM((items,), jnp.int32),
            pltpu.SMEM((doc_blocks,), jnp.int32),
            pltpu.SemaphoreType.DMA((2,)),
            pltpu.SemaphoreType.DMA((SLOTS, 2)),
        ],
        compiler_params=pltpu.CompilerParams(vmem_limit_bytes=48 << 20),
        name="tiles",
    )(pair_list, own_load, doc_topics, word_topics, weight_table, counts_all)


def on_device(doc_topics, word_topics, word_weights, tile_pairs, tile_counts, tile_load):
    counts_all = tile_counts[0, 0]
    tile_words = counts_all.shape[2]
    blocks = word_topics.shape[0] // tile_words
    weight_table = word_weights.reshape(blocks, tile_words)
    doc_part, word_part = run_tiles(
        tile_pairs[0, 0], tile_load[0], doc_topics, word_topics, weight_table, counts_all
    )
    doc_sums = lax.psum(doc_part, "vocab")
    doc_scaled = doc_topics.astype(jnp.float32) * doc_sums + prior_doc
    doc_next = doc_topics.shape[1] * doc_scaled / jnp.sum(doc_scaled, axis=1, keepdims=True)
    row_count = word_topics.shape[0] // lax.axis_size("docs")
    docs_index = lax.axis_index("docs")
    word_sums = lax.psum_scatter(word_part, "docs", scatter_dimension=0, tiled=True)
    own_words = lax.dynamic_slice_in_dim(word_topics, docs_index * row_count, row_count, 0)
    word_scaled = own_words.astype(jnp.float32) * word_sums + prior_word
    column = lax.psum(jnp.sum(word_scaled, axis=0), ("docs", "vocab"))
    vocab_total = word_topics.shape[0] * lax.axis_size("vocab")
    word_next = vocab_total * word_scaled / column[None, :]
    return (doc_next, word_next)


def solution(mesh):
    placed = (
        P("docs", None),
        P("vocab", None),
        P("vocab"),
        P("docs", "vocab", None),
        P("docs", "vocab", None, None, None),
        P("docs", "vocab"),
    )
    return jax.shard_map(
        on_device,
        mesh=mesh,
        in_specs=placed,
        out_specs=(P("docs", None), P(("vocab", "docs"), None)),
        check_vma=False,
    )
```

time: 1110 us -> 307 us (0.28); the launches traced: 1100 us -> 306 us
  matrix products: 386 us -> 0 us
  loops' own time: 318 us -> 0 us
  local copies, waits for them, and re-layouts: 129 us -> 2.77 us
  Pallas kernels: 0 us -> 31 us
    dot_general x288 -> x0, matrix products: 386 us -> none  [the longest x96 172 us: tile_terms(): lax.dot_general(count_ratio, doc_rows, (((0,), (0,)), ((), ())), preferre...]
    another operation x1 -> x0, loops' own time: 318 us -> none  [run_tiles(): return lax.fori_loop(0, tile_total, tile_step, (doc_part, word_part))]
    mul x96 -> x0, local copies, waits for them, and re-layouts: 66.8 us -> none  [weigh_tile(): frequencies.astype(jnp.float32) * weight_rows[None, :]]
    dynamic_slice x96 -> x0, local copies, waits for them, and re-layouts: 56.3 us -> none  [own_tile(): tile_pair = pair_list[tile_slot]]
    pallas_call x0 -> x1, Pallas kernels: none -> 31 us  [run_tiles(): pl.pallas_call(tiles_kernel, out_shape=(jax.ShapeDtypeStruct(doc_topics.s...]
  transfers between devices with their start and end apart: 2 -> 2, of which waited for: 1 -> 1; matrix products, arithmetic and copies ran while one was open for 0% -> 1% of each run, Pallas kernels for 0% -> 0%
where the time goes in v1:
time: 307 us; the launch traced here: 306 us
  waiting for transfers between devices  185 us (60%)
  blocking collectives  64.4 us (21%)
  Pallas kernels  31 us (10%)
  between operations  16.2 us (5%)
  other arithmetic  7.03 us (2%)
    psum x1, waiting for transfers between devices, on_device(): doc_sums = lax.psum(doc_part, 'vocab')  184 us
    psum x1, blocking collectives, on_device(): column = lax.psum(jnp.sum(word_scaled, axis=0), ('docs', 'vocab'))  64.4 us
    pallas_call x1, Pallas kernels, run_tiles(): pl.pallas_call(tiles_kernel, out_shape=(jax.ShapeDtypeStruct(doc_topics.s...  31 us
  transfers between devices with their start and end apart: 2, of which 1 were waited for; matrix products, arithmetic and copies ran while one was open for 1% of the time, Pallas kernels for 0%

profile of v1, /device:TPU:0, one launch (start us, length us, event | category | flops | bytes accessed | tf_op | source)
XLA Modules:
  0.0 306.2 jit_solution(7450960241153541722)
XLA Ops:
  8.0 0.0 all-reduce.2.cloned.1.call-start
  8.7 0.0 copy-start
  8.7 1.2 copy-done
  9.9 0.0 copy-start.2
  9.9 0.8 copy-done.2
  10.7 0.0 copy-start.3
  10.7 0.7 copy-done.3
  11.3 31.0 %tiles.1 = (f32[2048,256]{1,0:T(8,128)}, f32[8192,256]{1,0:T(8,128)}) custom-call(s32[96]{0:T(128)S(1)} %bitcast.6, s32[1]{0:T(128)} %bitcast.4.load_ref, bf16[2048,256]{1,0:T(8,128)(2,1)S(1)} %copy-done, bf16[8192,256]{1,0:T(8,128)(2,1)} %word_hbm.1, f32[64,128]{1,0:T(8,128)S(1)} %bitcast.5, bf16[96,512,128]{2,1,0:T(8,128)(2,1)} %bitcast.7), custom_call_target="tpu_custom_call" | custom-call | tf_op jit(solution)/shard_map/tiles/pallas_call | solution.py:140
  42.3 0.0 all-reduce.2.cloned.1.call-update
  42.3 0.0 reduce-scatter.2.cloned.1.call-start
  42.4 0.0 copy-start.1
  42.4 0.5 reduce-scatter.2.cloned.1.call-update
  42.9 184.3 %all-reduce.2.cloned.1.call-done = f32[2048,256]{1,0:T(8,128)} async-done(((f32[2048,256]{1,0:T(8,128)}), f32[2048,256]{1,0:T(8,128)}) %all-reduce.2.cloned.1.call-update) | async-done | bytes 2097168 | tf_op jit(solution)/shard_map/psum | solution.py:182
  227.2 0.0 copy-done.1
  227.2 0.0 copy-start.4
  227.2 2.1 fusion
  229.3 0.1 copy-done.4
  229.4 1.7 multiply_divide_fusion
  231.2 0.0 reduce-scatter.2.cloned.1.call-done
  231.2 1.2 fusion.1
  232.4 64.4 %psum.15 = f32[256]{0:T(256)S(1)} all-reduce(f32[256]{0:T(256)S(1)} %fusion.1), channel_id=1, replica_groups=mesh['docs'=16,'vocab'=8] {'docs','vocab'}, use_global_device_ids=true, to_apply=%region_4.0 | all-reduce | flops 256 | bytes 2048 | tf_op jit(solution)/shard_map/psum | solution.py:190
  296.8 2.0 multiply_divide_fusion.1
Async XLA Ops:
  8.0 219.2 %all-reduce.2.cloned.1.call-start = ((), (), s32[]{:S(2)}) async-start(), calls=%async_computation.1 | async-start | bytes 4194304 | tf_op jit(solution)/shard_map/psum | solution.py:182
  8.7 1.2 copy-start
  9.9 0.8 copy-start.2
  10.7 0.7 copy-start.3
  42.3 188.8 %reduce-scatter.2.cloned.1.call-start = ((), (), s32[]{:S(2)}) async-start(), calls=%async_computation.2 | async-start | bytes 8912896 | tf_op jit(solution)/shard_map/reduce_scatter | solution.py:187
  42.4 184.8 %copy-start.1 = (bf16[2048,256]{1,0:T(8,128)(2,1)S(1)}, bf16[2048,256]{1,0:T(8,128)(2,1)}, u32[]{:S(2)}) copy-start(bf16[2048,256]{1,0:T(8,128)(2,1)} %doc_hbm.1) | copy-start | bytes 3145732
  227.2 2.2 copy-start.4
Sparse Core Ops, SparseCore 0:
  42.5 184.7 all-reduce.1
Sparse Core Ops, SparseCore 1:
  45.2 171.0 reduce-scatter.1

commit v2 on v1

--- a/solution.py
+++ b/solution.py
@@ -1,5 +1,3 @@
-import functools
-
 import jax
 import jax.numpy as jnp
 from jax import lax
@@ -10,17 +8,27 @@
 prior_doc = 0.5
 prior_word = 0.01
 SLOTS = 4
+N_Y, N_X_LO, N_CORE = 4, 2, 2
+N_Z, N_X_HI = 4, 2
+WORD_SCALE = 2.0**-7
+DOC_SCALE = 2.0**-8
 
 
 def tiles_kernel(
     pairs_ref,
     load_ref,
+    docs_index_ref,
+    vocab_index_ref,
     doc_hbm,
     word_hbm,
     weights_ref,
     counts_hbm,
-    doc_out,
-    word_out,
+    doc_parts_out,
+    keep_out,
+    send_out,
+    column_out,
+    doc_sums,
+    word_sums,
     doc_rows,
     word_rows,
     counts_buf,
@@ -30,11 +38,23 @@
     pending,
     topics_sem,
     counts_sem,
+    sums_sem,
 ):
     tile_docs, tile_words = counts_hbm.shape[1:]
     blocks = word_hbm.shape[0] // tile_words
     doc_blocks = doc_hbm.shape[0] // tile_docs
     load = load_ref[0]
+    y, own_core = docs_index_ref[0] // (N_X_LO * N_CORE), lax.rem(docs_index_ref[0], N_CORE)
+    z = vocab_index_ref[0] // N_X_HI
+    dest_blocks = blocks // (N_Y * N_X_LO * N_CORE)
+
+    def word_place(block):
+        dest = block // dest_blocks
+        core = lax.rem(dest, N_CORE)
+        x_lo = lax.rem(dest // N_CORE, N_X_LO)
+        step = lax.rem(dest // (N_CORE * N_X_LO) - y + N_Y, N_Y)
+        other = jnp.where(core == own_core, 0, 1)
+        return ((other * N_Y + step) * N_X_LO + x_lo) * dest_blocks + lax.rem(block, dest_blocks)
 
     doc_copy = pltpu.make_async_copy(doc_hbm, doc_rows, topics_sem.at[0])
     word_copy = pltpu.make_async_copy(word_hbm, word_rows, topics_sem.at[1])
@@ -85,8 +105,8 @@
         def _():
             start(ahead)
 
-    doc_out[...] = jnp.zeros_like(doc_out)
-    word_out[...] = jnp.zeros_like(word_out)
+    doc_sums[...] = jnp.zeros_like(doc_sums)
+    word_sums[...] = jnp.zeros_like(word_sums)
     doc_copy.wait()
     word_copy.wait()
 
@@ -121,41 +141,73 @@
         counts = jnp.concatenate([counts_buf[ring, 0], counts_buf[ring, 1]], axis=1)
         weighted = (counts.astype(jnp.float32) * weight).astype(jnp.bfloat16)
         ratio = (weighted.astype(jnp.float32) / predicted).astype(jnp.bfloat16)
-        doc_out[doc_at, :] += jnp.dot(ratio, words, preferred_element_type=jnp.float32)
+        doc_step = lax.rem(item_doc[item] - z + N_Z, N_Z)
+        doc_to = pl.ds(pl.multiple_of(doc_step * tile_docs, tile_docs), tile_docs)
+        doc_sums[doc_to, :] += jnp.dot(ratio, words, preferred_element_type=jnp.float32)
         terms = lax.dot_general(
             ratio, docs, (((0,), (0,)), ((), ())), preferred_element_type=jnp.float32
         )
-        word_out[first_at, :] += terms[:tile_words]
-        word_out[second_at, :] += terms[tile_words:]
+        for block, part in ((first_block, terms[:tile_words]), (second_block, terms[tile_words:])):
+            to = pl.multiple_of(word_place(block) * tile_words, tile_words)
+            word_sums[pl.ds(to, tile_words), :] += part
         return carry
 
     lax.fori_loop(0, made, run_item, 0)
 
-
-def run_tiles(pair_list, own_load, doc_topics, word_topics, weight_table, counts_all):
+    outgoing = []
+    rows = word_sums.shape[0] // (N_CORE * N_Y)
+    for n, out in enumerate((keep_out, send_out)):
+        for step in range(N_Y):
+            outgoing.append((word_sums.at[pl.ds((n * N_Y + step) * rows, rows)], out[step]))
+    for step in range(N_Z):
+        outgoing.append((doc_sums.at[pl.ds(step * tile_docs, tile_docs)], doc_parts_out[step]))
+    outgoing = [
+        pltpu.make_async_copy(source, target, sums_sem.at[n])
+        for n, (source, target) in enumerate(outgoing)
+    ]
+    for copy in outgoing:
+        copy.start()
+    column = jnp.zeros((1, doc_rows.shape[1]), jnp.float32)
+    for step in range(N_Z):
+        at = pl.multiple_of(lax.rem(z + step, N_Z) * tile_docs, tile_docs)
+        topics = doc_rows[pl.ds(at, tile_docs), :].astype(jnp.float32)
+        sums = doc_sums[pl.ds(step * tile_docs, tile_docs), :]
+        column = column + jnp.sum(topics * sums, axis=0, keepdims=True)
+    column_out[...] = column
+    for copy in outgoing:
+        copy.wait()
+
+
+def run_tiles(
+    pair_list, own_load, docs_index, vocab_index, doc_topics, word_topics, weight_table, counts_all
+):
     slots = pair_list.shape[0]
     tile_docs, tile_words = counts_all.shape[1:]
+    topics = doc_topics.shape[1]
     doc_blocks = doc_topics.shape[0] // tile_docs
     items = slots + doc_blocks + 8
+    doc_part = jax.ShapeDtypeStruct((doc_topics.shape[0] // N_Z, topics), jnp.float32)
+    word_part = jax.ShapeDtypeStruct((word_topics.shape[0] // (N_CORE * N_Y), topics), jnp.float32)
+    smem = pl.BlockSpec(memory_space=pltpu.SMEM)
+    hbm = pl.BlockSpec(memory_space=pl.ANY)
     return pl.pallas_call(
         tiles_kernel,
         out_shape=(
-            jax.ShapeDtypeStruct(doc_topics.shape, jnp.float32),
-            jax.ShapeDtypeStruct(word_topics.shape, jnp.float32),
+            (doc_part,) * N_Z,
+            (word_part,) * N_Y,
+            (word_part,) * N_Y,
+            jax.ShapeDtypeStruct((1, topics), jnp.float32),
         ),
-        in_specs=[
-            pl.BlockSpec(memory_space=pltpu.SMEM),
-            pl.BlockSpec(memory_space=pltpu.SMEM),
-            pl.BlockSpec(memory_space=pl.ANY),
-            pl.BlockSpec(memory_space=pl.ANY),
-            pl.BlockSpec(memory_space=pltpu.VMEM),
-            pl.BlockSpec(memory_space=pl.ANY),
-        ],
+        in_specs=[smem] * 4 + [hbm, hbm, pl.BlockSpec(memory_space=pltpu.VMEM), hbm],
         out_specs=(
-            pl.BlockSpec(memory_space=pltpu.VMEM),
+            (hbm,) * N_Z,
+            (hbm,) * N_Y,
+            (hbm,) * N_Y,
             pl.BlockSpec(memory_space=pltpu.VMEM),
         ),
         scratch_shapes=[
+            pltpu.VMEM(doc_topics.shape, jnp.float32),
+            pltpu.VMEM(word_topics.shape, jnp.float32),
             pltpu.VMEM(doc_topics.shape, doc_topics.dtype),
             pltpu.VMEM(word_topics.shape, word_topics.dtype),
             pltpu.VMEM((SLOTS, 2, tile_docs, tile_words), counts_all.dtype),
@@ -165,31 +217,140 @@
             pltpu.SMEM((doc_blocks,), jnp.int32),
             pltpu.SemaphoreType.DMA((2,)),
             pltpu.SemaphoreType.DMA((SLOTS, 2)),
+            pltpu.SemaphoreType.DMA((N_Z + 2 * N_Y,)),
         ],
         compiler_params=pltpu.CompilerParams(vmem_limit_bytes=48 << 20),
         name="tiles",
-    )(pair_list, own_load, doc_topics, word_topics, weight_table, counts_all)
+    )(
+        pair_list,
+        own_load,
+        docs_index,
+        vocab_index,
+        doc_topics,
+        word_topics,
+        weight_table,
+        counts_all,
+    )
+
+
+def moves(axis, size, move):
+    return lambda value: lax.ppermute(value, axis, [(n, move(n) % size) for n in range(size)])
+
+
+def to_half(value):
+    return value.astype(jnp.float16)
+
+
+def to_float(value):
+    return value.astype(jnp.float32)
 
 
 def on_device(doc_topics, word_topics, word_weights, tile_pairs, tile_counts, tile_load):
+    n_docs, n_vocab = lax.axis_size("docs"), lax.axis_size("vocab")
+    docs_index, vocab_index = lax.axis_index("docs"), lax.axis_index("vocab")
+    x_lo = docs_index // N_CORE % N_X_LO
+    z, x_hi = vocab_index // N_X_HI, vocab_index % N_X_HI
+    to_core = moves("docs", n_docs, lambda n: n ^ 1)
+    to_x_lo = moves("docs", n_docs, lambda n: n ^ N_CORE)
+    y_up = moves("docs", n_docs, lambda n: n + N_X_LO * N_CORE)
+    y_down = moves("docs", n_docs, lambda n: n - N_X_LO * N_CORE)
+    to_x_hi = moves("vocab", n_vocab, lambda n: n ^ 1)
+    z_up = moves("vocab", n_vocab, lambda n: n + N_X_HI)
+    z_down = moves("vocab", n_vocab, lambda n: n - N_X_HI)
+
     counts_all = tile_counts[0, 0]
     tile_words = counts_all.shape[2]
     blocks = word_topics.shape[0] // tile_words
     weight_table = word_weights.reshape(blocks, tile_words)
-    doc_part, word_part = run_tiles(
-        tile_pairs[0, 0], tile_load[0], doc_topics, word_topics, weight_table, counts_all
-    )
-    doc_sums = lax.psum(doc_part, "vocab")
-    doc_scaled = doc_topics.astype(jnp.float32) * doc_sums + prior_doc
-    doc_next = doc_topics.shape[1] * doc_scaled / jnp.sum(doc_scaled, axis=1, keepdims=True)
-    row_count = word_topics.shape[0] // lax.axis_size("docs")
-    docs_index = lax.axis_index("docs")
-    word_sums = lax.psum_scatter(word_part, "docs", scatter_dimension=0, tiled=True)
+    doc_parts, keep, send, column = run_tiles(
+        tile_pairs[0, 0],
+        tile_load[0],
+        docs_index.reshape(1),
+        vocab_index.reshape(1),
+        doc_topics,
+        word_topics,
+        weight_table,
+        counts_all,
+    )
+
+    y_across = moves("docs", n_docs, lambda n: n + 2 * N_X_LO * N_CORE)
+    z_across = moves("vocab", n_vocab, lambda n: n + 2 * N_X_HI)
+    meet = lambda *values: lax.optimization_barrier(values)
+    word_rows = keep[0].shape[0] // N_X_LO
+    doc_rows = doc_parts[0].shape[0] // N_X_HI
+
+    part = [piece * DOC_SCALE for piece in doc_parts]
+    word_far = to_core(send[2])
+    doc_up = z_up(to_half(part[2][:doc_rows]))
+    doc_down = z_down(to_half(part[2][doc_rows:]))
+    column = column + to_core(column)
+    word_far, doc_up, doc_down, column = meet(word_far, doc_up, doc_down, column)
+
+    far = (keep[2] + word_far) * WORD_SCALE
+    word_up = y_up(to_half(far[:word_rows]))
+    word_down = y_down(to_half(far[word_rows:]))
+    from_core = {step: to_core(send[step]) for step in (1, 3, 0)}
+    doc_below = z_up(
+        to_half(jnp.concatenate([part[1][:doc_rows] + to_float(doc_up), part[1][doc_rows:]]))
+    )
+    doc_above = z_down(
+        to_half(jnp.concatenate([part[3][:doc_rows], part[3][doc_rows:] + to_float(doc_down)]))
+    )
+    column = column + to_x_lo(column)
+    column = column + to_x_hi(column)
+    word_up, word_down, from_core[1], from_core[3], from_core[0], doc_below, doc_above, column = meet(
+        word_up, word_down, from_core[1], from_core[3], from_core[0], doc_below, doc_above, column
+    )
+
+    near = {step: (keep[step] + from_core[step]) * WORD_SCALE for step in (1, 3, 0)}
+    word_below = y_up(
+        to_half(jnp.concatenate([near[1][:word_rows] + to_float(word_up), near[1][word_rows:]]))
+    )
+    word_above = y_down(
+        to_half(jnp.concatenate([near[3][:word_rows], near[3][word_rows:] + to_float(word_down)]))
+    )
+    doc_pair = part[0] + to_float(doc_below) + to_float(doc_above)
+    doc_mine = lax.dynamic_slice_in_dim(doc_pair, x_hi * doc_rows, doc_rows, 0)
+    doc_other = lax.dynamic_slice_in_dim(doc_pair, (1 - x_hi) * doc_rows, doc_rows, 0)
+    doc_sums = (doc_mine + to_float(to_x_hi(to_half(doc_other)))) / DOC_SCALE
+    own_docs = lax.dynamic_slice_in_dim(doc_topics, vocab_index * doc_rows, doc_rows, 0)
+    doc_scaled = own_docs.astype(jnp.float32) * doc_sums + prior_doc
+    doc_block = to_half(
+        doc_topics.shape[1] * doc_scaled / jnp.sum(doc_scaled, axis=1, keepdims=True)
+    )
+    doc_far = to_x_hi(doc_block)
+    column = column + y_up(column)
+    column = column + y_across(column)
+    word_below, word_above, doc_block, doc_far, column = meet(
+        word_below, word_above, doc_block, doc_far, column
+    )
+
+    word_pair = near[0] + to_float(word_below) + to_float(word_above)
+    word_mine = lax.dynamic_slice_in_dim(word_pair, x_lo * word_rows, word_rows, 0)
+    word_other = lax.dynamic_slice_in_dim(word_pair, (1 - x_lo) * word_rows, word_rows, 0)
+    word_far = to_x_lo(to_half(word_other))
+    doc_here = jnp.concatenate(
+        [
+            jnp.where(x_hi == 0, doc_block, doc_far),
+            jnp.where(x_hi == 0, doc_far, doc_block),
+        ]
+    )
+    doc_below, doc_above = z_up(doc_here), z_down(doc_here)
+    column = column + z_up(column)
+    column = column + z_across(column)
+    word_far, doc_below, doc_above, column = meet(word_far, doc_below, doc_above, column)
+
+    low_across, high_across = z_up(doc_below[:doc_rows]), z_down(doc_above[doc_rows:])
+    word_sums = (word_mine + to_float(word_far)) / WORD_SCALE
+    vocab_total = word_topics.shape[0] * n_vocab
+    row_count = word_topics.shape[0] // n_docs
     own_words = lax.dynamic_slice_in_dim(word_topics, docs_index * row_count, row_count, 0)
     word_scaled = own_words.astype(jnp.float32) * word_sums + prior_word
-    column = lax.psum(jnp.sum(word_scaled, axis=0), ("docs", "vocab"))
-    vocab_total = word_topics.shape[0] * lax.axis_size("vocab")
-    word_next = vocab_total * word_scaled / column[None, :]
+    word_next = vocab_total * word_scaled / (column + vocab_total * prior_word)
+    by_step = (doc_here, doc_above, jnp.concatenate([low_across, high_across]), doc_below)
+    doc_next = jnp.concatenate(
+        [to_float(lax.select_n((place - z) % N_Z, *by_step)) for place in range(N_Z)]
+    )
     return (doc_next, word_next)
 
 

time: 307 us -> 115 us (0.37)
  waiting for transfers between devices: 185 us -> 33.3 us
  blocking collectives: 64.4 us -> 0 us
  starting transfers between devices: 0.08 us -> 43.7 us
  between operations: 16.2 us -> 1.56 us
  Pallas kernels: 31 us -> 19.5 us
  other arithmetic: 7.03 us -> 13 us
    psum x1 -> x0, waiting for transfers between devices: 184 us -> none  [on_device(): doc_sums = lax.psum(doc_part, 'vocab')]
    psum x1 -> x0, blocking collectives: 64.4 us -> none  [on_device(): column = lax.psum(jnp.sum(word_scaled, axis=0), ('docs', 'vocab'))]
    ppermute x0 -> x26, starting transfers between devices: none -> 43.7 us  [moves(): lax.ppermute(value, axis, [(n, move(n) % size) for n in range(size)])]
    ppermute x0 -> x26, waiting for transfers between devices: none -> 33.3 us  [moves(): lax.ppermute(value, axis, [(n, move(n) % size) for n in range(size)])]
    pallas_call x1, Pallas kernels: 31 us -> 19.5 us  [run_tiles(): pl.pallas_call(tiles_kernel, out_shape=((doc_part,) * N_Z, (word_part,) *...]
  transfers between devices with their start and end apart: 2 -> 26, of which waited for: 1 -> 10; matrix products, arithmetic and copies ran while one was open for 1% -> 9% of each run, Pallas kernels for 0% -> 0%
where the time goes in v2:
time: 115 us; the launch traced here: 114 us
  starting transfers between devices  43.7 us (38%)
  waiting for transfers between devices  33.3 us (29%)
  Pallas kernels  19.5 us (17%)
  other arithmetic  13 us (11%)
  local copies, waits for them, and re-layouts  3.18 us (3%)
  between operations  1.56 us (1%)
    ppermute x26, starting transfers between devices, moves(): lax.ppermute(value, axis, [(n, move(n) % size) for n in range(size)])  43.7 us
    ppermute x26, waiting for transfers between devices, moves(): lax.ppermute(value, axis, [(n, move(n) % size) for n in range(size)])  33.3 us
    pallas_call x1, Pallas kernels, run_tiles(): pl.pallas_call(tiles_kernel, out_shape=((doc_part,) * N_Z, (word_part,) *...  19.5 us
  transfers between devices with their start and end apart: 26, of which 10 were waited for; matrix products, arithmetic and copies ran while one was open for 9% of the time, Pallas kernels for 0%

profile of v2, /device:TPU:0, one launch (start us, length us, event | category | flops | bytes accessed | tf_op | source)
XLA Modules:
  0.0 114.2 jit_solution(17873155440435472535)
XLA Ops:
  1.3 0.7 copy-done
  2.0 0.7 copy-done.1
  2.7 19.5 %tiles.1 = (f32[512,256]{1,0:T(8,128)S(1)}, f32[512,256]{1,0:T(8,128)S(1)}, f32[512,256]{1,0:T(8,128)S(1)}, f32[512,256]{1,0:T(8,128)S(1)}, f32[1024,256]{1,0:T(...) custom-call(s32[96]{0:T(128)S(1)} %bitcast.9, ...), custom_call_target="tpu_custom_call" | custom-call | tf_op jit(solution)/shard_map/tiles/pallas_call | solution.py:193
  22.2 0.1 collective-permute-start
  22.2 0.5 collective-permute-start.3
  22.7 0.1 multiply_convert_fusion.1
  22.8 0.1 fusion.6
  22.9 17.6 %collective-permute-start.1 = (f16[256,256]{1,0:T(8,128)(2,1)S(1)}, f16[256,256]{1,0:T(8,128)(2,1)S(1)}, u32[]{:S(2)}, u32[]{:S(2)}) collective-permute-start(f16[256,256]{1,0:T(8,128)(2,1)S(1)} %get-tuple-element.86), channel_id=1, source_target_pairs={{0,2},{1,3},{2,4},{3,5},{4,6},{5,7},{6,0},{7,1},{8,10},{9,11},{10,... | collective-permute-start | bytes 393224 | tf_op jit(solution)/shard_map/ppermute | solution.py:237
  40.5 0.2 collective-permute-start.6
  40.7 0.0 collective-permute-done.3
  40.8 0.4 collective-permute-start.7
  41.2 2.7 %collective-permute-done.1 = f16[256,256]{1,0:T(8,128)(2,1)S(1)} collective-permute-done((f16[256,256]{1,0:T(8,128)(2,1)S(1)}, f16[256,256]{1,0:T(8,128)(2,1)S(1)}, u32[]{:S(2)}, u32[]{:S(2)}) %collective-permute-start.1) | collective-permute-done | bytes 131104 | tf_op jit(solution)/shard_map/ppermute | solution.py:237
  43.9 2.2 %collective-permute-done.2 = f16[256,256]{1,0:T(8,128)(2,1)S(1)} collective-permute-done((f16[256,256]{1,0:T(8,128)(2,1)S(1)}, f16[256,256]{1,0:T(8,128)(2,1)S(1)}, u32[]{:S(2)}, u32[]{:S(2)}) %collective-permute-start.2) | collective-permute-done | bytes 131104 | tf_op jit(solution)/shard_map/ppermute | solution.py:237
  46.1 0.0 collective-permute-done
  46.1 0.0 collective-permute-start.11
  46.1 0.1 slice_convert_fusion.2
  46.1 0.1 pad_maximum_fusion.3
  46.2 1.6 %collective-permute-start.10 = (f16[512,256]{1,0:T(8,128)(2,1)S(1)}, f16[512,256]{1,0:T(8,128)(2,1)}, u32[]{:S(2)}, u32[]{:S(2)}) collective-permute-start(f16[512,256]{1,0:T(8,128)(2,1)S(1)} %pad_maximum_fusion.3), channel_id=1, source_target_pairs={{0,6},{1,7},{2,0},{3,1},{4,2},{5,3},{6,4},{7,5},{8,14},{9,15},{10,... | collective-permute-start | bytes 786440 | tf_op jit(solution)/shard_map/ppermute | solution.py:237
  47.8 0.2 multiply_convert_fusion
  47.9 0.9 fusion.5
  48.8 0.1 fusion.3
  48.9 0.7 collective-permute-done.11
  49.6 5.4 %collective-permute-start.12 = (f32[1,256]{1,0:T(1,128)S(1)}, f32[1,256]{1,0:T(1,128)S(1)}, u32[]{:S(2)}, u32[]{:S(2)}) collective-permute-start(f32[1,256]{1,0:T(1,128)S(1)} %add.126), channel_id=1, source_target_pairs={{0,1},{1,0},{2,3},{3,2},{4,5},{5,4},{6,7},{7,6},{8,9},{9,8},{10,11... | collective-permute-start | bytes 3080 | tf_op jit(solution)/shard_map/ppermute | solution.py:237
  55.1 0.8 pad_maximum_fusion.2
  55.8 0.2 collective-permute-start.9
  56.1 0.0 collective-permute-done.7
  56.1 0.0 collective-permute-start.4
  56.1 0.5 collective-permute-done.12
  56.6 2.7 %collective-permute-start.5 = (f16[512,256]{1,0:T(8,128)(2,1)}, f16[512,256]{1,0:T(8,128)(2,1)S(1)}, u32[]{:S(2)}, u32[]{:S(2)}) collective-permute-start(f16[512,256]{1,0:T(8,128)(2,1)} %get-tuple-element.81), channel_id=1, source_target_pairs={{0,96},{8,104},{16,112},{24,120},{32,0},{40,8},{48,16},{56,24},{64... | collective-permute-start | bytes 786440 | tf_op jit(solution)/shard_map/ppermute | solution.py:237
  59.3 0.0 collective-permute-done.8
  59.3 0.0 collective-permute-done.10
  59.3 4.9 %collective-permute-done.9 = f16[512,256]{1,0:T(8,128)(2,1)} collective-permute-done((f16[512,256]{1,0:T(8,128)(2,1)}, f16[512,256]{1,0:T(8,128)(2,1)}, u32[]{:S(2)}, u32[]{:S(2)}) %collective-permute-start.9) | collective-permute-done | bytes 262176 | tf_op jit(solution)/shard_map/ppermute | solution.py:237
  64.3 0.7 copy-done.2
  65.0 1.2 %convert_add_fusion.1 = f32[512,256]{1,0:T(8,128)S(1)} fusion(f16[512,256]{1,0:T(8,128)(2,1)} %collective-permute-done.10, f16[512,256]{1,0:T(8,128)(2,1)} %collective-permute-done.9, f32[512,256]{1,0:T(8,128)S(1)} %get-tuple-element.55), kind=kLoop, calls=%fused_computation.15 | loop fusion | flops 655360 | bytes 1572864 | tf_op jit(solution)/shard_map/add | solution.py:312
  66.2 2.5 %collective-permute-start.15 = (f16[256,256]{1,0:T(8,128)(2,1)S(1)}, f16[256,256]{1,0:T(8,128)(2,1)S(1)}, u32[]{:S(2)}, u32[]{:S(2)}) collective-permute-start(f16[256,256]{1,0:T(8,128)(2,1)S(1)} %dynamic-slice_convert_fusion.1), channel_id=1, source_target_pairs={{0,1},{1,0},{2,3},{3,2},{4,5},{5,4},{6,7},{7,6},{8,9},{9,8},{10,11... | collective-permute-start | bytes 393224 | tf_op jit(solution)/shard_map/ppermute | solution.py:237
  68.7 2.1 %add_multiply_fusion = (f32[1024,256]{1,0:T(8,128)S(1)}, f32[1024,256]{1,0:T(8,128)S(1)}) fusion(f32[1024,256]{1,0:T(8,128)} %get-tuple-element.52, f32[1024,256]{1,0:T(8,128)} %collective-permute-done.7, f32[1024,256]{1,0:T(8,128)S(1)} %get-tuple-element.36, f32[1024,256]{1,0:T(8,128)} %collective-permute-done.6), kind=kLoop, calls=%fused_computation.2 | loop fusion | flops 1048576 | bytes 6291456 | tf_op jit(solution)/shard_map/mul | solution.py:305
  70.8 0.1 slice_convert_fusion
  71.0 0.1 pad_maximum_fusion.1
  71.1 1.3 %collective-permute-start.14 = (f16[1024,256]{1,0:T(8,128)(2,1)S(1)}, f16[1024,256]{1,0:T(8,128)(2,1)}, u32[]{:S(2)}, u32[]{:S(2)}) collective-permute-start(f16[1024,256]{1,0:T(8,128)(2,1)S(1)} %pad_maximum_fusion.1), channel_id=1, source_target_pairs={{0,96},{8,104},{16,112},{24,120},{32,0},{40,8},{48,16},{56,24},{64... | collective-permute-start | bytes 1572872 | tf_op jit(solution)/shard_map/ppermute | solution.py:237
  72.4 0.1 fusion.1
  72.5 0.1 pad_maximum_fusion
  72.7 0.9 collective-permute-start.13
  73.5 1.0 fusion.4
  74.6 1.0 divide_convert_fusion
  75.6 2.1 %collective-permute-start.16 = (f16[256,256]{1,0:T(8,128)(2,1)S(1)}, f16[256,256]{1,0:T(8,128)(2,1)S(1)}, u32[]{:S(2)}, u32[]{:S(2)}) collective-permute-start(f16[256,256]{1,0:T(8,128)(2,1)S(1)} %divide_convert_fusion), channel_id=1, source_target_pairs={{0,1},{1,0},{2,3},{3,2},{4,5},{5,4},{6,7},{7,6},{8,9},{9,8},{10,11... | collective-permute-start | bytes 393224 | tf_op jit(solution)/shard_map/ppermute | solution.py:237
  77.7 6.6 %collective-permute-done.17 = f32[1,256]{1,0:T(1,128)S(1)} collective-permute-done((f32[1,256]{1,0:T(1,128)S(1)}, f32[1,256]{1,0:T(1,128)S(1)}, u32[]{:S(2)}, u32[]{:S(2)}) %collective-permute-start.17) | collective-permute-done | bytes 1056 | tf_op jit(solution)/shard_map/ppermute | solution.py:237
  84.3 0.2 collective-permute-start.18
  84.5 4.9 %collective-permute-done.18 = f32[1,256]{1,0:T(1,128)S(1)} collective-permute-done((f32[1,256]{1,0:T(1,128)S(1)}, f32[1,256]{1,0:T(1,128)S(1)}, u32[]{:S(2)}, u32[]{:S(2)}) %collective-permute-start.18) | collective-permute-done | bytes 1056 | tf_op jit(solution)/shard_map/ppermute | solution.py:237
  89.4 0.1 broadcast_select_fusion.1
  89.5 0.1 pad_maximum_fusion.4
  89.5 0.3 collective-permute-start.20
  89.9 3.0 %collective-permute-start.21 = (f16[512,256]{1,0:T(8,128)(2,1)S(1)}, f16[512,256]{1,0:T(8,128)(2,1)S(1)}, u32[]{:S(2)}, u32[]{:S(2)}) collective-permute-start(f16[512,256]{1,0:T(8,128)(2,1)S(1)} %pad_maximum_fusion.4), channel_id=1, source_target_pairs={{0,6},{1,7},{2,0},{3,1},{4,2},{5,3},{6,4},{7,5},{8,14},{9,15},{10,... | collective-permute-start | bytes 786440 | tf_op jit(solution)/shard_map/ppermute | solution.py:237
  92.8 1.8 %convert_add_fusion = f32[1024,256]{1,0:T(8,128)S(1)} fusion(f16[1024,256]{1,0:T(8,128)(2,1)} %collective-permute-done.14, f16[1024,256]{1,0:T(8,128)(2,1)} %collective-permute-done.13, f32[1024,256]{1,0:T(8,128)S(1)} %get-tuple-element.61, f32[1024,256]{1,0:T(8,128)} %collective-permute-done.8), kind=kLoop, calls=%fused_computation.1 | loop fusion | flops 1572864 | bytes 4194304 | tf_op jit(solution)/shard_map/add | solution.py:328
  94.7 1.2 %collective-permute-start.19 = (f16[512,256]{1,0:T(8,128)(2,1)S(1)}, f16[512,256]{1,0:T(8,128)(2,1)S(1)}, u32[]{:S(2)}, u32[]{:S(2)}) collective-permute-start(f16[512,256]{1,0:T(8,128)(2,1)S(1)} %dynamic-slice_convert_fusion), channel_id=1, source_target_pairs={{0,16},{8,24},{16,0},{24,8},{32,48},{40,56},{48,32},{56,40},{64,80... | collective-permute-start | bytes 786440 | tf_op jit(solution)/shard_map/ppermute | solution.py:237
  95.9 0.1 collective-permute-start.22
  96.0 4.7 %collective-permute-done.22 = f32[1,256]{1,0:T(1,128)S(1)} collective-permute-done((f32[1,256]{1,0:T(1,128)S(1)}, f32[1,256]{1,0:T(1,128)S(1)}, u32[]{:S(2)}, u32[]{:S(2)}) %collective-permute-start.22) | collective-permute-done | bytes 1056 | tf_op jit(solution)/shard_map/ppermute | solution.py:237
  100.7 5.1 %collective-permute-done.23 = f32[1,256]{1,0:T(1,128)S(1)} collective-permute-done((f32[1,256]{1,0:T(1,128)S(1)}, f32[1,256]{1,0:T(1,128)S(1)}, u32[]{:S(2)}, u32[]{:S(2)}) %collective-permute-start.23) | collective-permute-done | bytes 1056 | tf_op jit(solution)/shard_map/ppermute | solution.py:237
  105.8 0.1 collective-permute-start.24
  105.9 3.3 %collective-permute-start.25 = (f16[256,256]{1,0:T(8,128)(2,1)S(1)}, f16[256,256]{1,0:T(8,128)(2,1)S(1)}, u32[]{:S(2)}, u32[]{:S(2)}) collective-permute-start(f16[256,256]{1,0:T(8,128)(2,1)S(1)} %slice.63), channel_id=1, source_target_pairs={{0,6},{1,7},{2,0},{3,1},{4,2},{5,3},{6,4},{7,5},{8,14},{9,15},{10,... | collective-permute-start | bytes 393224 | tf_op jit(solution)/shard_map/ppermute | solution.py:237
  109.2 1.9 %multiply_divide_fusion = f32[512,256]{1,0:T(8,128)} fusion(f16[512,256]{1,0:T(8,128)(2,1)S(1)} %collective-permute-done.19, f32[1024,256]{1,0:T(8,128)S(1)} %convert_add_fusion, s32[]{:T(128)S(6)} %select_n.224, f32[256]{0:T(256)S(1)} %bitcast.11, bf16[8192,256]{1,0:T(8,128)(2,1)} %word_hbm.1, s32[]{:T(128)S(6)} %select_n.223), kind=kLoop, calls=%fused_computation.13 | loop fusion | flops 1048576 | bytes 1573896 | tf_op jit(solution)/shard_map/div | solution.py:349
  111.1 1.0 collective-permute-done.24
  112.1 0.2 select_select_fusion.2
  112.3 0.3 select_select_fusion.3
  112.6 1.5 %maximum_convert_fusion = f32[2048,256]{1,0:T(8,128)} fusion(f16[512,256]{1,0:T(8,128)(2,1)S(1)} %get-tuple-element.71, f16[512,256]{1,0:T(8,128)(2,1)S(1)} %get-tuple-element.72, f16[512,256]{1,0:T(8,128)(2,1)S(1)} %select_select_fusion.2, f16[512,256]{1,0:T(8,128)(2,1)S(1)} %get-tuple-element.70), kind=kLoop, calls=%fused_computation | loop fusion | flops 2097152 | bytes 3145728 | tf_op jit(solution)/shard_map/concatenate | solution.py:351
  (36 shorter events, 0.3 us)
Async XLA Ops:
  1.3 0.8 copy-start
  2.0 0.7 copy-start.1
  22.2 23.9 %collective-permute-start = (f32[1024,256]{1,0:T(8,128)}, f32[1024,256]{1,0:T(8,128)S(1)}, u32[]{:S(2)}, u32[]{:S(2)}) collective-permute-start(f32[1024,256]{1,0:T(8,128)} %get-tuple-element.38), channel_id=1, source_target_pairs={{0,8},{8,0},{16,24},{24,16},{32,40},{40,32},{48,56},{56,48},{64,72... | collective-permute-start | bytes 3145736 | tf_op jit(solution)/shard_map/ppermute | solution.py:237
  22.2 18.5 %collective-permute-start.3 = (f32[1,256]{1,0:T(1,128)S(1)}, f32[1,256]{1,0:T(1,128)S(1)}, u32[]{:S(2)}, u32[]{:S(2)}) collective-permute-start(f32[1,256]{1,0:T(1,128)S(1)} %get-tuple-element.40), channel_id=1, source_target_pairs={{0,8},{8,0},{16,24},{24,16},{32,40},{40,32},{48,56},{56,48},{64,72... | collective-permute-start | bytes 3080 | tf_op jit(solution)/shard_map/ppermute | solution.py:237
  22.9 21.0 %collective-permute-start.1 = (f16[256,256]{1,0:T(8,128)(2,1)S(1)}, f16[256,256]{1,0:T(8,128)(2,1)S(1)}, u32[]{:S(2)}, u32[]{:S(2)}) collective-permute-start(f16[256,256]{1,0:T(8,128)(2,1)S(1)} %get-tuple-element.86), channel_id=1, source_target_pairs={{0,2},{1,3},{2,4},{3,5},{4,6},{5,7},{6,0},{7,1},{8,10},{9,11},{10,... | collective-permute-start | bytes 393224 | tf_op jit(solution)/shard_map/ppermute | solution.py:237
  40.5 5.6 %collective-permute-start.2 = (f16[256,256]{1,0:T(8,128)(2,1)S(1)}, f16[256,256]{1,0:T(8,128)(2,1)S(1)}, u32[]{:S(2)}, u32[]{:S(2)}) collective-permute-start(f16[256,256]{1,0:T(8,128)(2,1)S(1)} %get-tuple-element.85), channel_id=1, source_target_pairs={{0,6},{1,7},{2,0},{3,1},{4,2},{5,3},{6,4},{7,5},{8,14},{9,15},{10,... | collective-permute-start | bytes 393224 | tf_op jit(solution)/shard_map/ppermute | solution.py:237
  40.5 15.3 %collective-permute-start.6 = (f32[1024,256]{1,0:T(8,128)}, f32[1024,256]{1,0:T(8,128)}, u32[]{:S(2)}, u32[]{:S(2)}) collective-permute-start(f32[1024,256]{1,0:T(8,128)} %get-tuple-element.42), channel_id=1, source_target_pairs={{0,8},{8,0},{16,24},{24,16},{32,40},{40,32},{48,56},{56,48},{64,72... | collective-permute-start | bytes 3145736 | tf_op jit(solution)/shard_map/ppermute | solution.py:237
  40.8 15.3 %collective-permute-start.7 = (f32[1024,256]{1,0:T(8,128)}, f32[1024,256]{1,0:T(8,128)}, u32[]{:S(2)}, u32[]{:S(2)}) collective-permute-start(f32[1024,256]{1,0:T(8,128)} %get-tuple-element.43), channel_id=1, source_target_pairs={{0,8},{8,0},{16,24},{24,16},{32,40},{40,32},{48,56},{56,48},{64,72... | collective-permute-start | bytes 3145736 | tf_op jit(solution)/shard_map/ppermute | solution.py:237
  43.9 15.5 %collective-permute-start.8 = (f32[1024,256]{1,0:T(8,128)}, f32[1024,256]{1,0:T(8,128)}, u32[]{:S(2)}, u32[]{:S(2)}) collective-permute-start(f32[1024,256]{1,0:T(8,128)} %get-tuple-element.44), channel_id=1, source_target_pairs={{0,8},{8,0},{16,24},{24,16},{32,40},{40,32},{48,56},{56,48},{64,72... | collective-permute-start | bytes 3145736 | tf_op jit(solution)/shard_map/ppermute | solution.py:237
  46.1 3.6 %collective-permute-start.11 = (f32[1,256]{1,0:T(1,128)S(1)}, f32[1,256]{1,0:T(1,128)S(1)}, u32[]{:S(2)}, u32[]{:S(2)}) collective-permute-start(f32[1,256]{1,0:T(1,128)S(1)} %add.122), channel_id=1, source_target_pairs={{0,16},{8,24},{16,0},{24,8},{32,48},{40,56},{48,32},{56,40},{64,80... | collective-permute-start | bytes 3080 | tf_op jit(solution)/shard_map/ppermute | solution.py:237
  46.2 13.1 %collective-permute-start.10 = (f16[512,256]{1,0:T(8,128)(2,1)S(1)}, f16[512,256]{1,0:T(8,128)(2,1)}, u32[]{:S(2)}, u32[]{:S(2)}) collective-permute-start(f16[512,256]{1,0:T(8,128)(2,1)S(1)} %pad_maximum_fusion.3), channel_id=1, source_target_pairs={{0,6},{1,7},{2,0},{3,1},{4,2},{5,3},{6,4},{7,5},{8,14},{9,15},{10,... | collective-permute-start | bytes 786440 | tf_op jit(solution)/shard_map/ppermute | solution.py:237
  49.6 7.0 %collective-permute-start.12 = (f32[1,256]{1,0:T(1,128)S(1)}, f32[1,256]{1,0:T(1,128)S(1)}, u32[]{:S(2)}, u32[]{:S(2)}) collective-permute-start(f32[1,256]{1,0:T(1,128)S(1)} %add.126), channel_id=1, source_target_pairs={{0,1},{1,0},{2,3},{3,2},{4,5},{5,4},{6,7},{7,6},{8,9},{9,8},{10,11... | collective-permute-start | bytes 3080 | tf_op jit(solution)/shard_map/ppermute | solution.py:237
  55.8 8.4 %collective-permute-start.9 = (f16[512,256]{1,0:T(8,128)(2,1)}, f16[512,256]{1,0:T(8,128)(2,1)}, u32[]{:S(2)}, u32[]{:S(2)}) collective-permute-start(f16[512,256]{1,0:T(8,128)(2,1)} %pad_maximum_fusion.2), channel_id=1, source_target_pairs={{0,2},{1,3},{2,4},{3,5},{4,6},{5,7},{6,0},{7,1},{8,10},{9,11},{10,... | collective-permute-start | bytes 786440 | tf_op jit(solution)/shard_map/ppermute | solution.py:237
  56.1 8.2 %collective-permute-start.4 = (f16[512,256]{1,0:T(8,128)(2,1)}, f16[512,256]{1,0:T(8,128)(2,1)S(1)}, u32[]{:S(2)}, u32[]{:S(2)}) collective-permute-start(f16[512,256]{1,0:T(8,128)(2,1)} %get-tuple-element.82), channel_id=1, source_target_pairs={{0,32},{8,40},{16,48},{24,56},{32,64},{40,72},{48,80},{56,88},{64,... | collective-permute-start | bytes 786440 | tf_op jit(solution)/shard_map/ppermute | solution.py:237
  56.6 7.7 %collective-permute-start.5 = (f16[512,256]{1,0:T(8,128)(2,1)}, f16[512,256]{1,0:T(8,128)(2,1)S(1)}, u32[]{:S(2)}, u32[]{:S(2)}) collective-permute-start(f16[512,256]{1,0:T(8,128)(2,1)} %get-tuple-element.81), channel_id=1, source_target_pairs={{0,96},{8,104},{16,112},{24,120},{32,0},{40,8},{48,16},{56,24},{64... | collective-permute-start | bytes 786440 | tf_op jit(solution)/shard_map/ppermute | solution.py:237
  64.3 0.7 copy-start.2
  65.0 5.9 %copy-start.3 = (f16[512,256]{1,0:T(8,128)(2,1)S(1)}, f16[512,256]{1,0:T(8,128)(2,1)}, u32[]{:S(2)}) copy-start(f16[512,256]{1,0:T(8,128)(2,1)} %copy-done.2) | copy-start | bytes 786436
  66.2 7.4 %collective-permute-start.15 = (f16[256,256]{1,0:T(8,128)(2,1)S(1)}, f16[256,256]{1,0:T(8,128)(2,1)S(1)}, u32[]{:S(2)}, u32[]{:S(2)}) collective-permute-start(f16[256,256]{1,0:T(8,128)(2,1)S(1)} %dynamic-slice_convert_fusion.1), channel_id=1, source_target_pairs={{0,1},{1,0},{2,3},{3,2},{4,5},{5,4},{6,7},{7,6},{8,9},{9,8},{10,11... | collective-permute-start | bytes 393224 | tf_op jit(solution)/shard_map/ppermute | solution.py:237
  71.1 18.3 %collective-permute-start.14 = (f16[1024,256]{1,0:T(8,128)(2,1)S(1)}, f16[1024,256]{1,0:T(8,128)(2,1)}, u32[]{:S(2)}, u32[]{:S(2)}) collective-permute-start(f16[1024,256]{1,0:T(8,128)(2,1)S(1)} %pad_maximum_fusion.1), channel_id=1, source_target_pairs={{0,96},{8,104},{16,112},{24,120},{32,0},{40,8},{48,16},{56,24},{64... | collective-permute-start | bytes 1572872 | tf_op jit(solution)/shard_map/ppermute | solution.py:237
  72.7 16.7 %collective-permute-start.13 = (f16[1024,256]{1,0:T(8,128)(2,1)S(1)}, f16[1024,256]{1,0:T(8,128)(2,1)}, u32[]{:S(2)}, u32[]{:S(2)}) collective-permute-start(f16[1024,256]{1,0:T(8,128)(2,1)S(1)} %pad_maximum_fusion), channel_id=1, source_target_pairs={{0,32},{8,40},{16,48},{24,56},{32,64},{40,72},{48,80},{56,88},{64,... | collective-permute-start | bytes 1572872 | tf_op jit(solution)/shard_map/ppermute | solution.py:237
  75.6 13.8 %collective-permute-start.16 = (f16[256,256]{1,0:T(8,128)(2,1)S(1)}, f16[256,256]{1,0:T(8,128)(2,1)S(1)}, u32[]{:S(2)}, u32[]{:S(2)}) collective-permute-start(f16[256,256]{1,0:T(8,128)(2,1)S(1)} %divide_convert_fusion), channel_id=1, source_target_pairs={{0,1},{1,0},{2,3},{3,2},{4,5},{5,4},{6,7},{7,6},{8,9},{9,8},{10,11... | collective-permute-start | bytes 393224 | tf_op jit(solution)/shard_map/ppermute | solution.py:237
  77.7 6.6 %collective-permute-start.17 = (f32[1,256]{1,0:T(1,128)S(1)}, f32[1,256]{1,0:T(1,128)S(1)}, u32[]{:S(2)}, u32[]{:S(2)}) collective-permute-start(f32[1,256]{1,0:T(1,128)S(1)} %add.127), channel_id=1, source_target_pairs={{0,32},{8,40},{16,48},{24,56},{32,64},{40,72},{48,80},{56,88},{64,... | collective-permute-start | bytes 3080 | tf_op jit(solution)/shard_map/ppermute | solution.py:237
  84.3 5.1 %collective-permute-start.18 = (f32[1,256]{1,0:T(1,128)S(1)}, f32[1,256]{1,0:T(1,128)S(1)}, u32[]{:S(2)}, u32[]{:S(2)}) collective-permute-start(f32[1,256]{1,0:T(1,128)S(1)} %add.140), channel_id=1, source_target_pairs={{0,64},{8,72},{16,80},{24,88},{32,96},{40,104},{48,112},{56,120},{... | collective-permute-start | bytes 3080 | tf_op jit(solution)/shard_map/ppermute | solution.py:237
  89.5 16.2 %collective-permute-start.20 = (f16[512,256]{1,0:T(8,128)(2,1)S(1)}, f16[512,256]{1,0:T(8,128)(2,1)S(1)}, u32[]{:S(2)}, u32[]{:S(2)}) collective-permute-start(f16[512,256]{1,0:T(8,128)(2,1)S(1)} %pad_maximum_fusion.4), channel_id=1, source_target_pairs={{0,2},{1,3},{2,4},{3,5},{4,6},{5,7},{6,0},{7,1},{8,10},{9,11},{10,... | collective-permute-start | bytes 786440 | tf_op jit(solution)/shard_map/ppermute | solution.py:237
  89.9 15.9 %collective-permute-start.21 = (f16[512,256]{1,0:T(8,128)(2,1)S(1)}, f16[512,256]{1,0:T(8,128)(2,1)S(1)}, u32[]{:S(2)}, u32[]{:S(2)}) collective-permute-start(f16[512,256]{1,0:T(8,128)(2,1)S(1)} %pad_maximum_fusion.4), channel_id=1, source_target_pairs={{0,6},{1,7},{2,0},{3,1},{4,2},{5,3},{6,4},{7,5},{8,14},{9,15},{10,... | collective-permute-start | bytes 786440 | tf_op jit(solution)/shard_map/ppermute | solution.py:237
  94.7 11.1 %collective-permute-start.19 = (f16[512,256]{1,0:T(8,128)(2,1)S(1)}, f16[512,256]{1,0:T(8,128)(2,1)S(1)}, u32[]{:S(2)}, u32[]{:S(2)}) collective-permute-start(f16[512,256]{1,0:T(8,128)(2,1)S(1)} %dynamic-slice_convert_fusion), channel_id=1, source_target_pairs={{0,16},{8,24},{16,0},{24,8},{32,48},{40,56},{48,32},{56,40},{64,80... | collective-permute-start | bytes 786440 | tf_op jit(solution)/shard_map/ppermute | solution.py:237
  95.9 4.8 %collective-permute-start.22 = (f32[1,256]{1,0:T(1,128)S(1)}, f32[1,256]{1,0:T(1,128)S(1)}, u32[]{:S(2)}, u32[]{:S(2)}) collective-permute-start(f32[1,256]{1,0:T(1,128)S(1)} %add.141), channel_id=1, source_target_pairs={{0,2},{1,3},{2,4},{3,5},{4,6},{5,7},{6,0},{7,1},{8,10},{9,11},{10,... | collective-permute-start | bytes 3080 | tf_op jit(solution)/shard_map/ppermute | solution.py:237
  100.7 5.1 %collective-permute-start.23 = (f32[1,256]{1,0:T(1,128)S(1)}, f32[1,256]{1,0:T(1,128)S(1)}, u32[]{:S(2)}, u32[]{:S(2)}) collective-permute-start(f32[1,256]{1,0:T(1,128)S(1)} %add.147), channel_id=1, source_target_pairs={{0,4},{1,5},{2,6},{3,7},{4,0},{5,1},{6,2},{7,3},{8,12},{9,13},{10,... | collective-permute-start | bytes 3080 | tf_op jit(solution)/shard_map/ppermute | solution.py:237
  105.8 6.2 %collective-permute-start.24 = (f16[256,256]{1,0:T(8,128)(2,1)S(1)}, f16[256,256]{1,0:T(8,128)(2,1)S(1)}, u32[]{:S(2)}, u32[]{:S(2)}) collective-permute-start(f16[256,256]{1,0:T(8,128)(2,1)S(1)} %slice.62), channel_id=1, source_target_pairs={{0,2},{1,3},{2,4},{3,5},{4,6},{5,7},{6,0},{7,1},{8,10},{9,11},{10,... | collective-permute-start | bytes 393224 | tf_op jit(solution)/shard_map/ppermute | solution.py:237
  105.9 6.2 %collective-permute-start.25 = (f16[256,256]{1,0:T(8,128)(2,1)S(1)}, f16[256,256]{1,0:T(8,128)(2,1)S(1)}, u32[]{:S(2)}, u32[]{:S(2)}) collective-permute-start(f16[256,256]{1,0:T(8,128)(2,1)S(1)} %slice.63), channel_id=1, source_target_pairs={{0,6},{1,7},{2,0},{3,1},{4,2},{5,3},{6,4},{7,5},{8,14},{9,15},{10,... | collective-permute-start | bytes 393224 | tf_op jit(solution)/shard_map/ppermute | solution.py:237

commit v3 on v2

v3 whole, which is shorter than its diff:
```python
import jax
import jax.numpy as jnp
from jax import lax
from jax.experimental import pallas as pl
from jax.experimental.pallas import tpu as pltpu
from jax.sharding import PartitionSpec as P

prior_doc = 0.5
prior_word = 0.01
SLOTS = 16
AT_ONCE = 4
N_Y, N_X_LO, N_CORE = 4, 2, 2
N_Z, N_X_HI = 4, 2
WORD_SCALE = 2.0**-7
DOC_SCALE = 2.0**-8
TOTAL_SCALE = 2.0**-9
TOTAL_ROWS = 16


def tiles_kernel(
    pairs_hbm,
    load_ref,
    docs_index_ref,
    vocab_index_ref,
    doc_hbm,
    word_hbm,
    weights_hbm,
    counts_hbm,
    doc_parts_out,
    keep_out,
    send_out,
    pairs_ref,
    weights_ref,
    doc_sums,
    word_sums,
    doc_rows,
    word_rows,
    counts_buf,
    first_slot,
    second_slot,
    item_doc,
    pending,
    topics_sem,
    counts_sem,
    sums_sem,
):
    tile_docs, tile_words = counts_hbm.shape[1:]
    blocks = word_hbm.shape[0] // tile_words
    doc_blocks = doc_hbm.shape[0] // tile_docs
    load = load_ref[0, 0]
    y, own_core = docs_index_ref[0] // (N_X_LO * N_CORE), lax.rem(docs_index_ref[0], N_CORE)
    z = vocab_index_ref[0] // N_X_HI
    dest_blocks = blocks // (N_Y * N_X_LO * N_CORE)

    part_rows = dest_blocks * tile_words + TOTAL_ROWS

    def word_place(block):
        dest = block // dest_blocks
        core = lax.rem(dest, N_CORE)
        x_lo = lax.rem(dest // N_CORE, N_X_LO)
        step = lax.rem(dest // (N_CORE * N_X_LO) - y + N_Y, N_Y)
        other = jnp.where(core == own_core, 0, 1)
        place = jnp.where(step == 0, 3, jnp.where(step == 2, 0, (step + 1) // 2))
        return ((other * N_Y + place) * N_X_LO + x_lo) * part_rows + (
            lax.rem(block, dest_blocks) * tile_words
        )

    doc_copy = pltpu.make_async_copy(doc_hbm, doc_rows, topics_sem.at[0])
    word_copy = pltpu.make_async_copy(word_hbm, word_rows, topics_sem.at[1])
    pairs_copy = pltpu.make_async_copy(pairs_hbm.at[0], pairs_ref, topics_sem.at[2])
    weights_copy = pltpu.make_async_copy(weights_hbm, weights_ref, topics_sem.at[3])
    pairs_copy.start()
    doc_copy.start()
    word_copy.start()
    weights_copy.start()

    for b in range(doc_blocks):
        pending[b] = -1

    pairs_copy.wait()

    def sort_slot(s, made):
        b = pairs_ref[0, s] // blocks
        waiting = pending[b]
        first_slot[made] = waiting
        second_slot[made] = s
        item_doc[made] = b
        pending[b] = jnp.where(waiting >= 0, -1, s)
        return made + jnp.where(waiting >= 0, 1, 0)

    made = lax.fori_loop(0, load, sort_slot, 0)
    for b in range(doc_blocks):
        waiting = pending[b]
        first_slot[made] = waiting
        second_slot[made] = -1
        item_doc[made] = b
        made = made + jnp.where(waiting >= 0, 1, 0)

    def pad_item(n, carry):
        first_slot[made + n] = -1
        second_slot[made + n] = -1
        item_doc[made + n] = 0
        return carry

    lax.fori_loop(0, AT_ONCE - 1, pad_item, 0)
    rounds = (made + AT_ONCE - 1) // AT_ONCE

    def copies(item):
        ring = lax.rem(item, SLOTS)
        return [
            pltpu.make_async_copy(
                counts_hbm.at[jnp.maximum(slots[item], 0)],
                counts_buf.at[ring, n],
                counts_sem.at[ring, n],
            )
            for n, slots in enumerate((first_slot, second_slot))
        ]

    def start(n):
        @pl.when(n < rounds)
        def _():
            for item in range(AT_ONCE):
                for copy in copies(n * AT_ONCE + item):
                    copy.start()

    for ahead in range(SLOTS // AT_ONCE - 1):
        start(ahead)

    doc_sums[...] = jnp.zeros_like(doc_sums)
    word_sums[...] = jnp.zeros_like(word_sums)
    doc_copy.wait()
    word_copy.wait()
    weights_copy.wait()

    def load_item(item):
        doc_at = pl.multiple_of(item_doc[item] * tile_docs, tile_docs)
        docs = doc_rows[pl.ds(doc_at, tile_docs), :]
        words, weight, counts, word_blocks = [], [], [], []
        for n, slots in enumerate((first_slot, second_slot)):
            block = lax.rem(pairs_ref[0, jnp.maximum(slots[item], 0)], blocks)
            word_at = pl.multiple_of(block * tile_words, tile_words)
            words.append(word_rows[pl.ds(word_at, tile_words), :])
            live = jnp.where(slots[item] >= 0, 1.0, 0.0)
            weight.append(weights_ref[pl.ds(block, 1), :] * live)
            counts.append(counts_buf[lax.rem(item, SLOTS), n])
            word_blocks.append(block)
        words = jnp.concatenate(words, axis=0)
        weight = jnp.concatenate(weight, axis=1)
        counts = jnp.concatenate(counts, axis=1)
        return docs, words, weight, counts, word_blocks

    def count_ratio(docs, words, weight, counts):
        predicted = lax.dot_general(
            docs, words, (((1,), (1,)), ((), ())), preferred_element_type=jnp.float32
        )
        weighted = (counts.astype(jnp.float32) * weight).astype(jnp.bfloat16)
        return (weighted.astype(jnp.float32) / predicted).astype(jnp.bfloat16)

    def add_terms(item, ratio, docs, words, word_blocks):
        doc_step = lax.rem(item_doc[item] - z + N_Z, N_Z)
        doc_to = pl.ds(pl.multiple_of(doc_step * tile_docs, tile_docs), tile_docs)
        doc_sums[doc_to, :] += jnp.dot(ratio, words, preferred_element_type=jnp.float32)
        terms = lax.dot_general(
            ratio, docs, (((0,), (0,)), ((), ())), preferred_element_type=jnp.float32
        )
        for n, block in enumerate(word_blocks):
            to = pl.multiple_of(word_place(block), TOTAL_ROWS)
            word_sums[pl.ds(to, tile_words), :] += terms[n * tile_words : (n + 1) * tile_words]

    def run_items(n, carry):
        start(n + SLOTS // AT_ONCE - 1)
        items = [n * AT_ONCE + item for item in range(AT_ONCE)]
        for item in items:
            for copy in copies(item):
                copy.wait()
        loaded = [load_item(item) for item in items]
        ratios = [count_ratio(*fields[:4]) for fields in loaded]
        for item, ratio, (docs, words, _, _, word_blocks) in zip(items, ratios, loaded):
            add_terms(item, ratio, docs, words, word_blocks)
        return carry

    lax.fori_loop(0, rounds, run_items, 0)

    def leave(n, source, target):
        copy = pltpu.make_async_copy(source, target, sums_sem.at[n])
        copy.start()
        return copy

    leaving = [
        leave(step, doc_sums.at[pl.ds(step * tile_docs, tile_docs)], doc_parts_out[step])
        for step in range(N_Z)
    ]
    total = jnp.zeros((1, doc_rows.shape[1]), jnp.float32)
    for step in range(N_Z):
        at = pl.multiple_of(lax.rem(z + step, N_Z) * tile_docs, tile_docs)
        topics = doc_rows[pl.ds(at, tile_docs), :].astype(jnp.float32)
        sums = doc_sums[pl.ds(step * tile_docs, tile_docs), :]
        total = total + jnp.sum(topics * sums, axis=0, keepdims=True)
    total = jnp.broadcast_to(total * TOTAL_SCALE, (TOTAL_ROWS, doc_rows.shape[1]))
    for n in range(word_sums.shape[0] // part_rows):
        word_sums[(n + 1) * part_rows - TOTAL_ROWS : (n + 1) * part_rows, :] = total
    near_rows = N_X_LO * part_rows
    start_row = N_Y * near_rows
    for out in send_out:
        leaving.append(leave(len(leaving), word_sums.at[pl.ds(start_row, out.shape[0])], out))
        start_row += out.shape[0]
    start_row = 0
    for out in keep_out:
        leaving.append(leave(len(leaving), word_sums.at[pl.ds(start_row, out.shape[0])], out))
        start_row += out.shape[0]
    for copy in leaving:
        copy.wait()


def run_tiles(
    pair_list, own_load, docs_index, vocab_index, doc_topics, word_topics, weight_table, counts_all
):
    slots = pair_list.shape[-1]
    tile_docs, tile_words = counts_all.shape[1:]
    topics = doc_topics.shape[1]
    doc_blocks = doc_topics.shape[0] // tile_docs
    items = slots + doc_blocks + AT_ONCE
    doc_part = jax.ShapeDtypeStruct((doc_topics.shape[0] // N_Z, topics), jnp.float32)
    word_rows = word_topics.shape[0] // (N_CORE * N_Y) + N_X_LO * TOTAL_ROWS
    first_part = jax.ShapeDtypeStruct((word_rows, topics), jnp.float32)
    later_part = jax.ShapeDtypeStruct(((N_Y - 1) * word_rows, topics), jnp.float32)
    smem = pl.BlockSpec(memory_space=pltpu.SMEM)
    hbm = pl.BlockSpec(memory_space=pl.ANY)
    return pl.pallas_call(
        tiles_kernel,
        out_shape=(
            (doc_part,) * N_Z,
            (first_part, later_part),
            (first_part, later_part),
        ),
        in_specs=[hbm] + [smem] * 3 + [hbm] * 4,
        out_specs=((hbm,) * N_Z, (hbm,) * 2, (hbm,) * 2),
        scratch_shapes=[
            pltpu.SMEM(pair_list.shape[1:], jnp.int32),
            pltpu.VMEM(weight_table.shape, jnp.float32),
            pltpu.VMEM(doc_topics.shape, jnp.float32),
            pltpu.VMEM((N_CORE * N_Y * word_rows, topics), jnp.float32),
            pltpu.VMEM(doc_topics.shape, doc_topics.dtype),
            pltpu.VMEM(word_topics.shape, word_topics.dtype),
            pltpu.VMEM((SLOTS, 2, tile_docs, tile_words), counts_all.dtype),
            pltpu.SMEM((items,), jnp.int32),
            pltpu.SMEM((items,), jnp.int32),
            pltpu.SMEM((items,), jnp.int32),
            pltpu.SMEM((doc_blocks,), jnp.int32),
            pltpu.SemaphoreType.DMA((4,)),
            pltpu.SemaphoreType.DMA((SLOTS, 2)),
            pltpu.SemaphoreType.DMA((N_Z + 4,)),
        ],
        compiler_params=pltpu.CompilerParams(vmem_limit_bytes=48 << 20),
        name="tiles",
    )(
        pair_list,
        own_load,
        docs_index,
        vocab_index,
        doc_topics,
        word_topics,
        weight_table,
        counts_all,
    )


def moves(axis, size, move):
    return lambda value: lax.ppermute(value, axis, [(n, move(n) % size) for n in range(size)])


def to_half(value):
    return value.astype(jnp.float16)


def to_float(value):
    return value.astype(jnp.float32)


def on_device(doc_topics, word_topics, word_weights, tile_pairs, tile_counts, tile_load):
    n_docs, n_vocab = lax.axis_size("docs"), lax.axis_size("vocab")
    docs_index, vocab_index = lax.axis_index("docs"), lax.axis_index("vocab")
    x_lo = docs_index // N_CORE % N_X_LO
    z, x_hi = vocab_index // N_X_HI, vocab_index % N_X_HI
    to_core = moves("docs", n_docs, lambda n: n ^ 1)
    to_x_lo = moves("docs", n_docs, lambda n: n ^ N_CORE)
    y_up = moves("docs", n_docs, lambda n: n + N_X_LO * N_CORE)
    y_down = moves("docs", n_docs, lambda n: n - N_X_LO * N_CORE)
    to_x_hi = moves("vocab", n_vocab, lambda n: n ^ 1)
    z_up = moves("vocab", n_vocab, lambda n: n + N_X_HI)
    z_down = moves("vocab", n_vocab, lambda n: n - N_X_HI)

    counts_all = tile_counts[0, 0]
    tile_words = counts_all.shape[2]
    blocks = word_topics.shape[0] // tile_words
    weight_table = word_weights.reshape(blocks, tile_words)
    doc_parts, keep, send = run_tiles(
        tile_pairs,
        tile_load,
        docs_index.reshape(1),
        vocab_index.reshape(1),
        doc_topics,
        word_topics,
        weight_table,
        counts_all,
    )

    z_across = moves("vocab", n_vocab, lambda n: n + 2 * N_X_HI)
    meet = lambda *values: lax.optimization_barrier(values)
    near_rows = keep[0].shape[0]
    word_rows = near_rows // N_X_LO
    doc_rows = doc_parts[0].shape[0] // N_X_HI

    part = [piece * DOC_SCALE for piece in doc_parts]
    word_far = to_core(send[0])
    doc_up = z_up(to_half(part[2][:doc_rows]))
    doc_down = z_down(to_half(part[2][doc_rows:]))
    word_far, doc_up, doc_down = meet(word_far, doc_up, doc_down)

    far = (keep[0] + word_far) * WORD_SCALE
    word_up = y_up(to_half(far[:word_rows]))
    word_down = y_down(to_half(far[word_rows:]))
    near_far = to_core(send[1])
    doc_below = z_up(
        to_half(jnp.concatenate([part[1][:doc_rows] + to_float(doc_up), part[1][doc_rows:]]))
    )
    doc_above = z_down(
        to_half(jnp.concatenate([part[3][:doc_rows], part[3][doc_rows:] + to_float(doc_down)]))
    )
    word_up, word_down, near_far, doc_below, doc_above = meet(
        word_up, word_down, near_far, doc_below, doc_above
    )

    near = (keep[1] + near_far) * WORD_SCALE
    above, below, here = near[:near_rows], near[near_rows : 2 * near_rows], near[2 * near_rows :]
    word_below = y_up(
        to_half(jnp.concatenate([above[:word_rows] + to_float(word_up), above[word_rows:]]))
    )
    word_above = y_down(
        to_half(jnp.concatenate([below[:word_rows], below[word_rows:] + to_float(word_down)]))
    )
    doc_pair = part[0] + to_float(doc_below) + to_float(doc_above)
    doc_mine = lax.dynamic_slice_in_dim(doc_pair, x_hi * doc_rows, doc_rows, 0)
    doc_other = lax.dynamic_slice_in_dim(doc_pair, (1 - x_hi) * doc_rows, doc_rows, 0)
    doc_sums = (doc_mine + to_float(to_x_hi(to_half(doc_other)))) / DOC_SCALE
    own_docs = lax.dynamic_slice_in_dim(doc_topics, vocab_index * doc_rows, doc_rows, 0)
    doc_scaled = own_docs.astype(jnp.float32) * doc_sums + prior_doc
    doc_block = to_half(
        doc_topics.shape[1] * doc_scaled / jnp.sum(doc_scaled, axis=1, keepdims=True)
    )
    doc_far = to_x_hi(doc_block)
    word_below, word_above, doc_block, doc_far = meet(word_below, word_above, doc_block, doc_far)

    word_pair = here + to_float(word_below) + to_float(word_above)
    word_mine = lax.dynamic_slice_in_dim(word_pair, x_lo * word_rows, word_rows, 0)
    word_other = lax.dynamic_slice_in_dim(word_pair, (1 - x_lo) * word_rows, word_rows, 0)
    word_far = to_x_lo(to_half(word_other))
    doc_here = jnp.concatenate(
        [
            jnp.where(x_hi == 0, doc_block, doc_far),
            jnp.where(x_hi == 0, doc_far, doc_block),
        ]
    )
    doc_below, doc_above = z_up(doc_here), z_down(doc_here)
    word_far, doc_below, doc_above = meet(word_far, doc_below, doc_above)

    low_across, high_across = z_up(doc_below[:doc_rows]), z_down(doc_above[doc_rows:])
    row_count = word_topics.shape[0] // n_docs
    word_sums = (word_mine + to_float(word_far)) / WORD_SCALE
    column = word_sums[row_count : row_count + 1] / TOTAL_SCALE
    column = column + to_x_hi(column)
    column = column + z_up(column) + z_down(column) + z_across(column)
    vocab_total = word_topics.shape[0] * n_vocab
    own_words = lax.dynamic_slice_in_dim(word_topics, docs_index * row_count, row_count, 0)
    word_scaled = own_words.astype(jnp.float32) * word_sums[:row_count] + prior_word
    word_next = vocab_total * word_scaled / (column + vocab_total * prior_word)
    by_step = (doc_here, doc_above, jnp.concatenate([low_across, high_across]), doc_below)
    doc_next = jnp.concatenate(
        [to_float(lax.select_n((place - z) % N_Z, *by_step)) for place in range(N_Z)]
    )
    return (doc_next, word_next)


def solution(mesh):
    placed = (
        P("docs", None),
        P("vocab", None),
        P("vocab"),
        P("docs", "vocab", None),
        P("docs", "vocab", None, None, None),
        P("docs", "vocab"),
    )
    return jax.shard_map(
        on_device,
        mesh=mesh,
        in_specs=placed,
        out_specs=(P("docs", None), P(("vocab", "docs"), None)),
        check_vma=False,
    )
```

time: 115 us -> 102 us (0.89)
  starting transfers between devices: 43.7 us -> 30.5 us
  waiting for transfers between devices: 33.3 us -> 28.4 us
  other arithmetic: 13 us -> 14.8 us
  Pallas kernels: 19.5 us -> 21.1 us
    ppermute x26 -> x21, starting transfers between devices: 43.7 us -> 30.5 us  [moves(): lax.ppermute(value, axis, [(n, move(n) % size) for n in range(size)])]
    ppermute x26 -> x21, waiting for transfers between devices: 33.3 us -> 28.4 us  [moves(): lax.ppermute(value, axis, [(n, move(n) % size) for n in range(size)])]
    another operation x6, other arithmetic: 0.59 us -> 3.96 us
    mul x1 -> x0, other arithmetic: 2.13 us -> none  [on_device(): (keep[step] + from_core[step]) * WORD_SCALE]
    pallas_call x1, Pallas kernels: 19.5 us -> 21.1 us  [run_tiles(): pl.pallas_call(tiles_kernel, out_shape=((doc_part,) * N_Z, (first_part, l...]
    unnamed x9 -> x19, local copies, waits for them, and re-layouts: 2.14 us -> 3.78 us
    concatenate x2, other arithmetic: 0.25 us -> 1.85 us  [the longest x1 0.93 us: on_device(): jnp.concatenate([below[:word_rows], below[word_rows:] + to_float(word_dow...]
  transfers between devices with their start and end apart: 26 -> 21, of which waited for: 10 -> 10; matrix products, arithmetic and copies ran while one was open for 9% -> 10% of each run, Pallas kernels for 0% -> 0%
where the time goes in v3:
time: 102 us; the launch traced here: 101 us
  starting transfers between devices  30.5 us (30%)
  waiting for transfers between devices  28.4 us (28%)
  Pallas kernels  21.1 us (21%)
  other arithmetic  14.8 us (15%)
  local copies, waits for them, and re-layouts  4.13 us (4%)
  between operations  1.58 us (2%)
    ppermute x21, starting transfers between devices, moves(): lax.ppermute(value, axis, [(n, move(n) % size) for n in range(size)])  30.5 us
    ppermute x21, waiting for transfers between devices, moves(): lax.ppermute(value, axis, [(n, move(n) % size) for n in range(size)])  28.4 us
    pallas_call x1, Pallas kernels, run_tiles(): pl.pallas_call(tiles_kernel, out_shape=((doc_part,) * N_Z, (first_part, l...  21.1 us
    another operation x6, other arithmetic  3.96 us
    unnamed x19, local copies, waits for them, and re-layouts  3.78 us
  transfers between devices with their start and end apart: 21, of which 10 were waited for; matrix products, arithmetic and copies ran while one was open for 10% of the time, Pallas kernels for 0%

profile of v3, /device:TPU:0, one launch (start us, length us, event | category | flops | bytes accessed | tf_op | source)
XLA Modules:
  0.0 100.6 jit_solution(14938590080682564904)
XLA Ops:
  1.3 0.0 copy-start
  1.3 1.2 %copy-done = bf16[2048,256]{1,0:T(8,128)(2,1)S(1)} copy-done((bf16[2048,256]{1,0:T(8,128)(2,1)S(1)}, bf16[2048,256]{1,0:T(8,128)(2,1)}, u32[]{:S(2)}) %copy-start) | copy-done | bytes 1048600
  2.5 0.8 copy-done.1
  3.3 0.7 copy-done.2
  3.9 21.1 %tiles.1 = (f32[512,256]{1,0:T(8,128)S(1)}, f32[512,256]{1,0:T(8,128)S(1)}, f32[512,256]{1,0:T(8,128)S(1)}, f32[512,256]{1,0:T(8,128)S(1)}, f32[1056,256]{1,0:T(...) custom-call(s32[1,1,96]{2,1,0:T(1,128)S(1)} %copy-done.2, ...), custom_call_target="tpu_custom_call" | custom-call | tf_op jit(solution)/shard_map/tiles/pallas_call | solution.py:229
  25.1 0.1 collective-permute-start.5
  25.1 0.5 collective-permute-start
  25.6 0.1 multiply_convert_fusion.1
  25.7 0.1 fusion.13
  25.8 0.1 collective-permute-start.1
  25.9 4.3 %collective-permute-start.2 = (f16[256,256]{1,0:T(8,128)(2,1)S(1)}, f16[256,256]{1,0:T(8,128)(2,1)S(1)}, u32[]{:S(2)}, u32[]{:S(2)}) collective-permute-start(f16[256,256]{1,0:T(8,128)(2,1)S(1)} %get-tuple-element.65), channel_id=1, source_target_pairs={{0,6},{1,7},{2,0},{3,1},{4,2},{5,3},{6,4},{7,5},{8,14},{9,15},{10,... | collective-permute-start | bytes 393224 | tf_op jit(solution)/shard_map/ppermute | solution.py:269
  30.2 3.6 %collective-permute-done.1 = f16[256,256]{1,0:T(8,128)(2,1)S(1)} collective-permute-done((f16[256,256]{1,0:T(8,128)(2,1)S(1)}, f16[256,256]{1,0:T(8,128)(2,1)S(1)}, u32[]{:S(2)}, u32[]{:S(2)}) %collective-permute-start.1) | collective-permute-done | bytes 131104 | tf_op jit(solution)/shard_map/ppermute | solution.py:269
  33.8 0.1 slice_convert_fusion
  33.9 0.1 pad_maximum_fusion.3
  33.9 3.1 %collective-permute-start.7 = (f16[512,256]{1,0:T(8,128)(2,1)S(1)}, f16[512,256]{1,0:T(8,128)(2,1)S(1)}, u32[]{:S(2)}, u32[]{:S(2)}) collective-permute-start(f16[512,256]{1,0:T(8,128)(2,1)S(1)} %pad_maximum_fusion.3), channel_id=1, source_target_pairs={{0,6},{1,7},{2,0},{3,1},{4,2},{5,3},{6,4},{7,5},{8,14},{9,15},{10,... | collective-permute-start | bytes 786440 | tf_op jit(solution)/shard_map/ppermute | solution.py:269
  37.0 0.2 multiply_convert_fusion
  37.2 0.1 fusion.12
  37.3 1.6 %collective-permute-start.3 = (f16[528,256]{1,0:T(8,128)(2,1)S(1)}, f16[528,256]{1,0:T(8,128)(2,1)S(1)}, u32[]{:S(2)}, u32[]{:S(2)}) collective-permute-start(f16[528,256]{1,0:T(8,128)(2,1)S(1)} %get-tuple-element.58), channel_id=1, source_target_pairs={{0,32},{8,40},{16,48},{24,56},{32,64},{40,72},{48,80},{56,88},{64,... | collective-permute-start | bytes 811016 | tf_op jit(solution)/shard_map/ppermute | solution.py:269
  38.9 1.7 %collective-permute-start.4 = (f16[528,256]{1,0:T(8,128)(2,1)S(1)}, f16[528,256]{1,0:T(8,128)(2,1)S(1)}, u32[]{:S(2)}, u32[]{:S(2)}) collective-permute-start(f16[528,256]{1,0:T(8,128)(2,1)S(1)} %get-tuple-element.57), channel_id=1, source_target_pairs={{0,96},{8,104},{16,112},{24,120},{32,0},{40,8},{48,16},{56,24},{64... | collective-permute-start | bytes 811016 | tf_op jit(solution)/shard_map/ppermute | solution.py:269
  40.6 0.1 fusion.7
  40.7 0.1 pad_maximum_fusion.2
  40.7 0.1 collective-permute-start.6
  40.8 1.8 %collective-permute-done.7 = f16[512,256]{1,0:T(8,128)(2,1)S(1)} collective-permute-done((f16[512,256]{1,0:T(8,128)(2,1)S(1)}, f16[512,256]{1,0:T(8,128)(2,1)S(1)}, u32[]{:S(2)}, u32[]{:S(2)}) %collective-permute-start.7) | collective-permute-done | bytes 262176 | tf_op jit(solution)/shard_map/ppermute | solution.py:269
  42.6 6.6 %collective-permute-done.6 = f16[512,256]{1,0:T(8,128)(2,1)S(1)} collective-permute-done((f16[512,256]{1,0:T(8,128)(2,1)S(1)}, f16[512,256]{1,0:T(8,128)(2,1)S(1)}, u32[]{:S(2)}, u32[]{:S(2)}) %collective-permute-start.6) | collective-permute-done | bytes 262176 | tf_op jit(solution)/shard_map/ppermute | solution.py:269
  49.2 0.0 copy-start.7
  49.3 0.1 convert_add_fusion
  49.4 0.7 collective-permute-start.10
  50.1 0.1 copy-done.4
  50.2 3.5 %fusion.10 = (f16[3168,256]{1,0:T(8,128)(2,1)S(1)}, f32[3168,256]{1,0:T(8,128)S(1)}) fusion(f32[3168,256]{1,0:T(8,128)} %get-tuple-element.25, f32[3168,256]{1,0:T(8,128)} %collective-permute-done.5), kind=kLoop, calls=%fused_computation.45 | loop fusion | flops 2433024 | bytes 11354112 | tf_op jit(solution)/shard_map/convert.6
  53.7 0.1 fusion.11
  53.8 0.2 fusion.1
  54.0 0.9 pad_maximum_fusion.1
  54.9 1.5 %collective-permute-start.9 = (f16[1056,256]{1,0:T(8,128)(2,1)}, f16[1056,256]{1,0:T(8,128)(2,1)}, u32[]{:S(2)}, u32[]{:S(2)}) collective-permute-start(f16[1056,256]{1,0:T(8,128)(2,1)} %pad_maximum_fusion.1), channel_id=1, source_target_pairs={{0,96},{8,104},{16,112},{24,120},{32,0},{40,8},{48,16},{56,24},{64... | collective-permute-start | bytes 1622024 | tf_op jit(solution)/shard_map/ppermute | solution.py:269
  56.5 0.9 pad_maximum_fusion
  57.4 0.5 collective-permute-start.8
  57.9 1.1 %fusion.8 = f32[256]{0:T(256)S(1)} fusion(f16[256,256]{1,0:T(8,128)(2,1)S(1)} %collective-permute-done.10, f32[512,256]{1,0:T(8,128)} %copy-done.4, s32[]{:T(128)S(6)} %select_n.181, bf16[2048,256]{1,0:T(8,128)(2,1)} %doc_hbm.1, s32[]{:T(128)S(6)} %select_n.180), kind=kLoop, calls=%fused_computation.39 | loop fusion | flops 458496 | bytes 525320 | tf_op jit(solution)/shard_map/reduce_sum | solution.py:349
  59.0 1.1 %divide_convert_fusion = f16[256,256]{1,0:T(8,128)(2,1)S(1)} fusion(f32[256]{0:T(256)S(1)} %fusion.8, f16[256,256]{1,0:T(8,128)(2,1)S(1)} %collective-permute-done.10, f32[512,256]{1,0:T(8,128)} %copy-done.4, s32[]{:T(128)S(6)} %select_n.181, bf16[2048,256]{1,0:T(8,128)(2,1)} %doc_hbm.1, s32[]{:T(128)S(6)} %select_n.180), kind=kLoop, calls=%fused_computation.32 | loop fusion | flops 589824 | bytes 656392 | tf_op jit(solution)/shard_map/convert_element_type | solution.py:273
  60.1 2.9 %collective-permute-start.11 = (f16[256,256]{1,0:T(8,128)(2,1)S(1)}, f16[256,256]{1,0:T(8,128)(2,1)S(1)}, u32[]{:S(2)}, u32[]{:S(2)}) collective-permute-start(f16[256,256]{1,0:T(8,128)(2,1)S(1)} %divide_convert_fusion), channel_id=1, source_target_pairs={{0,1},{1,0},{2,3},{3,2},{4,5},{5,4},{6,7},{7,6},{8,9},{9,8},{10,11... | collective-permute-start | bytes 393224 | tf_op jit(solution)/shard_map/ppermute | solution.py:269
  63.0 3.6 %collective-permute-done.11 = f16[256,256]{1,0:T(8,128)(2,1)S(1)} collective-permute-done((f16[256,256]{1,0:T(8,128)(2,1)S(1)}, f16[256,256]{1,0:T(8,128)(2,1)S(1)}, u32[]{:S(2)}, u32[]{:S(2)}) %collective-permute-start.11) | collective-permute-done | bytes 131104 | tf_op jit(solution)/shard_map/ppermute | solution.py:269
  66.6 0.8 collective-permute-done.9
  67.5 3.2 %collective-permute-done.8 = f16[1056,256]{1,0:T(8,128)(2,1)} collective-permute-done((f16[1056,256]{1,0:T(8,128)(2,1)}, f16[1056,256]{1,0:T(8,128)(2,1)}, u32[]{:S(2)}, u32[]{:S(2)}) %collective-permute-start.8) | collective-permute-done | bytes 540704 | tf_op jit(solution)/shard_map/ppermute | solution.py:269
  70.7 1.4 %fusion = f32[1056,256]{1,0:T(8,128)S(1)} fusion(f32[3168,256]{1,0:T(8,128)S(1)} %get-tuple-element.49, f16[1056,256]{1,0:T(8,128)(2,1)} %collective-permute-done.9, f16[1056,256]{1,0:T(8,128)(2,1)} %collective-permute-done.8), kind=kLoop, calls=%fused_computation.2 | loop fusion | flops 1081344 | bytes 3244032 | tf_op jit(solution)/shard_map/add | solution.py:354
  72.0 0.0 copy-start.3
  72.0 1.0 copy-done.3
  73.0 0.1 collective-permute-start.12
  73.1 0.1 broadcast_select_fusion.1
  73.2 0.1 pad_maximum_fusion.4
  73.3 0.1 collective-permute-start.13
  73.4 3.2 %collective-permute-start.14 = (f16[512,256]{1,0:T(8,128)(2,1)S(1)}, f16[512,256]{1,0:T(8,128)(2,1)S(1)}, u32[]{:S(2)}, u32[]{:S(2)}) collective-permute-start(f16[512,256]{1,0:T(8,128)(2,1)S(1)} %pad_maximum_fusion.4), channel_id=1, source_target_pairs={{0,6},{1,7},{2,0},{3,1},{4,2},{5,3},{6,4},{7,5},{8,14},{9,15},{10,... | collective-permute-start | bytes 786440 | tf_op jit(solution)/shard_map/ppermute | solution.py:269
  76.6 4.3 %collective-permute-done.13 = f16[512,256]{1,0:T(8,128)(2,1)S(1)} collective-permute-done((f16[512,256]{1,0:T(8,128)(2,1)S(1)}, f16[512,256]{1,0:T(8,128)(2,1)S(1)}, u32[]{:S(2)}, u32[]{:S(2)}) %collective-permute-start.13) | collective-permute-done | bytes 262176 | tf_op jit(solution)/shard_map/ppermute | solution.py:269
  80.9 1.1 %add_multiply_fusion.1 = f32[528,256]{1,0:T(8,128)S(1)} fusion(f16[528,256]{1,0:T(8,128)(2,1)S(1)} %collective-permute-done.12, f32[1056,256]{1,0:T(8,128)} %copy-done.3, s32[]{:T(128)S(6)} %select_n.224), kind=kLoop, calls=%fused_computation.11 | loop fusion | flops 405504 | bytes 1351684 | tf_op jit(solution)/shard_map/div | solution.py:369
  82.1 1.9 %collective-permute-start.17 = (f32[1,256]{1,0:T(1,128)S(1)}, f32[1,256]{1,0:T(1,128)S(1)}, u32[]{:S(2)}, u32[]{:S(2)}) collective-permute-start(f32[1,256]{1,0:T(1,128)S(1)} %slice_multiply_fusion.1), channel_id=1, source_target_pairs={{0,1},{1,0},{2,3},{3,2},{4,5},{5,4},{6,7},{7,6},{8,9},{9,8},{10,11... | collective-permute-start | bytes 3080 | tf_op jit(solution)/shard_map/ppermute | solution.py:269
  83.9 3.3 %collective-permute-done.17 = f32[1,256]{1,0:T(1,128)S(1)} collective-permute-done((f32[1,256]{1,0:T(1,128)S(1)}, f32[1,256]{1,0:T(1,128)S(1)}, u32[]{:S(2)}, u32[]{:S(2)}) %collective-permute-start.17) | collective-permute-done | bytes 1056 | tf_op jit(solution)/shard_map/ppermute | solution.py:269
  87.2 0.8 collective-permute-start.18
  88.0 2.4 %collective-permute-start.19 = (f32[1,256]{1,0:T(1,128)S(1)}, f32[1,256]{1,0:T(1,128)S(1)}, u32[]{:S(2)}, u32[]{:S(2)}) collective-permute-start(f32[1,256]{1,0:T(1,128)S(1)} %fusion.9), channel_id=1, source_target_pairs={{0,6},{1,7},{2,0},{3,1},{4,2},{5,3},{6,4},{7,5},{8,14},{9,15},{10,... | collective-permute-start | bytes 3080 | tf_op jit(solution)/shard_map/ppermute | solution.py:269
  90.5 1.7 %collective-permute-start.20 = (f32[1,256]{1,0:T(1,128)S(1)}, f32[1,256]{1,0:T(1,128)S(1)}, u32[]{:S(2)}, u32[]{:S(2)}) collective-permute-start(f32[1,256]{1,0:T(1,128)S(1)} %fusion.9), channel_id=1, source_target_pairs={{0,4},{1,5},{2,6},{3,7},{4,0},{5,1},{6,2},{7,3},{8,12},{9,13},{10,... | collective-permute-start | bytes 3080 | tf_op jit(solution)/shard_map/ppermute | solution.py:269
  92.1 1.3 %collective-permute-start.15 = (f16[256,256]{1,0:T(8,128)(2,1)S(1)}, f16[256,256]{1,0:T(8,128)(2,1)S(1)}, u32[]{:S(2)}, u32[]{:S(2)}) collective-permute-start(f16[256,256]{1,0:T(8,128)(2,1)S(1)} %slice.78), channel_id=1, source_target_pairs={{0,2},{1,3},{2,4},{3,5},{4,6},{5,7},{6,0},{7,1},{8,10},{9,11},{10,... | collective-permute-start | bytes 393224 | tf_op jit(solution)/shard_map/ppermute | solution.py:269
  93.5 2.1 %collective-permute-start.16 = (f16[256,256]{1,0:T(8,128)(2,1)S(1)}, f16[256,256]{1,0:T(8,128)(2,1)S(1)}, u32[]{:S(2)}, u32[]{:S(2)}) collective-permute-start(f16[256,256]{1,0:T(8,128)(2,1)S(1)} %slice.79), channel_id=1, source_target_pairs={{0,6},{1,7},{2,0},{3,1},{4,2},{5,3},{6,4},{7,5},{8,14},{9,15},{10,... | collective-permute-start | bytes 393224 | tf_op jit(solution)/shard_map/ppermute | solution.py:269
  95.6 1.8 %fusion.5 = f32[512,256]{1,0:T(8,128)} fusion(f32[528,256]{1,0:T(8,128)S(1)} %add_multiply_fusion.1, f32[256]{0:T(256)S(1)} %bitcast.7, bf16[8192,256]{1,0:T(8,128)(2,1)} %word_hbm.1, s32[]{:T(128)S(6)} %select_n.223), kind=kLoop, calls=%fused_computation.16 | loop fusion | flops 655360 | bytes 1311748 | tf_op jit(solution)/shard_map/div | solution.py:376
  97.4 1.0 collective-permute-done.15
  98.4 0.1 collective-permute-done.16
  98.5 0.2 select_select_fusion.2
  98.7 0.3 select_select_fusion.3
  99.0 1.5 %maximum_convert_fusion = f32[2048,256]{1,0:T(8,128)} fusion(f16[512,256]{1,0:T(8,128)(2,1)S(1)} %get-tuple-element.55, f16[512,256]{1,0:T(8,128)(2,1)S(1)} %get-tuple-element.56, f16[512,256]{1,0:T(8,128)(2,1)S(1)} %select_select_fusion.2, f16[512,256]{1,0:T(8,128)(2,1)S(1)} %get-tuple-element.54), kind=kLoop, calls=%fused_computation.4 | loop fusion | flops 2097152 | bytes 3145728 | tf_op jit(solution)/shard_map/concatenate | solution.py:378
  (31 shorter events, 0.3 us)
Async XLA Ops:
  1.3 1.2 %copy-start = (bf16[2048,256]{1,0:T(8,128)(2,1)S(1)}, bf16[2048,256]{1,0:T(8,128)(2,1)}, u32[]{:S(2)}) copy-start(bf16[2048,256]{1,0:T(8,128)(2,1)} %doc_hbm.1) | copy-start | bytes 3145732
  2.5 0.8 copy-start.1
  3.3 0.7 copy-start.2
  25.1 24.2 %collective-permute-start.5 = (f32[3168,256]{1,0:T(8,128)}, f32[3168,256]{1,0:T(8,128)}, u32[]{:S(2)}, u32[]{:S(2)}) collective-permute-start(f32[3168,256]{1,0:T(8,128)} %get-tuple-element.30), channel_id=1, source_target_pairs={{0,8},{8,0},{16,24},{24,16},{32,40},{40,32},{48,56},{56,48},{64,72... | collective-permute-start | bytes 9732104 | tf_op jit(solution)/shard_map/ppermute | solution.py:269
  25.1 8.7 %collective-permute-start = (f32[1056,256]{1,0:T(8,128)S(1)}, f32[1056,256]{1,0:T(8,128)S(1)}, u32[]{:S(2)}, u32[]{:S(2)}) collective-permute-start(f32[1056,256]{1,0:T(8,128)S(1)} %get-tuple-element.27), channel_id=1, source_target_pairs={{0,8},{8,0},{16,24},{24,16},{32,40},{40,32},{48,56},{56,48},{64,72... | collective-permute-start | bytes 3244040 | tf_op jit(solution)/shard_map/ppermute | solution.py:269
  25.8 8.0 %collective-permute-start.1 = (f16[256,256]{1,0:T(8,128)(2,1)S(1)}, f16[256,256]{1,0:T(8,128)(2,1)S(1)}, u32[]{:S(2)}, u32[]{:S(2)}) collective-permute-start(f16[256,256]{1,0:T(8,128)(2,1)S(1)} %get-tuple-element.66), channel_id=1, source_target_pairs={{0,2},{1,3},{2,4},{3,5},{4,6},{5,7},{6,0},{7,1},{8,10},{9,11},{10,... | collective-permute-start | bytes 393224 | tf_op jit(solution)/shard_map/ppermute | solution.py:269
  25.9 7.9 %collective-permute-start.2 = (f16[256,256]{1,0:T(8,128)(2,1)S(1)}, f16[256,256]{1,0:T(8,128)(2,1)S(1)}, u32[]{:S(2)}, u32[]{:S(2)}) collective-permute-start(f16[256,256]{1,0:T(8,128)(2,1)S(1)} %get-tuple-element.65), channel_id=1, source_target_pairs={{0,6},{1,7},{2,0},{3,1},{4,2},{5,3},{6,4},{7,5},{8,14},{9,15},{10,... | collective-permute-start | bytes 393224 | tf_op jit(solution)/shard_map/ppermute | solution.py:269
  33.9 8.7 %collective-permute-start.7 = (f16[512,256]{1,0:T(8,128)(2,1)S(1)}, f16[512,256]{1,0:T(8,128)(2,1)S(1)}, u32[]{:S(2)}, u32[]{:S(2)}) collective-permute-start(f16[512,256]{1,0:T(8,128)(2,1)S(1)} %pad_maximum_fusion.3), channel_id=1, source_target_pairs={{0,6},{1,7},{2,0},{3,1},{4,2},{5,3},{6,4},{7,5},{8,14},{9,15},{10,... | collective-permute-start | bytes 786440 | tf_op jit(solution)/shard_map/ppermute | solution.py:269
  37.3 11.9 %collective-permute-start.3 = (f16[528,256]{1,0:T(8,128)(2,1)S(1)}, f16[528,256]{1,0:T(8,128)(2,1)S(1)}, u32[]{:S(2)}, u32[]{:S(2)}) collective-permute-start(f16[528,256]{1,0:T(8,128)(2,1)S(1)} %get-tuple-element.58), channel_id=1, source_target_pairs={{0,32},{8,40},{16,48},{24,56},{32,64},{40,72},{48,80},{56,88},{64,... | collective-permute-start | bytes 811016 | tf_op jit(solution)/shard_map/ppermute | solution.py:269
  38.9 10.4 %collective-permute-start.4 = (f16[528,256]{1,0:T(8,128)(2,1)S(1)}, f16[528,256]{1,0:T(8,128)(2,1)S(1)}, u32[]{:S(2)}, u32[]{:S(2)}) collective-permute-start(f16[528,256]{1,0:T(8,128)(2,1)S(1)} %get-tuple-element.57), channel_id=1, source_target_pairs={{0,96},{8,104},{16,112},{24,120},{32,0},{40,8},{48,16},{56,24},{64... | collective-permute-start | bytes 811016 | tf_op jit(solution)/shard_map/ppermute | solution.py:269
  40.7 8.5 %collective-permute-start.6 = (f16[512,256]{1,0:T(8,128)(2,1)S(1)}, f16[512,256]{1,0:T(8,128)(2,1)S(1)}, u32[]{:S(2)}, u32[]{:S(2)}) collective-permute-start(f16[512,256]{1,0:T(8,128)(2,1)S(1)} %pad_maximum_fusion.2), channel_id=1, source_target_pairs={{0,2},{1,3},{2,4},{3,5},{4,6},{5,7},{6,0},{7,1},{8,10},{9,11},{10,... | collective-permute-start | bytes 786440 | tf_op jit(solution)/shard_map/ppermute | solution.py:269
  49.2 0.8 copy-start.5
  49.2 0.8 copy-start.7
  49.4 0.8 copy-start.4
  49.4 8.4 %collective-permute-start.10 = (f16[256,256]{1,0:T(8,128)(2,1)S(1)}, f16[256,256]{1,0:T(8,128)(2,1)S(1)}, u32[]{:S(2)}, u32[]{:S(2)}) collective-permute-start(f16[256,256]{1,0:T(8,128)(2,1)S(1)} %dynamic-slice_convert_fusion.1), channel_id=1, source_target_pairs={{0,1},{1,0},{2,3},{3,2},{4,5},{5,4},{6,7},{7,6},{8,9},{9,8},{10,11... | collective-permute-start | bytes 393224 | tf_op jit(solution)/shard_map/ppermute | solution.py:269
  50.2 3.6 %copy-start.6 = (f16[528,256]{1,0:T(8,128)(2,1)S(1)}, f16[528,256]{1,0:T(8,128)(2,1)}, u32[]{:S(2)}) copy-start(f16[528,256]{1,0:T(8,128)(2,1)} %copy-done.5) | copy-start | bytes 811012
  50.2 3.6 %copy-start.8 = (f16[528,256]{1,0:T(8,128)(2,1)S(1)}, f16[528,256]{1,0:T(8,128)(2,1)}, u32[]{:S(2)}) copy-start(f16[528,256]{1,0:T(8,128)(2,1)} %copy-done.7) | copy-start | bytes 811012
  54.9 12.6 %collective-permute-start.9 = (f16[1056,256]{1,0:T(8,128)(2,1)}, f16[1056,256]{1,0:T(8,128)(2,1)}, u32[]{:S(2)}, u32[]{:S(2)}) collective-permute-start(f16[1056,256]{1,0:T(8,128)(2,1)} %pad_maximum_fusion.1), channel_id=1, source_target_pairs={{0,96},{8,104},{16,112},{24,120},{32,0},{40,8},{48,16},{56,24},{64... | collective-permute-start | bytes 1622024 | tf_op jit(solution)/shard_map/ppermute | solution.py:269
  57.4 13.3 %collective-permute-start.8 = (f16[1056,256]{1,0:T(8,128)(2,1)}, f16[1056,256]{1,0:T(8,128)(2,1)}, u32[]{:S(2)}, u32[]{:S(2)}) collective-permute-start(f16[1056,256]{1,0:T(8,128)(2,1)} %pad_maximum_fusion), channel_id=1, source_target_pairs={{0,32},{8,40},{16,48},{24,56},{32,64},{40,72},{48,80},{56,88},{64,... | collective-permute-start | bytes 1622024 | tf_op jit(solution)/shard_map/ppermute | solution.py:269
  60.1 6.6 %collective-permute-start.11 = (f16[256,256]{1,0:T(8,128)(2,1)S(1)}, f16[256,256]{1,0:T(8,128)(2,1)S(1)}, u32[]{:S(2)}, u32[]{:S(2)}) collective-permute-start(f16[256,256]{1,0:T(8,128)(2,1)S(1)} %divide_convert_fusion), channel_id=1, source_target_pairs={{0,1},{1,0},{2,3},{3,2},{4,5},{5,4},{6,7},{7,6},{8,9},{9,8},{10,11... | collective-permute-start | bytes 393224 | tf_op jit(solution)/shard_map/ppermute | solution.py:269
  72.0 1.0 copy-start.3
  73.0 7.9 %collective-permute-start.12 = (f16[528,256]{1,0:T(8,128)(2,1)S(1)}, f16[528,256]{1,0:T(8,128)(2,1)S(1)}, u32[]{:S(2)}, u32[]{:S(2)}) collective-permute-start(f16[528,256]{1,0:T(8,128)(2,1)S(1)} %dynamic-slice_convert_fusion), channel_id=1, source_target_pairs={{0,16},{8,24},{16,0},{24,8},{32,48},{40,56},{48,32},{56,40},{64,80... | collective-permute-start | bytes 811016 | tf_op jit(solution)/shard_map/ppermute | solution.py:269
  73.3 7.7 %collective-permute-start.13 = (f16[512,256]{1,0:T(8,128)(2,1)S(1)}, f16[512,256]{1,0:T(8,128)(2,1)S(1)}, u32[]{:S(2)}, u32[]{:S(2)}) collective-permute-start(f16[512,256]{1,0:T(8,128)(2,1)S(1)} %pad_maximum_fusion.4), channel_id=1, source_target_pairs={{0,2},{1,3},{2,4},{3,5},{4,6},{5,7},{6,0},{7,1},{8,10},{9,11},{10,... | collective-permute-start | bytes 786440 | tf_op jit(solution)/shard_map/ppermute | solution.py:269
  73.4 7.6 %collective-permute-start.14 = (f16[512,256]{1,0:T(8,128)(2,1)S(1)}, f16[512,256]{1,0:T(8,128)(2,1)S(1)}, u32[]{:S(2)}, u32[]{:S(2)}) collective-permute-start(f16[512,256]{1,0:T(8,128)(2,1)S(1)} %pad_maximum_fusion.4), channel_id=1, source_target_pairs={{0,6},{1,7},{2,0},{3,1},{4,2},{5,3},{6,4},{7,5},{8,14},{9,15},{10,... | collective-permute-start | bytes 786440 | tf_op jit(solution)/shard_map/ppermute | solution.py:269
  82.1 5.2 %collective-permute-start.17 = (f32[1,256]{1,0:T(1,128)S(1)}, f32[1,256]{1,0:T(1,128)S(1)}, u32[]{:S(2)}, u32[]{:S(2)}) collective-permute-start(f32[1,256]{1,0:T(1,128)S(1)} %slice_multiply_fusion.1), channel_id=1, source_target_pairs={{0,1},{1,0},{2,3},{3,2},{4,5},{5,4},{6,7},{7,6},{8,9},{9,8},{10,11... | collective-permute-start | bytes 3080 | tf_op jit(solution)/shard_map/ppermute | solution.py:269
  87.2 8.3 %collective-permute-start.18 = (f32[1,256]{1,0:T(1,128)S(1)}, f32[1,256]{1,0:T(1,128)S(1)}, u32[]{:S(2)}, u32[]{:S(2)}) collective-permute-start(f32[1,256]{1,0:T(1,128)S(1)} %fusion.9), channel_id=1, source_target_pairs={{0,2},{1,3},{2,4},{3,5},{4,6},{5,7},{6,0},{7,1},{8,10},{9,11},{10,... | collective-permute-start | bytes 3080 | tf_op jit(solution)/shard_map/ppermute | solution.py:269
  88.0 7.5 %collective-permute-start.19 = (f32[1,256]{1,0:T(1,128)S(1)}, f32[1,256]{1,0:T(1,128)S(1)}, u32[]{:S(2)}, u32[]{:S(2)}) collective-permute-start(f32[1,256]{1,0:T(1,128)S(1)} %fusion.9), channel_id=1, source_target_pairs={{0,6},{1,7},{2,0},{3,1},{4,2},{5,3},{6,4},{7,5},{8,14},{9,15},{10,... | collective-permute-start | bytes 3080 | tf_op jit(solution)/shard_map/ppermute | solution.py:269
  90.5 5.1 %collective-permute-start.20 = (f32[1,256]{1,0:T(1,128)S(1)}, f32[1,256]{1,0:T(1,128)S(1)}, u32[]{:S(2)}, u32[]{:S(2)}) collective-permute-start(f32[1,256]{1,0:T(1,128)S(1)} %fusion.9), channel_id=1, source_target_pairs={{0,4},{1,5},{2,6},{3,7},{4,0},{5,1},{6,2},{7,3},{8,12},{9,13},{10,... | collective-permute-start | bytes 3080 | tf_op jit(solution)/shard_map/ppermute | solution.py:269
  92.1 6.2 %collective-permute-start.15 = (f16[256,256]{1,0:T(8,128)(2,1)S(1)}, f16[256,256]{1,0:T(8,128)(2,1)S(1)}, u32[]{:S(2)}, u32[]{:S(2)}) collective-permute-start(f16[256,256]{1,0:T(8,128)(2,1)S(1)} %slice.78), channel_id=1, source_target_pairs={{0,2},{1,3},{2,4},{3,5},{4,6},{5,7},{6,0},{7,1},{8,10},{9,11},{10,... | collective-permute-start | bytes 393224 | tf_op jit(solution)/shard_map/ppermute | solution.py:269
  93.5 5.0 %collective-permute-start.16 = (f16[256,256]{1,0:T(8,128)(2,1)S(1)}, f16[256,256]{1,0:T(8,128)(2,1)S(1)}, u32[]{:S(2)}, u32[]{:S(2)}) collective-permute-start(f16[256,256]{1,0:T(8,128)(2,1)S(1)} %slice.79), channel_id=1, source_target_pairs={{0,6},{1,7},{2,0},{3,1},{4,2},{5,3},{6,4},{7,5},{8,14},{9,15},{10,... | collective-permute-start | bytes 393224 | tf_op jit(solution)/shard_map/ppermute | solution.py:269

commit v4 on v3

--- a/solution.py
+++ b/solution.py
@@ -13,7 +13,7 @@
 N_Z, N_X_HI = 4, 2
 WORD_SCALE = 2.0**-7
 DOC_SCALE = 2.0**-8
-TOTAL_SCALE = 2.0**-9
+TOTAL_SCALE = 2.0**-6
 TOTAL_ROWS = 16
 
 
@@ -52,7 +52,8 @@
     z = vocab_index_ref[0] // N_X_HI
     dest_blocks = blocks // (N_Y * N_X_LO * N_CORE)
 
-    part_rows = dest_blocks * tile_words + TOTAL_ROWS
+    half_docs = tile_docs // N_X_HI
+    half_rows = half_docs + TOTAL_ROWS
 
     def word_place(block):
         dest = block // dest_blocks
@@ -61,9 +62,8 @@
         step = lax.rem(dest // (N_CORE * N_X_LO) - y + N_Y, N_Y)
         other = jnp.where(core == own_core, 0, 1)
         place = jnp.where(step == 0, 3, jnp.where(step == 2, 0, (step + 1) // 2))
-        return ((other * N_Y + place) * N_X_LO + x_lo) * part_rows + (
-            lax.rem(block, dest_blocks) * tile_words
-        )
+        part = (other * N_Y + place) * N_X_LO + x_lo
+        return (part * dest_blocks + lax.rem(block, dest_blocks)) * tile_words
 
     doc_copy = pltpu.make_async_copy(doc_hbm, doc_rows, topics_sem.at[0])
     word_copy = pltpu.make_async_copy(word_hbm, word_rows, topics_sem.at[1])
@@ -158,13 +158,15 @@
 
     def add_terms(item, ratio, docs, words, word_blocks):
         doc_step = lax.rem(item_doc[item] - z + N_Z, N_Z)
-        doc_to = pl.ds(pl.multiple_of(doc_step * tile_docs, tile_docs), tile_docs)
-        doc_sums[doc_to, :] += jnp.dot(ratio, words, preferred_element_type=jnp.float32)
+        doc_terms = jnp.dot(ratio, words, preferred_element_type=jnp.float32)
+        for half in range(N_X_HI):
+            to = pl.multiple_of((doc_step * N_X_HI + half) * half_rows, TOTAL_ROWS)
+            doc_sums[pl.ds(to, half_docs), :] += doc_terms[half * half_docs : (half + 1) * half_docs]
         terms = lax.dot_general(
             ratio, docs, (((0,), (0,)), ((), ())), preferred_element_type=jnp.float32
         )
         for n, block in enumerate(word_blocks):
-            to = pl.multiple_of(word_place(block), TOTAL_ROWS)
+            to = pl.multiple_of(word_place(block), tile_words)
             word_sums[pl.ds(to, tile_words), :] += terms[n * tile_words : (n + 1) * tile_words]
 
     def run_items(n, carry):
@@ -186,24 +188,24 @@
         copy.start()
         return copy
 
-    leaving = [
-        leave(step, doc_sums.at[pl.ds(step * tile_docs, tile_docs)], doc_parts_out[step])
-        for step in range(N_Z)
-    ]
-    total = jnp.zeros((1, doc_rows.shape[1]), jnp.float32)
-    for step in range(N_Z):
-        at = pl.multiple_of(lax.rem(z + step, N_Z) * tile_docs, tile_docs)
-        topics = doc_rows[pl.ds(at, tile_docs), :].astype(jnp.float32)
-        sums = doc_sums[pl.ds(step * tile_docs, tile_docs), :]
-        total = total + jnp.sum(topics * sums, axis=0, keepdims=True)
-    total = jnp.broadcast_to(total * TOTAL_SCALE, (TOTAL_ROWS, doc_rows.shape[1]))
-    for n in range(word_sums.shape[0] // part_rows):
-        word_sums[(n + 1) * part_rows - TOTAL_ROWS : (n + 1) * part_rows, :] = total
-    near_rows = N_X_LO * part_rows
-    start_row = N_Y * near_rows
+    leaving = []
+    start_row = N_Y * N_X_LO * dest_blocks * tile_words
     for out in send_out:
         leaving.append(leave(len(leaving), word_sums.at[pl.ds(start_row, out.shape[0])], out))
         start_row += out.shape[0]
+    total = jnp.zeros((1, doc_rows.shape[1]), jnp.float32)
+    for step in range(N_Z):
+        for half in range(N_X_HI):
+            at = pl.multiple_of(lax.rem(z + step, N_Z) * tile_docs + half * half_docs, half_docs)
+            topics = doc_rows[pl.ds(at, half_docs), :].astype(jnp.float32)
+            sums = doc_sums[pl.ds((step * N_X_HI + half) * half_rows, half_docs), :]
+            total = total + jnp.sum(topics * sums, axis=0, keepdims=True)
+    total = jnp.broadcast_to(total * TOTAL_SCALE, (TOTAL_ROWS, doc_rows.shape[1]))
+    for n in range(N_Z * N_X_HI):
+        doc_sums[(n + 1) * half_rows - TOTAL_ROWS : (n + 1) * half_rows, :] = total
+    for step in range(N_Z):
+        source = doc_sums.at[pl.ds(step * N_X_HI * half_rows, N_X_HI * half_rows)]
+        leaving.append(leave(len(leaving), source, doc_parts_out[step]))
     start_row = 0
     for out in keep_out:
         leaving.append(leave(len(leaving), word_sums.at[pl.ds(start_row, out.shape[0])], out))
@@ -220,11 +222,13 @@
     topics = doc_topics.shape[1]
     doc_blocks = doc_topics.shape[0] // tile_docs
     items = slots + doc_blocks + AT_ONCE
-    doc_part = jax.ShapeDtypeStruct((doc_topics.shape[0] // N_Z, topics), jnp.float32)
-    word_rows = word_topics.shape[0] // (N_CORE * N_Y) + N_X_LO * TOTAL_ROWS
+    doc_rows = doc_topics.shape[0] // N_Z + N_X_HI * TOTAL_ROWS
+    doc_part = jax.ShapeDtypeStruct((doc_rows, topics), jnp.float32)
+    word_rows = word_topics.shape[0] // (N_CORE * N_Y)
     first_part = jax.ShapeDtypeStruct((word_rows, topics), jnp.float32)
     later_part = jax.ShapeDtypeStruct(((N_Y - 1) * word_rows, topics), jnp.float32)
     smem = pl.BlockSpec(memory_space=pltpu.SMEM)
+    source = pl.BlockSpec(memory_space=pltpu.HBM)
     hbm = pl.BlockSpec(memory_space=pl.ANY)
     return pl.pallas_call(
         tiles_kernel,
@@ -233,13 +237,13 @@
             (first_part, later_part),
             (first_part, later_part),
         ),
-        in_specs=[hbm] + [smem] * 3 + [hbm] * 4,
+        in_specs=[source] + [smem] * 3 + [source] * 4,
         out_specs=((hbm,) * N_Z, (hbm,) * 2, (hbm,) * 2),
         scratch_shapes=[
             pltpu.SMEM(pair_list.shape[1:], jnp.int32),
             pltpu.VMEM(weight_table.shape, jnp.float32),
-            pltpu.VMEM(doc_topics.shape, jnp.float32),
-            pltpu.VMEM((N_CORE * N_Y * word_rows, topics), jnp.float32),
+            pltpu.VMEM((N_Z * doc_rows, topics), jnp.float32),
+            pltpu.VMEM(word_topics.shape, jnp.float32),
             pltpu.VMEM(doc_topics.shape, doc_topics.dtype),
             pltpu.VMEM(word_topics.shape, word_topics.dtype),
             pltpu.VMEM((SLOTS, 2, tile_docs, tile_words), counts_all.dtype),
@@ -277,6 +281,10 @@
     return value.astype(jnp.float32)
 
 
+def rows_around(value, before, after):
+    return lax.pad(value, jnp.zeros((), value.dtype), ((before, after, 0), (0, 0, 0)))
+
+
 def on_device(doc_topics, word_topics, word_weights, tile_pairs, tile_counts, tile_load):
     n_docs, n_vocab = lax.axis_size("docs"), lax.axis_size("vocab")
     docs_index, vocab_index = lax.axis_index("docs"), lax.axis_index("vocab")
@@ -286,6 +294,8 @@
     to_x_lo = moves("docs", n_docs, lambda n: n ^ N_CORE)
     y_up = moves("docs", n_docs, lambda n: n + N_X_LO * N_CORE)
     y_down = moves("docs", n_docs, lambda n: n - N_X_LO * N_CORE)
+    y_pair = moves("docs", n_docs, lambda n: n ^ (N_X_LO * N_CORE))
+    y_cross = moves("docs", n_docs, lambda n: n ^ ((N_Y - 1) * N_X_LO * N_CORE))
     to_x_hi = moves("vocab", n_vocab, lambda n: n ^ 1)
     z_up = moves("vocab", n_vocab, lambda n: n + N_X_HI)
     z_down = moves("vocab", n_vocab, lambda n: n - N_X_HI)
@@ -305,7 +315,6 @@
         counts_all,
     )
 
-    z_across = moves("vocab", n_vocab, lambda n: n + 2 * N_X_HI)
     meet = lambda *values: lax.optimization_barrier(values)
     near_rows = keep[0].shape[0]
     word_rows = near_rows // N_X_LO
@@ -321,63 +330,70 @@
     word_up = y_up(to_half(far[:word_rows]))
     word_down = y_down(to_half(far[word_rows:]))
     near_far = to_core(send[1])
-    doc_below = z_up(
-        to_half(jnp.concatenate([part[1][:doc_rows] + to_float(doc_up), part[1][doc_rows:]]))
-    )
-    doc_above = z_down(
-        to_half(jnp.concatenate([part[3][:doc_rows], part[3][doc_rows:] + to_float(doc_down)]))
-    )
+    doc_below = z_up(to_half(part[1] + rows_around(to_float(doc_up), 0, doc_rows)))
+    doc_above = z_down(to_half(part[3] + rows_around(to_float(doc_down), doc_rows, 0)))
     word_up, word_down, near_far, doc_below, doc_above = meet(
         word_up, word_down, near_far, doc_below, doc_above
     )
 
-    near = (keep[1] + near_far) * WORD_SCALE
-    above, below, here = near[:near_rows], near[near_rows : 2 * near_rows], near[2 * near_rows :]
-    word_below = y_up(
-        to_half(jnp.concatenate([above[:word_rows] + to_float(word_up), above[word_rows:]]))
-    )
-    word_above = y_down(
-        to_half(jnp.concatenate([below[:word_rows], below[word_rows:] + to_float(word_down)]))
-    )
-    doc_pair = part[0] + to_float(doc_below) + to_float(doc_above)
-    doc_mine = lax.dynamic_slice_in_dim(doc_pair, x_hi * doc_rows, doc_rows, 0)
-    doc_other = lax.dynamic_slice_in_dim(doc_pair, (1 - x_hi) * doc_rows, doc_rows, 0)
+    above = (keep[1][:near_rows] + near_far[:near_rows]) * WORD_SCALE
+    below = (
+        keep[1][near_rows : 2 * near_rows] + near_far[near_rows : 2 * near_rows]
+    ) * WORD_SCALE
+    word_below = y_up(to_half(above + rows_around(to_float(word_up), 0, word_rows)))
+    word_above = y_down(to_half(below + rows_around(to_float(word_down), word_rows, 0)))
+
+    def doc_half(which):
+        rows = [
+            lax.dynamic_slice_in_dim(value, which * doc_rows, doc_rows, 0)
+            for value in (doc_parts[0], doc_below, doc_above)
+        ]
+        return rows[0] * DOC_SCALE + to_float(rows[1]) + to_float(rows[2])
+
+    doc_mine, doc_other = doc_half(x_hi), doc_half(1 - x_hi)
     doc_sums = (doc_mine + to_float(to_x_hi(to_half(doc_other)))) / DOC_SCALE
-    own_docs = lax.dynamic_slice_in_dim(doc_topics, vocab_index * doc_rows, doc_rows, 0)
-    doc_scaled = own_docs.astype(jnp.float32) * doc_sums + prior_doc
+    own_rows = doc_topics.shape[0] // n_vocab
+    own_docs = lax.dynamic_slice_in_dim(doc_topics, vocab_index * own_rows, own_rows, 0)
+    doc_scaled = own_docs.astype(jnp.float32) * doc_sums[:own_rows] + prior_doc
     doc_block = to_half(
         doc_topics.shape[1] * doc_scaled / jnp.sum(doc_scaled, axis=1, keepdims=True)
     )
     doc_far = to_x_hi(doc_block)
-    word_below, word_above, doc_block, doc_far = meet(word_below, word_above, doc_block, doc_far)
-
-    word_pair = here + to_float(word_below) + to_float(word_above)
-    word_mine = lax.dynamic_slice_in_dim(word_pair, x_lo * word_rows, word_rows, 0)
-    word_other = lax.dynamic_slice_in_dim(word_pair, (1 - x_lo) * word_rows, word_rows, 0)
-    word_far = to_x_lo(to_half(word_other))
-    doc_here = jnp.concatenate(
-        [
-            jnp.where(x_hi == 0, doc_block, doc_far),
-            jnp.where(x_hi == 0, doc_far, doc_block),
-        ]
+    column = doc_sums[own_rows : own_rows + 1] / TOTAL_SCALE
+    column = column + to_core(column)
+    column = column + y_pair(column)
+    word_below, word_above, doc_block, doc_far, column = meet(
+        word_below, word_above, doc_block, doc_far, column
+    )
+
+    def word_half(which):
+        at = which * word_rows
+        here = lax.dynamic_slice_in_dim(keep[1], 2 * near_rows + at, word_rows, 0)
+        far = lax.dynamic_slice_in_dim(near_far, 2 * near_rows + at, word_rows, 0)
+        below = lax.dynamic_slice_in_dim(word_below, at, word_rows, 0)
+        above = lax.dynamic_slice_in_dim(word_above, at, word_rows, 0)
+        return (here + far) * WORD_SCALE + to_float(below) + to_float(above)
+
+    word_far = to_x_lo(to_half(word_half(1 - x_lo)))
+    doc_here = rows_around(jnp.where(x_hi == 0, doc_block, doc_far), 0, own_rows) + rows_around(
+        jnp.where(x_hi == 0, doc_far, doc_block), own_rows, 0
     )
     doc_below, doc_above = z_up(doc_here), z_down(doc_here)
-    word_far, doc_below, doc_above = meet(word_far, doc_below, doc_above)
-
-    low_across, high_across = z_up(doc_below[:doc_rows]), z_down(doc_above[doc_rows:])
+    column = column + y_cross(column)
+    column = column + to_x_lo(column)
+    word_far, doc_below, doc_above, column = meet(word_far, doc_below, doc_above, column)
+
+    doc_across = z_up(doc_below)
+    doc_next = jnp.zeros(doc_topics.shape, jnp.float32)
+    for step, value in ((0, doc_here), (1, doc_above), (3, doc_below), (2, doc_across)):
+        at = (z + step) % N_Z * (N_X_HI * own_rows)
+        doc_next = lax.dynamic_update_slice_in_dim(doc_next, to_float(value), at, 0)
     row_count = word_topics.shape[0] // n_docs
-    word_sums = (word_mine + to_float(word_far)) / WORD_SCALE
-    column = word_sums[row_count : row_count + 1] / TOTAL_SCALE
-    column = column + to_x_hi(column)
-    column = column + z_up(column) + z_down(column) + z_across(column)
+    word_sums = (word_half(x_lo) + to_float(word_far)) / WORD_SCALE
     vocab_total = word_topics.shape[0] * n_vocab
     own_words = lax.dynamic_slice_in_dim(word_topics, docs_index * row_count, row_count, 0)
-    word_scaled = own_words.astype(jnp.float32) * word_sums[:row_count] + prior_word
+    word_scaled = own_words.astype(jnp.float32) * word_sums + prior_word
     word_next = vocab_total * word_scaled / (column + vocab_total * prior_word)
-    by_step = (doc_here, doc_above, jnp.concatenate([low_across, high_across]), doc_below)
-    doc_next = jnp.concatenate(
-        [to_float(lax.select_n((place - z) % N_Z, *by_step)) for place in range(N_Z)]
-    )
     return (doc_next, word_next)
 
 

time: 102 us -> 86.9 us (0.85); the launches traced: 101 us -> 86.6 us
  Pallas kernels: 21.1 us -> 10.5 us
  starting transfers between devices: 30.5 us -> 37.7 us
  other arithmetic: 14.8 us -> 9.15 us
  waiting for transfers between devices: 28.4 us -> 23.5 us
    pallas_call x1, Pallas kernels: 21.1 us -> 10.5 us  [run_tiles(): pl.pallas_call(tiles_kernel, out_shape=((doc_part,) * N_Z, (first_part, l...]
    ppermute x21 -> x20, starting transfers between devices: 30.5 us -> 37.7 us  [moves(): lax.ppermute(value, axis, [(n, move(n) % size) for n in range(size)])]
    ppermute x21 -> x20, waiting for transfers between devices: 28.4 us -> 23.5 us  [moves(): lax.ppermute(value, axis, [(n, move(n) % size) for n in range(size)])]
    convert_element_type x3 -> x6, other arithmetic: 1.16 us -> 5.15 us  [to_half(): return value.astype(jnp.float16)]
    another operation x6 -> x2, other arithmetic: 3.96 us -> 0.21 us
    concatenate x6 -> x0, other arithmetic: 3.59 us -> none  [the longest x1 1.55 us: on_device(): jnp.concatenate([to_float(lax.select_n((place - z) % N_Z, *by_step)) for...]
    add x3 -> x5, other arithmetic: 1.45 us -> 0.08 us  [the longest x1 0.06 us: on_device(): rows_around(jnp.where(x_hi == 0, doc_block, doc_far), 0, own_rows)]
    div x2, other arithmetic: 1.11 us -> 0.09 us  [the longest x1 0.09 us: on_device(): doc_sums = (doc_mine + to_float(to_x_hi(to_half(doc_other)))) / DOC_SCALE]
  transfers between devices with their start and end apart: 21 -> 20, of which waited for: 10 -> 7; matrix products, arithmetic and copies ran while one was open for 10% -> 11% of each run, Pallas kernels for 0% -> 0%
where the time goes in v4:
time: 86.9 us; the launch traced here: 86.6 us
  starting transfers between devices  37.7 us (43%)
  waiting for transfers between devices  23.5 us (27%)
  Pallas kernels  10.5 us (12%)
  other arithmetic  9.15 us (11%)
  local copies, waits for them, and re-layouts  4.24 us (5%)
  between operations  1.55 us (2%)
    ppermute x20, starting transfers between devices, moves(): lax.ppermute(value, axis, [(n, move(n) % size) for n in range(size)])  37.7 us
    ppermute x20, waiting for transfers between devices, moves(): lax.ppermute(value, axis, [(n, move(n) % size) for n in range(size)])  23.5 us
    pallas_call x1, Pallas kernels, run_tiles(): pl.pallas_call(tiles_kernel, out_shape=((doc_part,) * N_Z, (first_part, l...  10.5 us
    convert_element_type x6, other arithmetic, to_half(): return value.astype(jnp.float16)  5.15 us
    unnamed x8, local copies, waits for them, and re-layouts  3.95 us
    div x1, other arithmetic, on_device(): word_next = vocab_total * word_scaled / (column + vocab_total * prior_word)  2.34 us
  transfers between devices with their start and end apart: 20, of which 7 were waited for; matrix products, arithmetic and copies ran while one was open for 11% of the time, Pallas kernels for 0%

profile of v4, /device:TPU:0, one launch (start us, length us, event | category | flops | bytes accessed | tf_op | source)
XLA Modules:
  0.0 86.6 jit_solution(6711322659850743679)
XLA Ops:
  1.3 0.0 copy-start
  1.3 1.2 %copy-done = bf16[2048,256]{1,0:T(8,128)(2,1)S(1)} copy-done((bf16[2048,256]{1,0:T(8,128)(2,1)S(1)}, bf16[2048,256]{1,0:T(8,128)(2,1)}, u32[]{:S(2)}) %copy-start) | copy-done | bytes 1048600
  2.5 0.8 copy-done.1
  3.3 0.7 copy-done.2
  3.9 10.5 %tiles.1 = (f32[544,256]{1,0:T(8,128)S(1)}, f32[544,256]{1,0:T(8,128)S(1)}, f32[544,256]{1,0:T(8,128)S(1)}, f32[544,256]{1,0:T(8,128)S(1)}, f32[1024,256]{1,0:T(...) custom-call(s32[1,1,96]{2,1,0:T(1,128)S(1)} %copy-done.2, ...), custom_call_target="tpu_custom_call" | custom-call | tf_op jit(solution)/shard_map/tiles/pallas_call | solution.py:233
  14.4 0.3 collective-permute-start.5
  14.7 0.2 collective-permute-start
  15.0 0.1 multiply_convert_fusion.1
  15.0 0.1 fusion.4
  15.1 2.7 %collective-permute-start.1 = (f16[272,256]{1,0:T(8,128)(2,1)S(1)}, f16[272,256]{1,0:T(8,128)(2,1)S(1)}, u32[]{:S(2)}, u32[]{:S(2)}) collective-permute-start(f16[272,256]{1,0:T(8,128)(2,1)S(1)} %get-tuple-element.57), channel_id=1, source_target_pairs={{0,2},{1,3},{2,4},{3,5},{4,6},{5,7},{6,0},{7,1},{8,10},{9,11},{10,... | collective-permute-start | bytes 417800 | tf_op jit(solution)/shard_map/ppermute | solution.py:273
  17.8 3.5 %collective-permute-start.2 = (f16[272,256]{1,0:T(8,128)(2,1)S(1)}, f16[272,256]{1,0:T(8,128)(2,1)S(1)}, u32[]{:S(2)}, u32[]{:S(2)}) collective-permute-start(f16[272,256]{1,0:T(8,128)(2,1)S(1)} %get-tuple-element.56), channel_id=1, source_target_pairs={{0,6},{1,7},{2,0},{3,1},{4,2},{5,3},{6,4},{7,5},{8,14},{9,15},{10,... | collective-permute-start | bytes 417800 | tf_op jit(solution)/shard_map/ppermute | solution.py:273
  21.3 4.2 %collective-permute-done.1 = f16[272,256]{1,0:T(8,128)(2,1)S(1)} collective-permute-done((f16[272,256]{1,0:T(8,128)(2,1)S(1)}, f16[272,256]{1,0:T(8,128)(2,1)S(1)}, u32[]{:S(2)}, u32[]{:S(2)}) %collective-permute-start.1) | collective-permute-done | bytes 139296 | tf_op jit(solution)/shard_map/ppermute | solution.py:273
  25.4 0.0 collective-permute-done.2
  25.4 0.0 collective-permute-done
  25.4 0.1 add_convert_fusion.2
  25.5 3.1 %collective-permute-start.7 = (f16[544,256]{1,0:T(8,128)(2,1)S(1)}, f16[544,256]{1,0:T(8,128)(2,1)S(1)}, u32[]{:S(2)}, u32[]{:S(2)}) collective-permute-start(f16[544,256]{1,0:T(8,128)(2,1)S(1)} %add_convert_fusion.2), channel_id=1, source_target_pairs={{0,6},{1,7},{2,0},{3,1},{4,2},{5,3},{6,4},{7,5},{8,14},{9,15},{10,... | collective-permute-start | bytes 835592 | tf_op jit(solution)/shard_map/ppermute | solution.py:273
  28.7 0.1 add_convert_fusion.3
  28.7 0.1 collective-permute-start.6
  28.8 0.2 multiply_convert_fusion
  29.0 0.1 fusion.3
  29.1 3.2 %collective-permute-start.3 = (f16[512,256]{1,0:T(8,128)(2,1)S(1)}, f16[512,256]{1,0:T(8,128)(2,1)S(1)}, u32[]{:S(2)}, u32[]{:S(2)}) collective-permute-start(f16[512,256]{1,0:T(8,128)(2,1)S(1)} %get-tuple-element.55), channel_id=1, source_target_pairs={{0,32},{8,40},{16,48},{24,56},{32,64},{40,72},{48,80},{56,88},{64,... | collective-permute-start | bytes 786440 | tf_op jit(solution)/shard_map/ppermute | solution.py:273
  32.3 4.2 %collective-permute-start.4 = (f16[512,256]{1,0:T(8,128)(2,1)S(1)}, f16[512,256]{1,0:T(8,128)(2,1)S(1)}, u32[]{:S(2)}, u32[]{:S(2)}) collective-permute-start(f16[512,256]{1,0:T(8,128)(2,1)S(1)} %get-tuple-element.54), channel_id=1, source_target_pairs={{0,96},{8,104},{16,112},{24,120},{32,0},{40,8},{48,16},{56,24},{64... | collective-permute-start | bytes 786440 | tf_op jit(solution)/shard_map/ppermute | solution.py:273
  36.6 5.0 %collective-permute-done.3 = f16[512,256]{1,0:T(8,128)(2,1)S(1)} collective-permute-done((f16[512,256]{1,0:T(8,128)(2,1)S(1)}, f16[512,256]{1,0:T(8,128)(2,1)S(1)}, u32[]{:S(2)}, u32[]{:S(2)}) %collective-permute-start.3) | collective-permute-done | bytes 262176 | tf_op jit(solution)/shard_map/ppermute | solution.py:273
  41.6 0.0 collective-permute-done.4
  41.6 0.0 collective-permute-done.7
  41.6 0.0 collective-permute-done.6
  41.6 0.0 collective-permute-done.5
  41.7 0.1 add_convert_fusion.5
  41.7 6.8 %collective-permute-start.10 = (f16[272,256]{1,0:T(8,128)(2,1)S(1)}, f16[272,256]{1,0:T(8,128)(2,1)S(1)}, u32[]{:S(2)}, u32[]{:S(2)}) collective-permute-start(f16[272,256]{1,0:T(8,128)(2,1)S(1)} %add_convert_fusion.5), channel_id=1, source_target_pairs={{0,1},{1,0},{2,3},{3,2},{4,5},{5,4},{6,7},{7,6},{8,9},{9,8},{10,11... | collective-permute-start | bytes 417800 | tf_op jit(solution)/shard_map/ppermute | solution.py:273
  48.5 2.5 %add_convert_fusion = (f16[1024,256]{1,0:T(8,128)(2,1)S(1)}, f16[1024,256]{1,0:T(8,128)(2,1)S(1)}) fusion(f32[3072,256]{1,0:T(8,128)} %collective-permute-done.5, f32[3072,256]{1,0:T(8,128)} %get-tuple-element.27, f16[512,256]{1,0:T(8,128)(2,1)S(1)} %collective-permute-done.4, f16[512,256]{1,0:T(8,128)(2,1)S(1)} %collective-permute-done.3), kind=kLoop, calls=%fused_computation | loop fusion | flops 2621440 | bytes 5767168 | tf_op jit(solution)/shard_map/convert_element_type | solution.py:277
  51.1 1.0 %collective-permute-start.8 = (f16[1024,256]{1,0:T(8,128)(2,1)S(1)}, f16[1024,256]{1,0:T(8,128)(2,1)S(1)}, u32[]{:S(2)}, u32[]{:S(2)}) collective-permute-start(f16[1024,256]{1,0:T(8,128)(2,1)S(1)} %get-tuple-element.53), channel_id=1, source_target_pairs={{0,32},{8,40},{16,48},{24,56},{32,64},{40,72},{48,80},{56,88},{64,... | collective-permute-start | bytes 1572872 | tf_op jit(solution)/shard_map/ppermute | solution.py:273
  52.1 2.3 %collective-permute-start.9 = (f16[1024,256]{1,0:T(8,128)(2,1)S(1)}, f16[1024,256]{1,0:T(8,128)(2,1)S(1)}, u32[]{:S(2)}, u32[]{:S(2)}) collective-permute-start(f16[1024,256]{1,0:T(8,128)(2,1)S(1)} %get-tuple-element.52), channel_id=1, source_target_pairs={{0,96},{8,104},{16,112},{24,120},{32,0},{40,8},{48,16},{56,24},{64... | collective-permute-start | bytes 1572872 | tf_op jit(solution)/shard_map/ppermute | solution.py:273
  54.4 0.0 collective-permute-done.10
  54.4 0.1 add_multiply_fusion
  54.5 0.1 collective-permute-start.12
  54.6 1.0 %fusion.1 = f32[256]{0:T(256)S(1)} fusion(f32[272,256]{1,0:T(8,128)S(1)} %add_multiply_fusion, bf16[2048,256]{1,0:T(8,128)(2,1)} %doc_hbm.1, s32[]{:T(128)S(6)} %select_n.92), kind=kLoop, calls=%fused_computation.18 | loop fusion | flops 261888 | bytes 394244 | tf_op jit(solution)/shard_map/reduce_sum | solution.py:359
  55.6 1.0 %divide_convert_fusion = f16[256,256]{1,0:T(8,128)(2,1)S(1)} fusion(f32[272,256]{1,0:T(8,128)S(1)} %add_multiply_fusion, f32[256]{0:T(256)S(1)} %fusion.1, bf16[2048,256]{1,0:T(8,128)(2,1)} %doc_hbm.1, s32[]{:T(128)S(6)} %select_n.92), kind=kLoop, calls=%fused_computation.17 | loop fusion | flops 393216 | bytes 525316 | tf_op jit(solution)/shard_map/convert_element_type | solution.py:277
  56.7 0.8 collective-permute-start.11
  57.4 0.0 collective-permute-done.12
  57.5 0.9 %collective-permute-start.13 = (f32[1,256]{1,0:T(1,128)S(1)}, f32[1,256]{1,0:T(1,128)S(1)}, u32[]{:S(2)}, u32[]{:S(2)}) collective-permute-start(f32[1,256]{1,0:T(1,128)S(1)} %fusion.2), channel_id=1, source_target_pairs={{0,32},{8,40},{16,48},{24,56},{32,0},{40,8},{48,16},{56,24},{64,96... | collective-permute-start | bytes 3080 | tf_op jit(solution)/shard_map/ppermute | solution.py:273
  58.4 5.4 %collective-permute-done.13 = f32[1,256]{1,0:T(1,128)S(1)} collective-permute-done((f32[1,256]{1,0:T(1,128)S(1)}, f32[1,256]{1,0:T(1,128)S(1)}, u32[]{:S(2)}, u32[]{:S(2)}) %collective-permute-start.13) | collective-permute-done | bytes 1056 | tf_op jit(solution)/shard_map/ppermute | solution.py:273
  63.8 0.3 collective-permute-done.11
  64.1 0.0 collective-permute-done.8
  64.1 0.0 collective-permute-done.9
  64.1 0.1 broadcast_select_fusion.1
  64.2 0.1 pad_add_fusion
  64.3 1.9 %collective-permute-start.15 = (f16[512,256]{1,0:T(8,128)(2,1)S(1)}, f16[512,256]{1,0:T(8,128)(2,1)S(1)}, u32[]{:S(2)}, u32[]{:S(2)}) collective-permute-start(f16[512,256]{1,0:T(8,128)(2,1)S(1)} %pad_add_fusion), channel_id=1, source_target_pairs={{0,2},{1,3},{2,4},{3,5},{4,6},{5,7},{6,0},{7,1},{8,10},{9,11},{10,... | collective-permute-start | bytes 786440 | tf_op jit(solution)/shard_map/ppermute | solution.py:273
  66.2 1.4 %collective-permute-start.16 = (f16[512,256]{1,0:T(8,128)(2,1)S(1)}, f16[512,256]{1,0:T(8,128)(2,1)S(1)}, u32[]{:S(2)}, u32[]{:S(2)}) collective-permute-start(f16[512,256]{1,0:T(8,128)(2,1)S(1)} %pad_add_fusion), channel_id=1, source_target_pairs={{0,6},{1,7},{2,0},{3,1},{4,2},{5,3},{6,4},{7,5},{8,14},{9,15},{10,... | collective-permute-start | bytes 786440 | tf_op jit(solution)/shard_map/ppermute | solution.py:273
  67.6 1.3 %add_convert_fusion.4 = f16[512,256]{1,0:T(8,128)(2,1)S(1)} fusion(f32[3072,256]{1,0:T(8,128)} %collective-permute-done.5, s32[]{:T(128)S(6)} %select_n.102, f32[3072,256]{1,0:T(8,128)} %get-tuple-element.27, f16[1024,256]{1,0:T(8,128)(2,1)S(1)} %collective-permute-done.9, s32[]{:T(128)S(6)} %select_n.103, f16[1024,256]{1,0:T(8,128)(2,1)S(1)} %collective-permute-done.8), kind=kLoop, calls=%fused_computation.10 | loop fusion | flops 917504 | bytes 1835016 | tf_op jit(solution)/shard_map/convert_element_type | solution.py:277
  68.9 0.1 collective-permute-start.14
  69.1 2.3 %collective-permute-start.17 = (f32[1,256]{1,0:T(1,128)S(1)}, f32[1,256]{1,0:T(1,128)S(1)}, u32[]{:S(2)}, u32[]{:S(2)}) collective-permute-start(f32[1,256]{1,0:T(1,128)S(1)} %add.207), channel_id=1, source_target_pairs={{0,96},{8,104},{16,112},{24,120},{32,64},{40,72},{48,80},{56,88},{... | collective-permute-start | bytes 3080 | tf_op jit(solution)/shard_map/ppermute | solution.py:273
  71.4 2.5 %collective-permute-done.17 = f32[1,256]{1,0:T(1,128)S(1)} collective-permute-done((f32[1,256]{1,0:T(1,128)S(1)}, f32[1,256]{1,0:T(1,128)S(1)}, u32[]{:S(2)}, u32[]{:S(2)}) %collective-permute-start.17) | collective-permute-done | bytes 1056 | tf_op jit(solution)/shard_map/ppermute | solution.py:273
  74.0 1.9 %collective-permute-start.18 = (f32[1,256]{1,0:T(1,128)S(1)}, f32[1,256]{1,0:T(1,128)S(1)}, u32[]{:S(2)}, u32[]{:S(2)}) collective-permute-start(f32[1,256]{1,0:T(1,128)S(1)} %add.218), channel_id=1, source_target_pairs={{0,16},{8,24},{16,0},{24,8},{32,48},{40,56},{48,32},{56,40},{64,80... | collective-permute-start | bytes 3080 | tf_op jit(solution)/shard_map/ppermute | solution.py:273
  75.8 0.1 broadcast_in_dim.4
  75.9 0.1 convert_dynamic-update-slice_fusion.3
  76.0 1.5 %collective-permute-done.18 = f32[1,256]{1,0:T(1,128)S(1)} collective-permute-done((f32[1,256]{1,0:T(1,128)S(1)}, f32[1,256]{1,0:T(1,128)S(1)}, u32[]{:S(2)}, u32[]{:S(2)}) %collective-permute-start.18) | collective-permute-done | bytes 1056 | tf_op jit(solution)/shard_map/ppermute | solution.py:273
  77.5 0.0 collective-permute-done.14
  77.6 0.8 collective-permute-start.19
  78.3 0.1 convert_dynamic-update-slice_fusion.2
  78.4 2.3 %multiply_divide_fusion = (f32[512,256]{1,0:T(8,128)}, f32[2048,256]{1,0:T(8,128)S(1)}) fusion(f16[512,256]{1,0:T(8,128)(2,1)S(1)} %collective-permute-done.14, f32[3072,256]{1,0:T(8,128)} %collective-permute-done.5, s32[]{:T(128)S(6)} %select_n.111, f32[3072,256]{1,0:T(8,128)} %get-tuple-element.27, f32[256]{0:T(256)S(1)} %bitcast.7, ...), kind=kLoop, calls=%fused_computation.6 | loop fusion | flops 1966080 | bytes 3408912 | tf_op jit(solution)/shard_map/div | solution.py:396
  80.7 4.5 %collective-permute-done.19 = f16[512,256]{1,0:T(8,128)(2,1)S(1)} collective-permute-done((f16[512,256]{1,0:T(8,128)(2,1)S(1)}, f16[512,256]{1,0:T(8,128)(2,1)S(1)}, u32[]{:S(2)}, u32[]{:S(2)}) %collective-permute-start.19) | collective-permute-done | bytes 262176 | tf_op jit(solution)/shard_map/ppermute | solution.py:273
  85.2 0.1 convert_dynamic-update-slice_fusion
  85.3 0.0 copy-start.3
  85.3 1.3 %copy-done.3 = f32[2048,256]{1,0:T(8,128)} copy-done((f32[2048,256]{1,0:T(8,128)}, f32[2048,256]{1,0:T(8,128)S(1)}, u32[]{:S(2)}) %copy-start.3) | copy-done | bytes 2097176
  (10 shorter events, 0.0 us)
Async XLA Ops:
  1.3 1.2 %copy-start = (bf16[2048,256]{1,0:T(8,128)(2,1)S(1)}, bf16[2048,256]{1,0:T(8,128)(2,1)}, u32[]{:S(2)}) copy-start(bf16[2048,256]{1,0:T(8,128)(2,1)} %doc_hbm.1) | copy-start | bytes 3145732
  2.5 0.8 copy-start.1
  3.3 0.7 copy-start.2
  14.4 27.3 %collective-permute-start.5 = (f32[3072,256]{1,0:T(8,128)}, f32[3072,256]{1,0:T(8,128)}, u32[]{:S(2)}, u32[]{:S(2)}) collective-permute-start(f32[3072,256]{1,0:T(8,128)} %get-tuple-element.32), channel_id=1, source_target_pairs={{0,8},{8,0},{16,24},{24,16},{32,40},{40,32},{48,56},{56,48},{64,72... | collective-permute-start | bytes 9437192 | tf_op jit(solution)/shard_map/ppermute | solution.py:273
  14.7 10.7 %collective-permute-start = (f32[1024,256]{1,0:T(8,128)S(1)}, f32[1024,256]{1,0:T(8,128)S(1)}, u32[]{:S(2)}, u32[]{:S(2)}) collective-permute-start(f32[1024,256]{1,0:T(8,128)S(1)} %get-tuple-element.29), channel_id=1, source_target_pairs={{0,8},{8,0},{16,24},{24,16},{32,40},{40,32},{48,56},{56,48},{64,72... | collective-permute-start | bytes 3145736 | tf_op jit(solution)/shard_map/ppermute | solution.py:273
  15.1 10.3 %collective-permute-start.1 = (f16[272,256]{1,0:T(8,128)(2,1)S(1)}, f16[272,256]{1,0:T(8,128)(2,1)S(1)}, u32[]{:S(2)}, u32[]{:S(2)}) collective-permute-start(f16[272,256]{1,0:T(8,128)(2,1)S(1)} %get-tuple-element.57), channel_id=1, source_target_pairs={{0,2},{1,3},{2,4},{3,5},{4,6},{5,7},{6,0},{7,1},{8,10},{9,11},{10,... | collective-permute-start | bytes 417800 | tf_op jit(solution)/shard_map/ppermute | solution.py:273
  17.8 7.7 %collective-permute-start.2 = (f16[272,256]{1,0:T(8,128)(2,1)S(1)}, f16[272,256]{1,0:T(8,128)(2,1)S(1)}, u32[]{:S(2)}, u32[]{:S(2)}) collective-permute-start(f16[272,256]{1,0:T(8,128)(2,1)S(1)} %get-tuple-element.56), channel_id=1, source_target_pairs={{0,6},{1,7},{2,0},{3,1},{4,2},{5,3},{6,4},{7,5},{8,14},{9,15},{10,... | collective-permute-start | bytes 417800 | tf_op jit(solution)/shard_map/ppermute | solution.py:273
  25.5 16.1 %collective-permute-start.7 = (f16[544,256]{1,0:T(8,128)(2,1)S(1)}, f16[544,256]{1,0:T(8,128)(2,1)S(1)}, u32[]{:S(2)}, u32[]{:S(2)}) collective-permute-start(f16[544,256]{1,0:T(8,128)(2,1)S(1)} %add_convert_fusion.2), channel_id=1, source_target_pairs={{0,6},{1,7},{2,0},{3,1},{4,2},{5,3},{6,4},{7,5},{8,14},{9,15},{10,... | collective-permute-start | bytes 835592 | tf_op jit(solution)/shard_map/ppermute | solution.py:273
  28.7 12.9 %collective-permute-start.6 = (f16[544,256]{1,0:T(8,128)(2,1)S(1)}, f16[544,256]{1,0:T(8,128)(2,1)S(1)}, u32[]{:S(2)}, u32[]{:S(2)}) collective-permute-start(f16[544,256]{1,0:T(8,128)(2,1)S(1)} %add_convert_fusion.3), channel_id=1, source_target_pairs={{0,2},{1,3},{2,4},{3,5},{4,6},{5,7},{6,0},{7,1},{8,10},{9,11},{10,... | collective-permute-start | bytes 835592 | tf_op jit(solution)/shard_map/ppermute | solution.py:273
  29.1 12.5 %collective-permute-start.3 = (f16[512,256]{1,0:T(8,128)(2,1)S(1)}, f16[512,256]{1,0:T(8,128)(2,1)S(1)}, u32[]{:S(2)}, u32[]{:S(2)}) collective-permute-start(f16[512,256]{1,0:T(8,128)(2,1)S(1)} %get-tuple-element.55), channel_id=1, source_target_pairs={{0,32},{8,40},{16,48},{24,56},{32,64},{40,72},{48,80},{56,88},{64,... | collective-permute-start | bytes 786440 | tf_op jit(solution)/shard_map/ppermute | solution.py:273
  32.3 9.3 %collective-permute-start.4 = (f16[512,256]{1,0:T(8,128)(2,1)S(1)}, f16[512,256]{1,0:T(8,128)(2,1)S(1)}, u32[]{:S(2)}, u32[]{:S(2)}) collective-permute-start(f16[512,256]{1,0:T(8,128)(2,1)S(1)} %get-tuple-element.54), channel_id=1, source_target_pairs={{0,96},{8,104},{16,112},{24,120},{32,0},{40,8},{48,16},{56,24},{64... | collective-permute-start | bytes 786440 | tf_op jit(solution)/shard_map/ppermute | solution.py:273
  41.7 12.7 %collective-permute-start.10 = (f16[272,256]{1,0:T(8,128)(2,1)S(1)}, f16[272,256]{1,0:T(8,128)(2,1)S(1)}, u32[]{:S(2)}, u32[]{:S(2)}) collective-permute-start(f16[272,256]{1,0:T(8,128)(2,1)S(1)} %add_convert_fusion.5), channel_id=1, source_target_pairs={{0,1},{1,0},{2,3},{3,2},{4,5},{5,4},{6,7},{7,6},{8,9},{9,8},{10,11... | collective-permute-start | bytes 417800 | tf_op jit(solution)/shard_map/ppermute | solution.py:273
  51.1 13.0 %collective-permute-start.8 = (f16[1024,256]{1,0:T(8,128)(2,1)S(1)}, f16[1024,256]{1,0:T(8,128)(2,1)S(1)}, u32[]{:S(2)}, u32[]{:S(2)}) collective-permute-start(f16[1024,256]{1,0:T(8,128)(2,1)S(1)} %get-tuple-element.53), channel_id=1, source_target_pairs={{0,32},{8,40},{16,48},{24,56},{32,64},{40,72},{48,80},{56,88},{64,... | collective-permute-start | bytes 1572872 | tf_op jit(solution)/shard_map/ppermute | solution.py:273
  52.1 12.0 %collective-permute-start.9 = (f16[1024,256]{1,0:T(8,128)(2,1)S(1)}, f16[1024,256]{1,0:T(8,128)(2,1)S(1)}, u32[]{:S(2)}, u32[]{:S(2)}) collective-permute-start(f16[1024,256]{1,0:T(8,128)(2,1)S(1)} %get-tuple-element.52), channel_id=1, source_target_pairs={{0,96},{8,104},{16,112},{24,120},{32,0},{40,8},{48,16},{56,24},{64... | collective-permute-start | bytes 1572872 | tf_op jit(solution)/shard_map/ppermute | solution.py:273
  54.5 2.9 %collective-permute-start.12 = (f32[1,256]{1,0:T(1,128)S(1)}, f32[1,256]{1,0:T(1,128)S(1)}, u32[]{:S(2)}, u32[]{:S(2)}) collective-permute-start(f32[1,256]{1,0:T(1,128)S(1)} %slice_multiply_fusion.1), channel_id=1, source_target_pairs={{0,8},{8,0},{16,24},{24,16},{32,40},{40,32},{48,56},{56,48},{64,72... | collective-permute-start | bytes 3080 | tf_op jit(solution)/shard_map/ppermute | solution.py:273
  56.7 7.5 %collective-permute-start.11 = (f16[256,256]{1,0:T(8,128)(2,1)S(1)}, f16[256,256]{1,0:T(8,128)(2,1)S(1)}, u32[]{:S(2)}, u32[]{:S(2)}) collective-permute-start(f16[256,256]{1,0:T(8,128)(2,1)S(1)} %divide_convert_fusion), channel_id=1, source_target_pairs={{0,1},{1,0},{2,3},{3,2},{4,5},{5,4},{6,7},{7,6},{8,9},{9,8},{10,11... | collective-permute-start | bytes 393224 | tf_op jit(solution)/shard_map/ppermute | solution.py:273
  57.5 6.4 %collective-permute-start.13 = (f32[1,256]{1,0:T(1,128)S(1)}, f32[1,256]{1,0:T(1,128)S(1)}, u32[]{:S(2)}, u32[]{:S(2)}) collective-permute-start(f32[1,256]{1,0:T(1,128)S(1)} %fusion.2), channel_id=1, source_target_pairs={{0,32},{8,40},{16,48},{24,56},{32,0},{40,8},{48,16},{56,24},{64,96... | collective-permute-start | bytes 3080 | tf_op jit(solution)/shard_map/ppermute | solution.py:273
  64.3 13.3 %collective-permute-start.15 = (f16[512,256]{1,0:T(8,128)(2,1)S(1)}, f16[512,256]{1,0:T(8,128)(2,1)S(1)}, u32[]{:S(2)}, u32[]{:S(2)}) collective-permute-start(f16[512,256]{1,0:T(8,128)(2,1)S(1)} %pad_add_fusion), channel_id=1, source_target_pairs={{0,2},{1,3},{2,4},{3,5},{4,6},{5,7},{6,0},{7,1},{8,10},{9,11},{10,... | collective-permute-start | bytes 786440 | tf_op jit(solution)/shard_map/ppermute | solution.py:273
  66.2 11.4 %collective-permute-start.16 = (f16[512,256]{1,0:T(8,128)(2,1)S(1)}, f16[512,256]{1,0:T(8,128)(2,1)S(1)}, u32[]{:S(2)}, u32[]{:S(2)}) collective-permute-start(f16[512,256]{1,0:T(8,128)(2,1)S(1)} %pad_add_fusion), channel_id=1, source_target_pairs={{0,6},{1,7},{2,0},{3,1},{4,2},{5,3},{6,4},{7,5},{8,14},{9,15},{10,... | collective-permute-start | bytes 786440 | tf_op jit(solution)/shard_map/ppermute | solution.py:273
  68.9 8.6 %collective-permute-start.14 = (f16[512,256]{1,0:T(8,128)(2,1)S(1)}, f16[512,256]{1,0:T(8,128)(2,1)S(1)}, u32[]{:S(2)}, u32[]{:S(2)}) collective-permute-start(f16[512,256]{1,0:T(8,128)(2,1)S(1)} %add_convert_fusion.4), channel_id=1, source_target_pairs={{0,16},{8,24},{16,0},{24,8},{32,48},{40,56},{48,32},{56,40},{64,80... | collective-permute-start | bytes 786440 | tf_op jit(solution)/shard_map/ppermute | solution.py:273
  69.1 4.9 %collective-permute-start.17 = (f32[1,256]{1,0:T(1,128)S(1)}, f32[1,256]{1,0:T(1,128)S(1)}, u32[]{:S(2)}, u32[]{:S(2)}) collective-permute-start(f32[1,256]{1,0:T(1,128)S(1)} %add.207), channel_id=1, source_target_pairs={{0,96},{8,104},{16,112},{24,120},{32,64},{40,72},{48,80},{56,88},{... | collective-permute-start | bytes 3080 | tf_op jit(solution)/shard_map/ppermute | solution.py:273
  74.0 3.6 %collective-permute-start.18 = (f32[1,256]{1,0:T(1,128)S(1)}, f32[1,256]{1,0:T(1,128)S(1)}, u32[]{:S(2)}, u32[]{:S(2)}) collective-permute-start(f32[1,256]{1,0:T(1,128)S(1)} %add.218), channel_id=1, source_target_pairs={{0,16},{8,24},{16,0},{24,8},{32,48},{40,56},{48,32},{56,40},{64,80... | collective-permute-start | bytes 3080 | tf_op jit(solution)/shard_map/ppermute | solution.py:273
  77.6 7.7 %collective-permute-start.19 = (f16[512,256]{1,0:T(8,128)(2,1)S(1)}, f16[512,256]{1,0:T(8,128)(2,1)S(1)}, u32[]{:S(2)}, u32[]{:S(2)}) collective-permute-start(f16[512,256]{1,0:T(8,128)(2,1)S(1)} %collective-permute-done.15), channel_id=1, source_target_pairs={{0,2},{1,3},{2,4},{3,5},{4,6},{5,7},{6,0},{7,1},{8,10},{9,11},{10,... | collective-permute-start | bytes 786440 | tf_op jit(solution)/shard_map/ppermute | solution.py:273
  85.3 1.3 %copy-start.3 = (f32[2048,256]{1,0:T(8,128)}, f32[2048,256]{1,0:T(8,128)S(1)}, u32[]{:S(2)}) copy-start(f32[2048,256]{1,0:T(8,128)S(1)} %convert_dynamic-update-slice_fusion) | copy-start | bytes 6291460

commit v5 on v4

--- a/solution.py
+++ b/solution.py
@@ -212,6 +212,10 @@
         start_row += out.shape[0]
     for copy in leaving:
         copy.wait()
+
+
+def in_hbm(value):
+    return pltpu.with_memory_space_constraint(value, pltpu.HBM)
 
 
 def run_tiles(
@@ -258,13 +262,13 @@
         compiler_params=pltpu.CompilerParams(vmem_limit_bytes=48 << 20),
         name="tiles",
     )(
-        pair_list,
+        in_hbm(pair_list),
         own_load,
         docs_index,
         vocab_index,
-        doc_topics,
+        in_hbm(doc_topics),
         word_topics,
-        weight_table,
+        in_hbm(weight_table),
         counts_all,
     )
 
@@ -361,7 +365,7 @@
     doc_far = to_x_hi(doc_block)
     column = doc_sums[own_rows : own_rows + 1] / TOTAL_SCALE
     column = column + to_core(column)
-    column = column + y_pair(column)
+    column = column + to_x_lo(column)
     word_below, word_above, doc_block, doc_far, column = meet(
         word_below, word_above, doc_block, doc_far, column
     )
@@ -379,8 +383,7 @@
         jnp.where(x_hi == 0, doc_far, doc_block), own_rows, 0
     )
     doc_below, doc_above = z_up(doc_here), z_down(doc_here)
-    column = column + y_cross(column)
-    column = column + to_x_lo(column)
+    column = column + y_pair(column)
     word_far, doc_below, doc_above, column = meet(word_far, doc_below, doc_above, column)
 
     doc_across = z_up(doc_below)
@@ -388,6 +391,7 @@
     for step, value in ((0, doc_here), (1, doc_above), (3, doc_below), (2, doc_across)):
         at = (z + step) % N_Z * (N_X_HI * own_rows)
         doc_next = lax.dynamic_update_slice_in_dim(doc_next, to_float(value), at, 0)
+    column = column + y_cross(column)
     row_count = word_topics.shape[0] // n_docs
     word_sums = (word_half(x_lo) + to_float(word_far)) / WORD_SCALE
     vocab_total = word_topics.shape[0] * n_vocab

time: 86.9 us -> 84.1 us (0.968); the launches traced: 86.6 us -> 82.8 us
  local copies, waits for them, and re-layouts: 4.24 us -> 1.61 us
  Pallas kernels: 10.5 us -> 13.1 us
  starting transfers between devices: 37.7 us -> 35.6 us
  waiting for transfers between devices: 23.5 us -> 21.9 us
    pallas_call x1, Pallas kernels: 10.5 us -> 13.1 us  [run_tiles(): pl.pallas_call(tiles_kernel, out_shape=((doc_part,) * N_Z, (first_part, l...]
    unnamed x8 -> x2, local copies, waits for them, and re-layouts: 3.95 us -> 1.31 us
    ppermute x20, starting transfers between devices: 37.7 us -> 35.6 us  [moves(): lax.ppermute(value, axis, [(n, move(n) % size) for n in range(size)])]
    ppermute x20, waiting for transfers between devices: 23.5 us -> 21.9 us  [moves(): lax.ppermute(value, axis, [(n, move(n) % size) for n in range(size)])]
  transfers between devices with their start and end apart: 20 -> 20, of which waited for: 7 -> 9; matrix products, arithmetic and copies ran while one was open for 11% -> 11% of each run, Pallas kernels for 0% -> 0%
where the time goes in v5:
time: 84.1 us; the launch traced here: 82.8 us
  starting transfers between devices  35.6 us (42%)
  waiting for transfers between devices  21.9 us (26%)
  Pallas kernels  13.1 us (16%)
  other arithmetic  9.18 us (11%)
  local copies, waits for them, and re-layouts  1.61 us (2%)
  between operations  1.46 us (2%)
    ppermute x20, starting transfers between devices, moves(): lax.ppermute(value, axis, [(n, move(n) % size) for n in range(size)])  35.6 us
    ppermute x20, waiting for transfers between devices, moves(): lax.ppermute(value, axis, [(n, move(n) % size) for n in range(size)])  21.9 us
    pallas_call x1, Pallas kernels, run_tiles(): pl.pallas_call(tiles_kernel, out_shape=((doc_part,) * N_Z, (first_part, l...  13.1 us
    convert_element_type x6, other arithmetic, to_half(): return value.astype(jnp.float16)  5.15 us
    div x1, other arithmetic, on_device(): word_next = vocab_total * word_scaled / (column + vocab_total * prior_word)  2.3 us
  transfers between devices with their start and end apart: 20, of which 9 were waited for; matrix products, arithmetic and copies ran while one was open for 11% of the time, Pallas kernels for 0%

profile of v5, /device:TPU:0, one launch (start us, length us, event | category | flops | bytes accessed | tf_op | source)
XLA Modules:
  0.0 82.8 jit_solution(5032379116500125537)
XLA Ops:
  1.3 13.1 %tiles.1 = (f32[544,256]{1,0:T(8,128)S(1)}, f32[544,256]{1,0:T(8,128)S(1)}, f32[544,256]{1,0:T(8,128)S(1)}, f32[544,256]{1,0:T(8,128)S(1)}, f32[1024,256]{1,0:T(...) custom-call(s32[1,1,96]{2,1,0:T(1,128)} %pairs_hbm.1, s32[1,1]{1,0:T(1,128)S(6)} %copy.12.load_ref, ...), custom_call_target="tpu_custom_call" | custom-call | tf_op jit(solution)/shard_map/tiles/pallas_call | solution.py:237
  14.4 0.1 collective-permute-start.5
  14.5 0.5 collective-permute-start
  15.0 0.1 multiply_convert_fusion.1
  15.0 0.1 fusion.4
  15.1 0.9 %collective-permute-start.1 = (f16[272,256]{1,0:T(8,128)(2,1)S(1)}, f16[272,256]{1,0:T(8,128)(2,1)S(1)}, u32[]{:S(2)}, u32[]{:S(2)}) collective-permute-start(f16[272,256]{1,0:T(8,128)(2,1)S(1)} %get-tuple-element.57), channel_id=1, source_target_pairs={{0,2},{1,3},{2,4},{3,5},{4,6},{5,7},{6,0},{7,1},{8,10},{9,11},{10,... | collective-permute-start | bytes 417800 | tf_op jit(solution)/shard_map/ppermute | solution.py:277
  16.0 2.4 %collective-permute-start.2 = (f16[272,256]{1,0:T(8,128)(2,1)S(1)}, f16[272,256]{1,0:T(8,128)(2,1)S(1)}, u32[]{:S(2)}, u32[]{:S(2)}) collective-permute-start(f16[272,256]{1,0:T(8,128)(2,1)S(1)} %get-tuple-element.56), channel_id=1, source_target_pairs={{0,6},{1,7},{2,0},{3,1},{4,2},{5,3},{6,4},{7,5},{8,14},{9,15},{10,... | collective-permute-start | bytes 417800 | tf_op jit(solution)/shard_map/ppermute | solution.py:277
  18.4 3.6 %collective-permute-done.1 = f16[272,256]{1,0:T(8,128)(2,1)S(1)} collective-permute-done((f16[272,256]{1,0:T(8,128)(2,1)S(1)}, f16[272,256]{1,0:T(8,128)(2,1)S(1)}, u32[]{:S(2)}, u32[]{:S(2)}) %collective-permute-start.1) | collective-permute-done | bytes 139296 | tf_op jit(solution)/shard_map/ppermute | solution.py:277
  22.1 0.7 collective-permute-done.2
  22.8 0.0 collective-permute-done
  22.8 0.1 add_convert_fusion.2
  22.9 2.3 %collective-permute-start.7 = (f16[544,256]{1,0:T(8,128)(2,1)S(1)}, f16[544,256]{1,0:T(8,128)(2,1)S(1)}, u32[]{:S(2)}, u32[]{:S(2)}) collective-permute-start(f16[544,256]{1,0:T(8,128)(2,1)S(1)} %add_convert_fusion.2), channel_id=1, source_target_pairs={{0,6},{1,7},{2,0},{3,1},{4,2},{5,3},{6,4},{7,5},{8,14},{9,15},{10,... | collective-permute-start | bytes 835592 | tf_op jit(solution)/shard_map/ppermute | solution.py:277
  25.2 0.1 add_convert_fusion.3
  25.3 0.1 collective-permute-start.6
  25.3 0.2 multiply_convert_fusion
  25.5 0.1 fusion.3
  25.6 8.0 %collective-permute-start.3 = (f16[512,256]{1,0:T(8,128)(2,1)S(1)}, f16[512,256]{1,0:T(8,128)(2,1)S(1)}, u32[]{:S(2)}, u32[]{:S(2)}) collective-permute-start(f16[512,256]{1,0:T(8,128)(2,1)S(1)} %get-tuple-element.55), channel_id=1, source_target_pairs={{0,32},{8,40},{16,48},{24,56},{32,64},{40,72},{48,80},{56,88},{64,... | collective-permute-start | bytes 786440 | tf_op jit(solution)/shard_map/ppermute | solution.py:277
  33.6 1.0 %collective-permute-start.4 = (f16[512,256]{1,0:T(8,128)(2,1)S(1)}, f16[512,256]{1,0:T(8,128)(2,1)S(1)}, u32[]{:S(2)}, u32[]{:S(2)}) collective-permute-start(f16[512,256]{1,0:T(8,128)(2,1)S(1)} %get-tuple-element.54), channel_id=1, source_target_pairs={{0,96},{8,104},{16,112},{24,120},{32,0},{40,8},{48,16},{56,24},{64... | collective-permute-start | bytes 786440 | tf_op jit(solution)/shard_map/ppermute | solution.py:277
  34.7 5.2 %collective-permute-done.3 = f16[512,256]{1,0:T(8,128)(2,1)S(1)} collective-permute-done((f16[512,256]{1,0:T(8,128)(2,1)S(1)}, f16[512,256]{1,0:T(8,128)(2,1)S(1)}, u32[]{:S(2)}, u32[]{:S(2)}) %collective-permute-start.3) | collective-permute-done | bytes 262176 | tf_op jit(solution)/shard_map/ppermute | solution.py:277
  39.9 0.7 collective-permute-done.4
  40.6 0.0 collective-permute-done.7
  40.6 0.0 collective-permute-done.6
  40.6 0.0 collective-permute-done.5
  40.6 0.1 add_convert_fusion.5
  40.7 2.7 %collective-permute-start.10 = (f16[272,256]{1,0:T(8,128)(2,1)S(1)}, f16[272,256]{1,0:T(8,128)(2,1)S(1)}, u32[]{:S(2)}, u32[]{:S(2)}) collective-permute-start(f16[272,256]{1,0:T(8,128)(2,1)S(1)} %add_convert_fusion.5), channel_id=1, source_target_pairs={{0,1},{1,0},{2,3},{3,2},{4,5},{5,4},{6,7},{7,6},{8,9},{9,8},{10,11... | collective-permute-start | bytes 417800 | tf_op jit(solution)/shard_map/ppermute | solution.py:277
  43.5 2.5 %add_convert_fusion = (f16[1024,256]{1,0:T(8,128)(2,1)S(1)}, f16[1024,256]{1,0:T(8,128)(2,1)S(1)}) fusion(f32[3072,256]{1,0:T(8,128)} %collective-permute-done.5, f32[3072,256]{1,0:T(8,128)} %get-tuple-element.27, f16[512,256]{1,0:T(8,128)(2,1)S(1)} %collective-permute-done.4, f16[512,256]{1,0:T(8,128)(2,1)S(1)} %collective-permute-done.3), kind=kLoop, calls=%fused_computation | loop fusion | flops 2621440 | bytes 5767168 | tf_op jit(solution)/shard_map/convert_element_type | solution.py:281
  46.0 1.8 %collective-permute-start.8 = (f16[1024,256]{1,0:T(8,128)(2,1)S(1)}, f16[1024,256]{1,0:T(8,128)(2,1)S(1)}, u32[]{:S(2)}, u32[]{:S(2)}) collective-permute-start(f16[1024,256]{1,0:T(8,128)(2,1)S(1)} %get-tuple-element.53), channel_id=1, source_target_pairs={{0,32},{8,40},{16,48},{24,56},{32,64},{40,72},{48,80},{56,88},{64,... | collective-permute-start | bytes 1572872 | tf_op jit(solution)/shard_map/ppermute | solution.py:277
  47.8 1.5 %collective-permute-start.9 = (f16[1024,256]{1,0:T(8,128)(2,1)S(1)}, f16[1024,256]{1,0:T(8,128)(2,1)S(1)}, u32[]{:S(2)}, u32[]{:S(2)}) collective-permute-start(f16[1024,256]{1,0:T(8,128)(2,1)S(1)} %get-tuple-element.52), channel_id=1, source_target_pairs={{0,96},{8,104},{16,112},{24,120},{32,0},{40,8},{48,16},{56,24},{64... | collective-permute-start | bytes 1572872 | tf_op jit(solution)/shard_map/ppermute | solution.py:277
  49.3 0.0 collective-permute-done.10
  49.3 0.1 add_multiply_fusion
  49.4 0.1 collective-permute-start.12
  49.5 1.0 %fusion.1 = f32[256]{0:T(256)S(1)} fusion(f32[272,256]{1,0:T(8,128)S(1)} %add_multiply_fusion, bf16[2048,256]{1,0:T(8,128)(2,1)} %doc_hbm.1, s32[]{:T(128)S(6)} %select_n.92), kind=kLoop, calls=%fused_computation.18 | loop fusion | flops 261888 | bytes 394244 | tf_op jit(solution)/shard_map/reduce_sum | solution.py:363
  50.5 1.0 %divide_convert_fusion = f16[256,256]{1,0:T(8,128)(2,1)S(1)} fusion(f32[272,256]{1,0:T(8,128)S(1)} %add_multiply_fusion, f32[256]{0:T(256)S(1)} %fusion.1, bf16[2048,256]{1,0:T(8,128)(2,1)} %doc_hbm.1, s32[]{:T(128)S(6)} %select_n.92), kind=kLoop, calls=%fused_computation.17 | loop fusion | flops 393216 | bytes 525316 | tf_op jit(solution)/shard_map/convert_element_type | solution.py:281
  51.6 1.0 %collective-permute-start.11 = (f16[256,256]{1,0:T(8,128)(2,1)S(1)}, f16[256,256]{1,0:T(8,128)(2,1)S(1)}, u32[]{:S(2)}, u32[]{:S(2)}) collective-permute-start(f16[256,256]{1,0:T(8,128)(2,1)S(1)} %divide_convert_fusion), channel_id=1, source_target_pairs={{0,1},{1,0},{2,3},{3,2},{4,5},{5,4},{6,7},{7,6},{8,9},{9,8},{10,11... | collective-permute-start | bytes 393224 | tf_op jit(solution)/shard_map/ppermute | solution.py:277
  52.5 0.0 collective-permute-done.12
  52.5 2.8 %collective-permute-start.13 = (f32[1,256]{1,0:T(1,128)S(1)}, f32[1,256]{1,0:T(1,128)S(1)}, u32[]{:S(2)}, u32[]{:S(2)}) collective-permute-start(f32[1,256]{1,0:T(1,128)S(1)} %fusion.2), channel_id=1, source_target_pairs={{0,16},{8,24},{16,0},{24,8},{32,48},{40,56},{48,32},{56,40},{64,80... | collective-permute-start | bytes 3080 | tf_op jit(solution)/shard_map/ppermute | solution.py:277
  55.4 3.9 %collective-permute-done.13 = f32[1,256]{1,0:T(1,128)S(1)} collective-permute-done((f32[1,256]{1,0:T(1,128)S(1)}, f32[1,256]{1,0:T(1,128)S(1)}, u32[]{:S(2)}, u32[]{:S(2)}) %collective-permute-start.13) | collective-permute-done | bytes 1056 | tf_op jit(solution)/shard_map/ppermute | solution.py:277
  59.2 0.0 collective-permute-done.11
  59.2 0.0 collective-permute-done.8
  59.2 0.0 collective-permute-done.9
  59.3 0.1 broadcast_select_fusion.1
  59.3 0.1 pad_add_fusion
  59.4 1.8 %collective-permute-start.15 = (f16[512,256]{1,0:T(8,128)(2,1)S(1)}, f16[512,256]{1,0:T(8,128)(2,1)S(1)}, u32[]{:S(2)}, u32[]{:S(2)}) collective-permute-start(f16[512,256]{1,0:T(8,128)(2,1)S(1)} %pad_add_fusion), channel_id=1, source_target_pairs={{0,2},{1,3},{2,4},{3,5},{4,6},{5,7},{6,0},{7,1},{8,10},{9,11},{10,... | collective-permute-start | bytes 786440 | tf_op jit(solution)/shard_map/ppermute | solution.py:277
  61.2 1.5 %collective-permute-start.16 = (f16[512,256]{1,0:T(8,128)(2,1)S(1)}, f16[512,256]{1,0:T(8,128)(2,1)S(1)}, u32[]{:S(2)}, u32[]{:S(2)}) collective-permute-start(f16[512,256]{1,0:T(8,128)(2,1)S(1)} %pad_add_fusion), channel_id=1, source_target_pairs={{0,6},{1,7},{2,0},{3,1},{4,2},{5,3},{6,4},{7,5},{8,14},{9,15},{10,... | collective-permute-start | bytes 786440 | tf_op jit(solution)/shard_map/ppermute | solution.py:277
  62.7 1.3 %add_convert_fusion.4 = f16[512,256]{1,0:T(8,128)(2,1)S(1)} fusion(f32[3072,256]{1,0:T(8,128)} %collective-permute-done.5, s32[]{:T(128)S(6)} %select_n.102, f32[3072,256]{1,0:T(8,128)} %get-tuple-element.27, f16[1024,256]{1,0:T(8,128)(2,1)S(1)} %collective-permute-done.9, s32[]{:T(128)S(6)} %select_n.103, f16[1024,256]{1,0:T(8,128)(2,1)S(1)} %collective-permute-done.8), kind=kLoop, calls=%fused_computation.10 | loop fusion | flops 917504 | bytes 1835016 | tf_op jit(solution)/shard_map/convert_element_type | solution.py:281
  64.0 2.9 %collective-permute-start.14 = (f16[512,256]{1,0:T(8,128)(2,1)S(1)}, f16[512,256]{1,0:T(8,128)(2,1)S(1)}, u32[]{:S(2)}, u32[]{:S(2)}) collective-permute-start(f16[512,256]{1,0:T(8,128)(2,1)S(1)} %add_convert_fusion.4), channel_id=1, source_target_pairs={{0,16},{8,24},{16,0},{24,8},{32,48},{40,56},{48,32},{56,40},{64,80... | collective-permute-start | bytes 786440 | tf_op jit(solution)/shard_map/ppermute | solution.py:277
  66.9 1.2 %collective-permute-start.17 = (f32[1,256]{1,0:T(1,128)S(1)}, f32[1,256]{1,0:T(1,128)S(1)}, u32[]{:S(2)}, u32[]{:S(2)}) collective-permute-start(f32[1,256]{1,0:T(1,128)S(1)} %add.207), channel_id=1, source_target_pairs={{0,32},{8,40},{16,48},{24,56},{32,0},{40,8},{48,16},{56,24},{64,96... | collective-permute-start | bytes 3080 | tf_op jit(solution)/shard_map/ppermute | solution.py:277
  68.1 0.1 broadcast_in_dim.4
  68.3 0.1 convert_dynamic-update-slice_fusion.3
  68.3 2.1 %collective-permute-done.17 = f32[1,256]{1,0:T(1,128)S(1)} collective-permute-done((f32[1,256]{1,0:T(1,128)S(1)}, f32[1,256]{1,0:T(1,128)S(1)}, u32[]{:S(2)}, u32[]{:S(2)}) %collective-permute-start.17) | collective-permute-done | bytes 1056 | tf_op jit(solution)/shard_map/ppermute | solution.py:277
  70.5 0.0 collective-permute-done.15
  70.5 0.0 collective-permute-done.16
  70.5 2.0 %collective-permute-done.14 = f16[512,256]{1,0:T(8,128)(2,1)S(1)} collective-permute-done((f16[512,256]{1,0:T(8,128)(2,1)S(1)}, f16[512,256]{1,0:T(8,128)(2,1)S(1)}, u32[]{:S(2)}, u32[]{:S(2)}) %collective-permute-start.14) | collective-permute-done | bytes 262176 | tf_op jit(solution)/shard_map/ppermute | solution.py:277
  72.5 1.3 %collective-permute-start.19 = (f32[1,256]{1,0:T(1,128)S(1)}, f32[1,256]{1,0:T(1,128)S(1)}, u32[]{:S(2)}, u32[]{:S(2)}) collective-permute-start(f32[1,256]{1,0:T(1,128)S(1)} %add.218), channel_id=1, source_target_pairs={{0,96},{8,104},{16,112},{24,120},{32,64},{40,72},{48,80},{56,88},{... | collective-permute-start | bytes 3080 | tf_op jit(solution)/shard_map/ppermute | solution.py:277
  73.9 1.6 %collective-permute-start.18 = (f16[512,256]{1,0:T(8,128)(2,1)S(1)}, f16[512,256]{1,0:T(8,128)(2,1)S(1)}, u32[]{:S(2)}, u32[]{:S(2)}) collective-permute-start(f16[512,256]{1,0:T(8,128)(2,1)S(1)} %collective-permute-done.15), channel_id=1, source_target_pairs={{0,2},{1,3},{2,4},{3,5},{4,6},{5,7},{6,0},{7,1},{8,10},{9,11},{10,... | collective-permute-start | bytes 786440 | tf_op jit(solution)/shard_map/ppermute | solution.py:277
  75.4 0.1 convert_dynamic-update-slice_fusion.2
  75.5 0.1 convert_dynamic-update-slice_fusion.1
  75.6 1.7 %collective-permute-done.19 = f32[1,256]{1,0:T(1,128)S(1)} collective-permute-done((f32[1,256]{1,0:T(1,128)S(1)}, f32[1,256]{1,0:T(1,128)S(1)}, u32[]{:S(2)}, u32[]{:S(2)}) %collective-permute-start.19) | collective-permute-done | bytes 1056 | tf_op jit(solution)/shard_map/ppermute | solution.py:277
  77.3 2.3 %multiply_divide_fusion = f32[512,256]{1,0:T(8,128)} fusion(f16[512,256]{1,0:T(8,128)(2,1)S(1)} %collective-permute-done.14, f32[3072,256]{1,0:T(8,128)} %collective-permute-done.5, s32[]{:T(128)S(6)} %select_n.111, f32[3072,256]{1,0:T(8,128)} %get-tuple-element.27, f32[256]{0:T(256)S(1)} %bitcast.7, f16[1024,256]{1,0:T(8,128)(2,1)S(1)} %collective-permute-done.9, ...), kind=kLoop, calls=%fused_computation.6 | loop fusion | flops 1835008 | bytes 2622476 | tf_op jit(solution)/shard_map/div | solution.py:400
  79.6 1.8 %collective-permute-done.18 = f16[512,256]{1,0:T(8,128)(2,1)S(1)} collective-permute-done((f16[512,256]{1,0:T(8,128)(2,1)S(1)}, f16[512,256]{1,0:T(8,128)(2,1)S(1)}, u32[]{:S(2)}, u32[]{:S(2)}) %collective-permute-start.18) | collective-permute-done | bytes 262176 | tf_op jit(solution)/shard_map/ppermute | solution.py:277
  81.4 0.1 convert_dynamic-update-slice_fusion
  81.5 0.0 copy-start
  81.5 1.3 %copy-done = f32[2048,256]{1,0:T(8,128)} copy-done((f32[2048,256]{1,0:T(8,128)}, f32[2048,256]{1,0:T(8,128)S(1)}, u32[]{:S(2)}) %copy-start) | copy-done | bytes 2097176
  (5 shorter events, 0.0 us)
Async XLA Ops:
  14.4 26.2 %collective-permute-start.5 = (f32[3072,256]{1,0:T(8,128)}, f32[3072,256]{1,0:T(8,128)}, u32[]{:S(2)}, u32[]{:S(2)}) collective-permute-start(f32[3072,256]{1,0:T(8,128)} %get-tuple-element.32), channel_id=1, source_target_pairs={{0,8},{8,0},{16,24},{24,16},{32,40},{40,32},{48,56},{56,48},{64,72... | collective-permute-start | bytes 9437192 | tf_op jit(solution)/shard_map/ppermute | solution.py:277
  14.5 8.3 %collective-permute-start = (f32[1024,256]{1,0:T(8,128)S(1)}, f32[1024,256]{1,0:T(8,128)S(1)}, u32[]{:S(2)}, u32[]{:S(2)}) collective-permute-start(f32[1024,256]{1,0:T(8,128)S(1)} %get-tuple-element.29), channel_id=1, source_target_pairs={{0,8},{8,0},{16,24},{24,16},{32,40},{40,32},{48,56},{56,48},{64,72... | collective-permute-start | bytes 3145736 | tf_op jit(solution)/shard_map/ppermute | solution.py:277
  15.1 7.0 %collective-permute-start.1 = (f16[272,256]{1,0:T(8,128)(2,1)S(1)}, f16[272,256]{1,0:T(8,128)(2,1)S(1)}, u32[]{:S(2)}, u32[]{:S(2)}) collective-permute-start(f16[272,256]{1,0:T(8,128)(2,1)S(1)} %get-tuple-element.57), channel_id=1, source_target_pairs={{0,2},{1,3},{2,4},{3,5},{4,6},{5,7},{6,0},{7,1},{8,10},{9,11},{10,... | collective-permute-start | bytes 417800 | tf_op jit(solution)/shard_map/ppermute | solution.py:277
  16.0 6.8 %collective-permute-start.2 = (f16[272,256]{1,0:T(8,128)(2,1)S(1)}, f16[272,256]{1,0:T(8,128)(2,1)S(1)}, u32[]{:S(2)}, u32[]{:S(2)}) collective-permute-start(f16[272,256]{1,0:T(8,128)(2,1)S(1)} %get-tuple-element.56), channel_id=1, source_target_pairs={{0,6},{1,7},{2,0},{3,1},{4,2},{5,3},{6,4},{7,5},{8,14},{9,15},{10,... | collective-permute-start | bytes 417800 | tf_op jit(solution)/shard_map/ppermute | solution.py:277
  22.9 17.7 %collective-permute-start.7 = (f16[544,256]{1,0:T(8,128)(2,1)S(1)}, f16[544,256]{1,0:T(8,128)(2,1)S(1)}, u32[]{:S(2)}, u32[]{:S(2)}) collective-permute-start(f16[544,256]{1,0:T(8,128)(2,1)S(1)} %add_convert_fusion.2), channel_id=1, source_target_pairs={{0,6},{1,7},{2,0},{3,1},{4,2},{5,3},{6,4},{7,5},{8,14},{9,15},{10,... | collective-permute-start | bytes 835592 | tf_op jit(solution)/shard_map/ppermute | solution.py:277
  25.3 15.4 %collective-permute-start.6 = (f16[544,256]{1,0:T(8,128)(2,1)S(1)}, f16[544,256]{1,0:T(8,128)(2,1)S(1)}, u32[]{:S(2)}, u32[]{:S(2)}) collective-permute-start(f16[544,256]{1,0:T(8,128)(2,1)S(1)} %add_convert_fusion.3), channel_id=1, source_target_pairs={{0,2},{1,3},{2,4},{3,5},{4,6},{5,7},{6,0},{7,1},{8,10},{9,11},{10,... | collective-permute-start | bytes 835592 | tf_op jit(solution)/shard_map/ppermute | solution.py:277
  25.6 14.3 %collective-permute-start.3 = (f16[512,256]{1,0:T(8,128)(2,1)S(1)}, f16[512,256]{1,0:T(8,128)(2,1)S(1)}, u32[]{:S(2)}, u32[]{:S(2)}) collective-permute-start(f16[512,256]{1,0:T(8,128)(2,1)S(1)} %get-tuple-element.55), channel_id=1, source_target_pairs={{0,32},{8,40},{16,48},{24,56},{32,64},{40,72},{48,80},{56,88},{64,... | collective-permute-start | bytes 786440 | tf_op jit(solution)/shard_map/ppermute | solution.py:277
  33.6 7.0 %collective-permute-start.4 = (f16[512,256]{1,0:T(8,128)(2,1)S(1)}, f16[512,256]{1,0:T(8,128)(2,1)S(1)}, u32[]{:S(2)}, u32[]{:S(2)}) collective-permute-start(f16[512,256]{1,0:T(8,128)(2,1)S(1)} %get-tuple-element.54), channel_id=1, source_target_pairs={{0,96},{8,104},{16,112},{24,120},{32,0},{40,8},{48,16},{56,24},{64... | collective-permute-start | bytes 786440 | tf_op jit(solution)/shard_map/ppermute | solution.py:277
  40.7 8.6 %collective-permute-start.10 = (f16[272,256]{1,0:T(8,128)(2,1)S(1)}, f16[272,256]{1,0:T(8,128)(2,1)S(1)}, u32[]{:S(2)}, u32[]{:S(2)}) collective-permute-start(f16[272,256]{1,0:T(8,128)(2,1)S(1)} %add_convert_fusion.5), channel_id=1, source_target_pairs={{0,1},{1,0},{2,3},{3,2},{4,5},{5,4},{6,7},{7,6},{8,9},{9,8},{10,11... | collective-permute-start | bytes 417800 | tf_op jit(solution)/shard_map/ppermute | solution.py:277
  46.0 13.2 %collective-permute-start.8 = (f16[1024,256]{1,0:T(8,128)(2,1)S(1)}, f16[1024,256]{1,0:T(8,128)(2,1)S(1)}, u32[]{:S(2)}, u32[]{:S(2)}) collective-permute-start(f16[1024,256]{1,0:T(8,128)(2,1)S(1)} %get-tuple-element.53), channel_id=1, source_target_pairs={{0,32},{8,40},{16,48},{24,56},{32,64},{40,72},{48,80},{56,88},{64,... | collective-permute-start | bytes 1572872 | tf_op jit(solution)/shard_map/ppermute | solution.py:277
  47.8 11.4 %collective-permute-start.9 = (f16[1024,256]{1,0:T(8,128)(2,1)S(1)}, f16[1024,256]{1,0:T(8,128)(2,1)S(1)}, u32[]{:S(2)}, u32[]{:S(2)}) collective-permute-start(f16[1024,256]{1,0:T(8,128)(2,1)S(1)} %get-tuple-element.52), channel_id=1, source_target_pairs={{0,96},{8,104},{16,112},{24,120},{32,0},{40,8},{48,16},{56,24},{64... | collective-permute-start | bytes 1572872 | tf_op jit(solution)/shard_map/ppermute | solution.py:277
  49.4 3.1 %collective-permute-start.12 = (f32[1,256]{1,0:T(1,128)S(1)}, f32[1,256]{1,0:T(1,128)S(1)}, u32[]{:S(2)}, u32[]{:S(2)}) collective-permute-start(f32[1,256]{1,0:T(1,128)S(1)} %slice_multiply_fusion.1), channel_id=1, source_target_pairs={{0,8},{8,0},{16,24},{24,16},{32,40},{40,32},{48,56},{56,48},{64,72... | collective-permute-start | bytes 3080 | tf_op jit(solution)/shard_map/ppermute | solution.py:277
  51.6 7.7 %collective-permute-start.11 = (f16[256,256]{1,0:T(8,128)(2,1)S(1)}, f16[256,256]{1,0:T(8,128)(2,1)S(1)}, u32[]{:S(2)}, u32[]{:S(2)}) collective-permute-start(f16[256,256]{1,0:T(8,128)(2,1)S(1)} %divide_convert_fusion), channel_id=1, source_target_pairs={{0,1},{1,0},{2,3},{3,2},{4,5},{5,4},{6,7},{7,6},{8,9},{9,8},{10,11... | collective-permute-start | bytes 393224 | tf_op jit(solution)/shard_map/ppermute | solution.py:277
  52.5 6.7 %collective-permute-start.13 = (f32[1,256]{1,0:T(1,128)S(1)}, f32[1,256]{1,0:T(1,128)S(1)}, u32[]{:S(2)}, u32[]{:S(2)}) collective-permute-start(f32[1,256]{1,0:T(1,128)S(1)} %fusion.2), channel_id=1, source_target_pairs={{0,16},{8,24},{16,0},{24,8},{32,48},{40,56},{48,32},{56,40},{64,80... | collective-permute-start | bytes 3080 | tf_op jit(solution)/shard_map/ppermute | solution.py:277
  59.4 11.1 %collective-permute-start.15 = (f16[512,256]{1,0:T(8,128)(2,1)S(1)}, f16[512,256]{1,0:T(8,128)(2,1)S(1)}, u32[]{:S(2)}, u32[]{:S(2)}) collective-permute-start(f16[512,256]{1,0:T(8,128)(2,1)S(1)} %pad_add_fusion), channel_id=1, source_target_pairs={{0,2},{1,3},{2,4},{3,5},{4,6},{5,7},{6,0},{7,1},{8,10},{9,11},{10,... | collective-permute-start | bytes 786440 | tf_op jit(solution)/shard_map/ppermute | solution.py:277
  61.2 9.3 %collective-permute-start.16 = (f16[512,256]{1,0:T(8,128)(2,1)S(1)}, f16[512,256]{1,0:T(8,128)(2,1)S(1)}, u32[]{:S(2)}, u32[]{:S(2)}) collective-permute-start(f16[512,256]{1,0:T(8,128)(2,1)S(1)} %pad_add_fusion), channel_id=1, source_target_pairs={{0,6},{1,7},{2,0},{3,1},{4,2},{5,3},{6,4},{7,5},{8,14},{9,15},{10,... | collective-permute-start | bytes 786440 | tf_op jit(solution)/shard_map/ppermute | solution.py:277
  64.0 8.5 %collective-permute-start.14 = (f16[512,256]{1,0:T(8,128)(2,1)S(1)}, f16[512,256]{1,0:T(8,128)(2,1)S(1)}, u32[]{:S(2)}, u32[]{:S(2)}) collective-permute-start(f16[512,256]{1,0:T(8,128)(2,1)S(1)} %add_convert_fusion.4), channel_id=1, source_target_pairs={{0,16},{8,24},{16,0},{24,8},{32,48},{40,56},{48,32},{56,40},{64,80... | collective-permute-start | bytes 786440 | tf_op jit(solution)/shard_map/ppermute | solution.py:277
  66.9 3.6 %collective-permute-start.17 = (f32[1,256]{1,0:T(1,128)S(1)}, f32[1,256]{1,0:T(1,128)S(1)}, u32[]{:S(2)}, u32[]{:S(2)}) collective-permute-start(f32[1,256]{1,0:T(1,128)S(1)} %add.207), channel_id=1, source_target_pairs={{0,32},{8,40},{16,48},{24,56},{32,0},{40,8},{48,16},{56,24},{64,96... | collective-permute-start | bytes 3080 | tf_op jit(solution)/shard_map/ppermute | solution.py:277
  72.5 4.8 %collective-permute-start.19 = (f32[1,256]{1,0:T(1,128)S(1)}, f32[1,256]{1,0:T(1,128)S(1)}, u32[]{:S(2)}, u32[]{:S(2)}) collective-permute-start(f32[1,256]{1,0:T(1,128)S(1)} %add.218), channel_id=1, source_target_pairs={{0,96},{8,104},{16,112},{24,120},{32,64},{40,72},{48,80},{56,88},{... | collective-permute-start | bytes 3080 | tf_op jit(solution)/shard_map/ppermute | solution.py:277
  73.9 7.6 %collective-permute-start.18 = (f16[512,256]{1,0:T(8,128)(2,1)S(1)}, f16[512,256]{1,0:T(8,128)(2,1)S(1)}, u32[]{:S(2)}, u32[]{:S(2)}) collective-permute-start(f16[512,256]{1,0:T(8,128)(2,1)S(1)} %collective-permute-done.15), channel_id=1, source_target_pairs={{0,2},{1,3},{2,4},{3,5},{4,6},{5,7},{6,0},{7,1},{8,10},{9,11},{10,... | collective-permute-start | bytes 786440 | tf_op jit(solution)/shard_map/ppermute | solution.py:277
  81.5 1.3 %copy-start = (f32[2048,256]{1,0:T(8,128)}, f32[2048,256]{1,0:T(8,128)S(1)}, u32[]{:S(2)}) copy-start(f32[2048,256]{1,0:T(8,128)S(1)} %convert_dynamic-update-slice_fusion) | copy-start | bytes 6291460

commit v6 on v5

--- a/solution.py
+++ b/solution.py
@@ -7,8 +7,9 @@
 
 prior_doc = 0.5
 prior_word = 0.01
-SLOTS = 16
-AT_ONCE = 4
+WIDE = 4
+SLOTS = 8
+AT_ONCE = 2
 N_Y, N_X_LO, N_CORE = 4, 2, 2
 N_Z, N_X_HI = 4, 2
 WORD_SCALE = 2.0**-7
@@ -29,6 +30,7 @@
     doc_parts_out,
     keep_out,
     send_out,
+    doc_next_out,
     pairs_ref,
     weights_ref,
     doc_sums,
@@ -36,10 +38,10 @@
     doc_rows,
     word_rows,
     counts_buf,
-    first_slot,
-    second_slot,
+    slots,
     item_doc,
-    pending,
+    item_of,
+    filled,
     topics_sem,
     counts_sem,
     sums_sem,
@@ -74,46 +76,40 @@
     word_copy.start()
     weights_copy.start()
 
+    def clear_item(item, carry):
+        item_doc[item] = 0
+        for n in range(WIDE):
+            slots[item * WIDE + n] = -1
+        return carry
+
+    lax.fori_loop(0, item_doc.shape[0], clear_item, 0)
     for b in range(doc_blocks):
-        pending[b] = -1
+        filled[b] = 0
 
     pairs_copy.wait()
 
     def sort_slot(s, made):
         b = pairs_ref[0, s] // blocks
-        waiting = pending[b]
-        first_slot[made] = waiting
-        second_slot[made] = s
-        item_doc[made] = b
-        pending[b] = jnp.where(waiting >= 0, -1, s)
-        return made + jnp.where(waiting >= 0, 1, 0)
+        taken = filled[b]
+        item = jnp.where(taken == 0, made, item_of[b])
+        item_of[b] = item
+        item_doc[item] = b
+        slots[item * WIDE + taken] = s
+        filled[b] = lax.rem(taken + 1, WIDE)
+        return made + jnp.where(taken == 0, 1, 0)
 
     made = lax.fori_loop(0, load, sort_slot, 0)
-    for b in range(doc_blocks):
-        waiting = pending[b]
-        first_slot[made] = waiting
-        second_slot[made] = -1
-        item_doc[made] = b
-        made = made + jnp.where(waiting >= 0, 1, 0)
-
-    def pad_item(n, carry):
-        first_slot[made + n] = -1
-        second_slot[made + n] = -1
-        item_doc[made + n] = 0
-        return carry
-
-    lax.fori_loop(0, AT_ONCE - 1, pad_item, 0)
     rounds = (made + AT_ONCE - 1) // AT_ONCE
 
     def copies(item):
         ring = lax.rem(item, SLOTS)
         return [
             pltpu.make_async_copy(
-                counts_hbm.at[jnp.maximum(slots[item], 0)],
+                counts_hbm.at[jnp.maximum(slots[item * WIDE + n], 0)],
                 counts_buf.at[ring, n],
                 counts_sem.at[ring, n],
             )
-            for n, slots in enumerate((first_slot, second_slot))
+            for n in range(WIDE)
         ]
 
     def start(n):
@@ -136,12 +132,12 @@
         doc_at = pl.multiple_of(item_doc[item] * tile_docs, tile_docs)
         docs = doc_rows[pl.ds(doc_at, tile_docs), :]
         words, weight, counts, word_blocks = [], [], [], []
-        for n, slots in enumerate((first_slot, second_slot)):
-            block = lax.rem(pairs_ref[0, jnp.maximum(slots[item], 0)], blocks)
+        for n in range(WIDE):
+            slot = slots[item * WIDE + n]
+            block = lax.rem(pairs_ref[0, jnp.maximum(slot, 0)], blocks)
             word_at = pl.multiple_of(block * tile_words, tile_words)
             words.append(word_rows[pl.ds(word_at, tile_words), :])
-            live = jnp.where(slots[item] >= 0, 1.0, 0.0)
-            weight.append(weights_ref[pl.ds(block, 1), :] * live)
+            weight.append(weights_ref[pl.ds(block, 1), :] * jnp.where(slot >= 0, 1.0, 0.0))
             counts.append(counts_buf[lax.rem(item, SLOTS), n])
             word_blocks.append(block)
         words = jnp.concatenate(words, axis=0)
@@ -225,7 +221,7 @@
     tile_docs, tile_words = counts_all.shape[1:]
     topics = doc_topics.shape[1]
     doc_blocks = doc_topics.shape[0] // tile_docs
-    items = slots + doc_blocks + AT_ONCE
+    items = -(-slots // WIDE) + doc_blocks + AT_ONCE
     doc_rows = doc_topics.shape[0] // N_Z + N_X_HI * TOTAL_ROWS
     doc_part = jax.ShapeDtypeStruct((doc_rows, topics), jnp.float32)
     word_rows = word_topics.shape[0] // (N_CORE * N_Y)
@@ -240,9 +236,10 @@
             (doc_part,) * N_Z,
             (first_part, later_part),
             (first_part, later_part),
+            jax.ShapeDtypeStruct(doc_topics.shape, jnp.float32),
         ),
         in_specs=[source] + [smem] * 3 + [source] * 4,
-        out_specs=((hbm,) * N_Z, (hbm,) * 2, (hbm,) * 2),
+        out_specs=((hbm,) * N_Z, (hbm,) * 2, (hbm,) * 2, source),
         scratch_shapes=[
             pltpu.SMEM(pair_list.shape[1:], jnp.int32),
             pltpu.VMEM(weight_table.shape, jnp.float32),
@@ -250,13 +247,13 @@
             pltpu.VMEM(word_topics.shape, jnp.float32),
             pltpu.VMEM(doc_topics.shape, doc_topics.dtype),
             pltpu.VMEM(word_topics.shape, word_topics.dtype),
-            pltpu.VMEM((SLOTS, 2, tile_docs, tile_words), counts_all.dtype),
-            pltpu.SMEM((items,), jnp.int32),
-            pltpu.SMEM((items,), jnp.int32),
+            pltpu.VMEM((SLOTS, WIDE, tile_docs, tile_words), counts_all.dtype),
+            pltpu.SMEM((items * WIDE,), jnp.int32),
             pltpu.SMEM((items,), jnp.int32),
             pltpu.SMEM((doc_blocks,), jnp.int32),
+            pltpu.SMEM((doc_blocks,), jnp.int32),
             pltpu.SemaphoreType.DMA((4,)),
-            pltpu.SemaphoreType.DMA((SLOTS, 2)),
+            pltpu.SemaphoreType.DMA((SLOTS, WIDE)),
             pltpu.SemaphoreType.DMA((N_Z + 4,)),
         ],
         compiler_params=pltpu.CompilerParams(vmem_limit_bytes=48 << 20),
@@ -302,13 +299,14 @@
     y_cross = moves("docs", n_docs, lambda n: n ^ ((N_Y - 1) * N_X_LO * N_CORE))
     to_x_hi = moves("vocab", n_vocab, lambda n: n ^ 1)
     z_up = moves("vocab", n_vocab, lambda n: n + N_X_HI)
+    z_across = moves("vocab", n_vocab, lambda n: n + 2 * N_X_HI)
     z_down = moves("vocab", n_vocab, lambda n: n - N_X_HI)
 
     counts_all = tile_counts[0, 0]
     tile_words = counts_all.shape[2]
     blocks = word_topics.shape[0] // tile_words
     weight_table = word_weights.reshape(blocks, tile_words)
-    doc_parts, keep, send = run_tiles(
+    doc_parts, keep, send, doc_next = run_tiles(
         tile_pairs,
         tile_load,
         docs_index.reshape(1),
@@ -326,18 +324,16 @@
 
     part = [piece * DOC_SCALE for piece in doc_parts]
     word_far = to_core(send[0])
-    doc_up = z_up(to_half(part[2][:doc_rows]))
-    doc_down = z_down(to_half(part[2][doc_rows:]))
-    word_far, doc_up, doc_down = meet(word_far, doc_up, doc_down)
+    doc_below, doc_above, doc_across = (
+        move(to_half(part[step])) for move, step in ((z_up, 1), (z_down, 3), (z_across, 2))
+    )
 
     far = (keep[0] + word_far) * WORD_SCALE
     word_up = y_up(to_half(far[:word_rows]))
     word_down = y_down(to_half(far[word_rows:]))
     near_far = to_core(send[1])
-    doc_below = z_up(to_half(part[1] + rows_around(to_float(doc_up), 0, doc_rows)))
-    doc_above = z_down(to_half(part[3] + rows_around(to_float(doc_down), doc_rows, 0)))
-    word_up, word_down, near_far, doc_below, doc_above = meet(
-        word_up, word_down, near_far, doc_below, doc_above
+    word_up, word_down, near_far, doc_below, doc_above, doc_across = meet(
+        word_up, word_down, near_far, doc_below, doc_above, doc_across
     )
 
     above = (keep[1][:near_rows] + near_far[:near_rows]) * WORD_SCALE
@@ -350,9 +346,9 @@
     def doc_half(which):
         rows = [
             lax.dynamic_slice_in_dim(value, which * doc_rows, doc_rows, 0)
-            for value in (doc_parts[0], doc_below, doc_above)
+            for value in (doc_parts[0], doc_below, doc_above, doc_across)
         ]
-        return rows[0] * DOC_SCALE + to_float(rows[1]) + to_float(rows[2])
+        return rows[0] * DOC_SCALE + to_float(rows[1]) + to_float(rows[2]) + to_float(rows[3])
 
     doc_mine, doc_other = doc_half(x_hi), doc_half(1 - x_hi)
     doc_sums = (doc_mine + to_float(to_x_hi(to_half(doc_other)))) / DOC_SCALE
@@ -382,16 +378,12 @@
     doc_here = rows_around(jnp.where(x_hi == 0, doc_block, doc_far), 0, own_rows) + rows_around(
         jnp.where(x_hi == 0, doc_far, doc_block), own_rows, 0
     )
-    doc_below, doc_above = z_up(doc_here), z_down(doc_here)
+    doc_below, doc_above, doc_across = z_up(doc_here), z_down(doc_here), z_across(doc_here)
     column = column + y_pair(column)
-    word_far, doc_below, doc_above, column = meet(word_far, doc_below, doc_above, column)
-
-    doc_across = z_up(doc_below)
-    doc_next = jnp.zeros(doc_topics.shape, jnp.float32)
+    column = column + y_cross(column)
     for step, value in ((0, doc_here), (1, doc_above), (3, doc_below), (2, doc_across)):
         at = (z + step) % N_Z * (N_X_HI * own_rows)
         doc_next = lax.dynamic_update_slice_in_dim(doc_next, to_float(value), at, 0)
-    column = column + y_cross(column)
     row_count = word_topics.shape[0] // n_docs
     word_sums = (word_half(x_lo) + to_float(word_far)) / WORD_SCALE
     vocab_total = word_topics.shape[0] * n_vocab

time: 84.1 us -> 79.8 us (0.949); the launches traced: 82.8 us -> 79.9 us
  waiting for transfers between devices: 21.9 us -> 25.3 us
  starting transfers between devices: 35.6 us -> 32.5 us
  Pallas kernels: 13.1 us -> 10.5 us
  local copies, waits for them, and re-layouts: 1.61 us -> 0.12 us
    ppermute x20 -> x19, waiting for transfers between devices: 21.9 us -> 25.3 us  [moves(): lax.ppermute(value, axis, [(n, move(n) % size) for n in range(size)])]
    ppermute x20 -> x19, starting transfers between devices: 35.6 us -> 32.5 us  [moves(): lax.ppermute(value, axis, [(n, move(n) % size) for n in range(size)])]
    pallas_call x1, Pallas kernels: 13.1 us -> 10.5 us  [run_tiles(): pl.pallas_call(tiles_kernel, out_shape=((doc_part,) * N_Z, (first_part, l...]
    unnamed x2 -> x6, local copies, waits for them, and re-layouts: 1.31 us -> 0.02 us
    convert_element_type x6 -> x7, other arithmetic: 5.15 us -> 5.2 us  [to_half(): return value.astype(jnp.float16)]
  transfers between devices with their start and end apart: 20 -> 19, of which waited for: 9 -> 9; matrix products, arithmetic and copies ran while one was open for 11% -> 8% of each run, Pallas kernels for 0% -> 0%
where the time goes in v6:
time: 79.8 us; the launch traced here: 79.9 us
  starting transfers between devices  32.5 us (41%)
  waiting for transfers between devices  25.3 us (32%)
  Pallas kernels  10.5 us (13%)
  other arithmetic  9.93 us (12%)
  between operations  1.5 us (2%)
    ppermute x19, starting transfers between devices, moves(): lax.ppermute(value, axis, [(n, move(n) % size) for n in range(size)])  32.5 us
    ppermute x19, waiting for transfers between devices, moves(): lax.ppermute(value, axis, [(n, move(n) % size) for n in range(size)])  25.3 us
    pallas_call x1, Pallas kernels, run_tiles(): pl.pallas_call(tiles_kernel, out_shape=((doc_part,) * N_Z, (first_part, l...  10.5 us
    convert_element_type x7, other arithmetic, to_half(): return value.astype(jnp.float16)  5.2 us
    div x1, other arithmetic, on_device(): word_next = vocab_total * word_scaled / (column + vocab_total * prior_word)  3.06 us
  transfers between devices with their start and end apart: 19, of which 9 were waited for; matrix products, arithmetic and copies ran while one was open for 8% of the time, Pallas kernels for 0%

profile of v6, /device:TPU:0, one launch (start us, length us, event | category | flops | bytes accessed | tf_op | source)
XLA Modules:
  0.0 79.9 jit_solution(14497863754816344839)
XLA Ops:
  1.3 10.5 %tiles.1 = (f32[544,256]{1,0:T(8,128)S(1)}, f32[544,256]{1,0:T(8,128)S(1)}, f32[544,256]{1,0:T(8,128)S(1)}, f32[544,256]{1,0:T(8,128)S(1)}, f32[1024,256]{1,0:T(...) custom-call(s32[1,1,96]{2,1,0:T(1,128)} %pairs_hbm.1, ...), custom_call_target="tpu_custom_call" | custom-call | tf_op jit(solution)/shard_map/tiles/pallas_call | solution.py:233
  11.8 0.1 collective-permute-start.3
  11.9 0.5 collective-permute-start
  12.4 0.1 multiply_convert_fusion.1
  12.5 6.3 %collective-permute-start.6 = (f16[544,256]{1,0:T(8,128)(2,1)S(1)}, f16[544,256]{1,0:T(8,128)(2,1)S(1)}, u32[]{:S(2)}, u32[]{:S(2)}) collective-permute-start(f16[544,256]{1,0:T(8,128)(2,1)S(1)} %multiply_convert_fusion.1), channel_id=1, source_target_pairs={{0,4},{1,5},{2,6},{3,7},{4,0},{5,1},{6,2},{7,3},{8,12},{9,13},{10,... | collective-permute-start | bytes 835592 | tf_op jit(solution)/shard_map/ppermute | solution.py:274
  18.8 0.1 multiply_convert_fusion.2
  18.8 0.3 collective-permute-start.5
  19.1 0.1 multiply_convert_fusion.3
  19.2 1.8 %collective-permute-start.4 = (f16[544,256]{1,0:T(8,128)(2,1)S(1)}, f16[544,256]{1,0:T(8,128)(2,1)S(1)}, u32[]{:S(2)}, u32[]{:S(2)}) collective-permute-start(f16[544,256]{1,0:T(8,128)(2,1)S(1)} %multiply_convert_fusion.3), channel_id=1, source_target_pairs={{0,2},{1,3},{2,4},{3,5},{4,6},{5,7},{6,0},{7,1},{8,10},{9,11},{10,... | collective-permute-start | bytes 835592 | tf_op jit(solution)/shard_map/ppermute | solution.py:274
  21.0 0.0 collective-permute-done
  21.0 0.2 multiply_convert_fusion
  21.2 0.1 fusion.3
  21.3 11.2 %collective-permute-start.2 = (f16[512,256]{1,0:T(8,128)(2,1)S(1)}, f16[512,256]{1,0:T(8,128)(2,1)S(1)}, u32[]{:S(2)}, u32[]{:S(2)}) collective-permute-start(f16[512,256]{1,0:T(8,128)(2,1)S(1)} %get-tuple-element.44), channel_id=1, source_target_pairs={{0,96},{8,104},{16,112},{24,120},{32,0},{40,8},{48,16},{56,24},{64... | collective-permute-start | bytes 786440 | tf_op jit(solution)/shard_map/ppermute | solution.py:274
  32.5 0.0 collective-permute-done.6
  32.5 0.0 collective-permute-start.1
  32.5 0.0 collective-permute-done.5
  32.5 0.0 collective-permute-done.4
  32.5 5.2 %collective-permute-done.2 = f16[512,256]{1,0:T(8,128)(2,1)S(1)} collective-permute-done((f16[512,256]{1,0:T(8,128)(2,1)S(1)}, f16[512,256]{1,0:T(8,128)(2,1)S(1)}, u32[]{:S(2)}, u32[]{:S(2)}) %collective-permute-start.2) | collective-permute-done | bytes 262176 | tf_op jit(solution)/shard_map/ppermute | solution.py:274
  37.8 3.4 %collective-permute-done.1 = f16[512,256]{1,0:T(8,128)(2,1)S(1)} collective-permute-done((f16[512,256]{1,0:T(8,128)(2,1)S(1)}, f16[512,256]{1,0:T(8,128)(2,1)S(1)}, u32[]{:S(2)}, u32[]{:S(2)}) %collective-permute-start.1) | collective-permute-done | bytes 262176 | tf_op jit(solution)/shard_map/ppermute | solution.py:274
  41.2 0.0 copy-start
  41.2 0.0 collective-permute-done.3
  41.2 0.1 add_convert_fusion.3
  41.3 2.6 %collective-permute-start.9 = (f16[272,256]{1,0:T(8,128)(2,1)S(1)}, f16[272,256]{1,0:T(8,128)(2,1)S(1)}, u32[]{:S(2)}, u32[]{:S(2)}) collective-permute-start(f16[272,256]{1,0:T(8,128)(2,1)S(1)} %add_convert_fusion.3), channel_id=1, source_target_pairs={{0,1},{1,0},{2,3},{3,2},{4,5},{5,4},{6,7},{7,6},{8,9},{9,8},{10,11... | collective-permute-start | bytes 417800 | tf_op jit(solution)/shard_map/ppermute | solution.py:274
  44.0 0.0 copy-done
  44.0 2.6 %add_convert_fusion = (f16[1024,256]{1,0:T(8,128)(2,1)S(1)}, f16[1024,256]{1,0:T(8,128)(2,1)S(1)}) fusion(f32[3072,256]{1,0:T(8,128)} %collective-permute-done.3, f32[3072,256]{1,0:T(8,128)} %get-tuple-element.23, f16[512,256]{1,0:T(8,128)(2,1)S(1)} %collective-permute-done.2, f16[512,256]{1,0:T(8,128)(2,1)} %copy-done), kind=kLoop, calls=%fused_computation | loop fusion | flops 2621440 | bytes 5767168 | tf_op jit(solution)/shard_map/convert_element_type | solution.py:278
  46.5 3.0 %collective-permute-start.8 = (f16[1024,256]{1,0:T(8,128)(2,1)S(1)}, f16[1024,256]{1,0:T(8,128)(2,1)S(1)}, u32[]{:S(2)}, u32[]{:S(2)}) collective-permute-start(f16[1024,256]{1,0:T(8,128)(2,1)S(1)} %get-tuple-element.42), channel_id=1, source_target_pairs={{0,96},{8,104},{16,112},{24,120},{32,0},{40,8},{48,16},{56,24},{64... | collective-permute-start | bytes 1572872 | tf_op jit(solution)/shard_map/ppermute | solution.py:274
  49.5 0.0 collective-permute-start.7
  49.5 0.0 collective-permute-done.9
  49.5 0.1 add_multiply_fusion
  49.6 0.1 collective-permute-start.11
  49.7 1.0 %fusion.1 = f32[256]{0:T(256)S(1)} fusion(f32[272,256]{1,0:T(8,128)S(1)} %add_multiply_fusion, bf16[2048,256]{1,0:T(8,128)(2,1)} %doc_hbm.1, s32[]{:T(128)S(6)} %select_n.94), kind=kLoop, calls=%fused_computation.18 | loop fusion | flops 261888 | bytes 394244 | tf_op jit(solution)/shard_map/reduce_sum | solution.py:359
  50.7 1.0 %divide_convert_fusion = f16[256,256]{1,0:T(8,128)(2,1)S(1)} fusion(f32[272,256]{1,0:T(8,128)S(1)} %add_multiply_fusion, f32[256]{0:T(256)S(1)} %fusion.1, bf16[2048,256]{1,0:T(8,128)(2,1)} %doc_hbm.1, s32[]{:T(128)S(6)} %select_n.94), kind=kLoop, calls=%fused_computation.17 | loop fusion | flops 393216 | bytes 525316 | tf_op jit(solution)/shard_map/convert_element_type | solution.py:278
  51.8 1.6 %collective-permute-start.10 = (f16[256,256]{1,0:T(8,128)(2,1)S(1)}, f16[256,256]{1,0:T(8,128)(2,1)S(1)}, u32[]{:S(2)}, u32[]{:S(2)}) collective-permute-start(f16[256,256]{1,0:T(8,128)(2,1)S(1)} %divide_convert_fusion), channel_id=1, source_target_pairs={{0,1},{1,0},{2,3},{3,2},{4,5},{5,4},{6,7},{7,6},{8,9},{9,8},{10,11... | collective-permute-start | bytes 393224 | tf_op jit(solution)/shard_map/ppermute | solution.py:274
  53.3 0.0 collective-permute-done.11
  53.3 0.0 collective-permute-start.12
  53.4 0.0 copy-start.1
  53.4 3.5 %collective-permute-done.12 = f32[1,256]{1,0:T(1,128)S(1)} collective-permute-done((f32[1,256]{1,0:T(1,128)S(1)}, f32[1,256]{1,0:T(1,128)S(1)}, u32[]{:S(2)}, u32[]{:S(2)}) %collective-permute-start.12) | collective-permute-done | bytes 1056 | tf_op jit(solution)/shard_map/ppermute | solution.py:274
  56.9 2.3 %collective-permute-done.10 = f16[256,256]{1,0:T(8,128)(2,1)S(1)} collective-permute-done((f16[256,256]{1,0:T(8,128)(2,1)S(1)}, f16[256,256]{1,0:T(8,128)(2,1)S(1)}, u32[]{:S(2)}, u32[]{:S(2)}) %collective-permute-start.10) | collective-permute-done | bytes 131104 | tf_op jit(solution)/shard_map/ppermute | solution.py:274
  59.3 0.3 collective-permute-done.8
  59.6 3.4 %collective-permute-done.7 = f16[1024,256]{1,0:T(8,128)(2,1)S(1)} collective-permute-done((f16[1024,256]{1,0:T(8,128)(2,1)S(1)}, f16[1024,256]{1,0:T(8,128)(2,1)S(1)}, u32[]{:S(2)}, u32[]{:S(2)}) %collective-permute-start.7) | collective-permute-done | bytes 524320 | tf_op jit(solution)/shard_map/ppermute | solution.py:274
  63.0 0.1 broadcast_select_fusion.1
  63.0 0.1 pad_add_fusion
  63.1 1.1 %collective-permute-start.14 = (f16[512,256]{1,0:T(8,128)(2,1)S(1)}, f16[512,256]{1,0:T(8,128)(2,1)S(1)}, u32[]{:S(2)}, u32[]{:S(2)}) collective-permute-start(f16[512,256]{1,0:T(8,128)(2,1)S(1)} %pad_add_fusion), channel_id=1, source_target_pairs={{0,2},{1,3},{2,4},{3,5},{4,6},{5,7},{6,0},{7,1},{8,10},{9,11},{10,... | collective-permute-start | bytes 786440 | tf_op jit(solution)/shard_map/ppermute | solution.py:274
  64.2 2.2 %collective-permute-start.13 = (f16[512,256]{1,0:T(8,128)(2,1)S(1)}, f16[512,256]{1,0:T(8,128)(2,1)S(1)}, u32[]{:S(2)}, u32[]{:S(2)}) collective-permute-start(f16[512,256]{1,0:T(8,128)(2,1)S(1)} %pad_add_fusion), channel_id=1, source_target_pairs={{0,6},{1,7},{2,0},{3,1},{4,2},{5,3},{6,4},{7,5},{8,14},{9,15},{10,... | collective-permute-start | bytes 786440 | tf_op jit(solution)/shard_map/ppermute | solution.py:274
  66.4 1.3 %collective-permute-start.15 = (f16[512,256]{1,0:T(8,128)(2,1)S(1)}, f16[512,256]{1,0:T(8,128)(2,1)S(1)}, u32[]{:S(2)}, u32[]{:S(2)}) collective-permute-start(f16[512,256]{1,0:T(8,128)(2,1)S(1)} %pad_add_fusion), channel_id=1, source_target_pairs={{0,4},{1,5},{2,6},{3,7},{4,0},{5,1},{6,2},{7,3},{8,12},{9,13},{10,... | collective-permute-start | bytes 786440 | tf_op jit(solution)/shard_map/ppermute | solution.py:274
  67.7 0.0 collective-permute-start.17
  67.7 1.3 %add_convert_fusion.2 = f16[512,256]{1,0:T(8,128)(2,1)S(1)} fusion(f32[3072,256]{1,0:T(8,128)} %collective-permute-done.3, s32[]{:T(128)S(6)} %select_n.113, f32[3072,256]{1,0:T(8,128)} %get-tuple-element.23, f16[1024,256]{1,0:T(8,128)(2,1)S(1)} %collective-permute-done.8, s32[]{:T(128)S(6)} %select_n.114, f16[1024,256]{1,0:T(8,128)(2,1)S(1)} %collective-permute-done.7), kind=kLoop, calls=%fused_computation.7 | loop fusion | flops 917504 | bytes 1835016 | tf_op jit(solution)/shard_map/convert_element_type | solution.py:278
  69.1 0.1 collective-permute-start.16
  69.2 2.1 %collective-permute-done.17 = f32[1,256]{1,0:T(1,128)S(1)} collective-permute-done((f32[1,256]{1,0:T(1,128)S(1)}, f32[1,256]{1,0:T(1,128)S(1)}, u32[]{:S(2)}, u32[]{:S(2)}) %collective-permute-start.17) | collective-permute-done | bytes 1056 | tf_op jit(solution)/shard_map/ppermute | solution.py:274
  71.3 0.3 collective-permute-start.18
  71.6 0.0 copy-done.1
  71.6 0.1 convert_dynamic-update-slice_fusion.3
  71.7 4.4 %collective-permute-done.18 = f32[1,256]{1,0:T(1,128)S(1)} collective-permute-done((f32[1,256]{1,0:T(1,128)S(1)}, f32[1,256]{1,0:T(1,128)S(1)}, u32[]{:S(2)}, u32[]{:S(2)}) %collective-permute-start.18) | collective-permute-done | bytes 1056 | tf_op jit(solution)/shard_map/ppermute | solution.py:274
  76.1 0.0 collective-permute-done.13
  76.1 0.1 convert_dynamic-update-slice_fusion.2
  76.2 0.0 collective-permute-done.14
  76.2 0.1 convert_dynamic-update-slice_fusion.1
  76.2 0.5 collective-permute-done.15
  76.8 0.1 convert_dynamic-update-slice_fusion
  76.8 0.0 copy-start.2
  76.8 0.0 collective-permute-done.16
  76.9 3.1 %multiply_divide_fusion = f32[512,256]{1,0:T(8,128)} fusion(f16[512,256]{1,0:T(8,128)(2,1)S(1)} %collective-permute-done.16, f32[3072,256]{1,0:T(8,128)} %collective-permute-done.3, s32[]{:T(128)S(6)} %select_n.111, f32[3072,256]{1,0:T(8,128)} %get-tuple-element.23, f32[256]{0:T(256)S(1)} %bitcast.7, f16[1024,256]{1,0:T(8,128)(2,1)S(1)} %collective-permute-done.8, ...), kind=kLoop, calls=%fused_computation.6 | loop fusion | flops 1835008 | bytes 2622476 | tf_op jit(solution)/shard_map/div | solution.py:392
  79.9 0.0 copy-done.2
  (5 shorter events, 0.0 us)
Async XLA Ops:
  11.8 29.4 %collective-permute-start.3 = (f32[3072,256]{1,0:T(8,128)}, f32[3072,256]{1,0:T(8,128)}, u32[]{:S(2)}, u32[]{:S(2)}) collective-permute-start(f32[3072,256]{1,0:T(8,128)} %get-tuple-element.26), channel_id=1, source_target_pairs={{0,8},{8,0},{16,24},{24,16},{32,40},{40,32},{48,56},{56,48},{64,72... | collective-permute-start | bytes 9437192 | tf_op jit(solution)/shard_map/ppermute | solution.py:274
  11.9 9.1 %collective-permute-start = (f32[1024,256]{1,0:T(8,128)S(1)}, f32[1024,256]{1,0:T(8,128)S(1)}, u32[]{:S(2)}, u32[]{:S(2)}) collective-permute-start(f32[1024,256]{1,0:T(8,128)S(1)} %get-tuple-element.25), channel_id=1, source_target_pairs={{0,8},{8,0},{16,24},{24,16},{32,40},{40,32},{48,56},{56,48},{64,72... | collective-permute-start | bytes 3145736 | tf_op jit(solution)/shard_map/ppermute | solution.py:274
  12.5 20.1 %collective-permute-start.6 = (f16[544,256]{1,0:T(8,128)(2,1)S(1)}, f16[544,256]{1,0:T(8,128)(2,1)S(1)}, u32[]{:S(2)}, u32[]{:S(2)}) collective-permute-start(f16[544,256]{1,0:T(8,128)(2,1)S(1)} %multiply_convert_fusion.1), channel_id=1, source_target_pairs={{0,4},{1,5},{2,6},{3,7},{4,0},{5,1},{6,2},{7,3},{8,12},{9,13},{10,... | collective-permute-start | bytes 835592 | tf_op jit(solution)/shard_map/ppermute | solution.py:274
  18.8 13.7 %collective-permute-start.5 = (f16[544,256]{1,0:T(8,128)(2,1)S(1)}, f16[544,256]{1,0:T(8,128)(2,1)S(1)}, u32[]{:S(2)}, u32[]{:S(2)}) collective-permute-start(f16[544,256]{1,0:T(8,128)(2,1)S(1)} %multiply_convert_fusion.2), channel_id=1, source_target_pairs={{0,6},{1,7},{2,0},{3,1},{4,2},{5,3},{6,4},{7,5},{8,14},{9,15},{10,... | collective-permute-start | bytes 835592 | tf_op jit(solution)/shard_map/ppermute | solution.py:274
  19.2 13.3 %collective-permute-start.4 = (f16[544,256]{1,0:T(8,128)(2,1)S(1)}, f16[544,256]{1,0:T(8,128)(2,1)S(1)}, u32[]{:S(2)}, u32[]{:S(2)}) collective-permute-start(f16[544,256]{1,0:T(8,128)(2,1)S(1)} %multiply_convert_fusion.3), channel_id=1, source_target_pairs={{0,2},{1,3},{2,4},{3,5},{4,6},{5,7},{6,0},{7,1},{8,10},{9,11},{10,... | collective-permute-start | bytes 835592 | tf_op jit(solution)/shard_map/ppermute | solution.py:274
  21.3 16.5 %collective-permute-start.2 = (f16[512,256]{1,0:T(8,128)(2,1)S(1)}, f16[512,256]{1,0:T(8,128)(2,1)S(1)}, u32[]{:S(2)}, u32[]{:S(2)}) collective-permute-start(f16[512,256]{1,0:T(8,128)(2,1)S(1)} %get-tuple-element.44), channel_id=1, source_target_pairs={{0,96},{8,104},{16,112},{24,120},{32,0},{40,8},{48,16},{56,24},{64... | collective-permute-start | bytes 786440 | tf_op jit(solution)/shard_map/ppermute | solution.py:274
  32.5 8.7 %collective-permute-start.1 = (f16[512,256]{1,0:T(8,128)(2,1)S(1)}, f16[512,256]{1,0:T(8,128)(2,1)S(1)}, u32[]{:S(2)}, u32[]{:S(2)}) collective-permute-start(f16[512,256]{1,0:T(8,128)(2,1)S(1)} %get-tuple-element.45), channel_id=1, source_target_pairs={{0,32},{8,40},{16,48},{24,56},{32,64},{40,72},{48,80},{56,88},{64,... | collective-permute-start | bytes 786440 | tf_op jit(solution)/shard_map/ppermute | solution.py:274
  41.2 2.7 %copy-start = (f16[512,256]{1,0:T(8,128)(2,1)}, f16[512,256]{1,0:T(8,128)(2,1)S(1)}, u32[]{:S(2)}) copy-start(f16[512,256]{1,0:T(8,128)(2,1)S(1)} %collective-permute-done.1) | copy-start | bytes 786436
  41.3 8.2 %collective-permute-start.9 = (f16[272,256]{1,0:T(8,128)(2,1)S(1)}, f16[272,256]{1,0:T(8,128)(2,1)S(1)}, u32[]{:S(2)}, u32[]{:S(2)}) collective-permute-start(f16[272,256]{1,0:T(8,128)(2,1)S(1)} %add_convert_fusion.3), channel_id=1, source_target_pairs={{0,1},{1,0},{2,3},{3,2},{4,5},{5,4},{6,7},{7,6},{8,9},{9,8},{10,11... | collective-permute-start | bytes 417800 | tf_op jit(solution)/shard_map/ppermute | solution.py:274
  46.5 13.0 %collective-permute-start.8 = (f16[1024,256]{1,0:T(8,128)(2,1)S(1)}, f16[1024,256]{1,0:T(8,128)(2,1)S(1)}, u32[]{:S(2)}, u32[]{:S(2)}) collective-permute-start(f16[1024,256]{1,0:T(8,128)(2,1)S(1)} %get-tuple-element.42), channel_id=1, source_target_pairs={{0,96},{8,104},{16,112},{24,120},{32,0},{40,8},{48,16},{56,24},{64... | collective-permute-start | bytes 1572872 | tf_op jit(solution)/shard_map/ppermute | solution.py:274
  49.5 13.5 %collective-permute-start.7 = (f16[1024,256]{1,0:T(8,128)(2,1)S(1)}, f16[1024,256]{1,0:T(8,128)(2,1)S(1)}, u32[]{:S(2)}, u32[]{:S(2)}) collective-permute-start(f16[1024,256]{1,0:T(8,128)(2,1)S(1)} %get-tuple-element.43), channel_id=1, source_target_pairs={{0,32},{8,40},{16,48},{24,56},{32,64},{40,72},{48,80},{56,88},{64,... | collective-permute-start | bytes 1572872 | tf_op jit(solution)/shard_map/ppermute | solution.py:274
  49.6 3.7 %collective-permute-start.11 = (f32[1,256]{1,0:T(1,128)S(1)}, f32[1,256]{1,0:T(1,128)S(1)}, u32[]{:S(2)}, u32[]{:S(2)}) collective-permute-start(f32[1,256]{1,0:T(1,128)S(1)} %slice_multiply_fusion.1), channel_id=1, source_target_pairs={{0,8},{8,0},{16,24},{24,16},{32,40},{40,32},{48,56},{56,48},{64,72... | collective-permute-start | bytes 3080 | tf_op jit(solution)/shard_map/ppermute | solution.py:274
  51.8 7.5 %collective-permute-start.10 = (f16[256,256]{1,0:T(8,128)(2,1)S(1)}, f16[256,256]{1,0:T(8,128)(2,1)S(1)}, u32[]{:S(2)}, u32[]{:S(2)}) collective-permute-start(f16[256,256]{1,0:T(8,128)(2,1)S(1)} %divide_convert_fusion), channel_id=1, source_target_pairs={{0,1},{1,0},{2,3},{3,2},{4,5},{5,4},{6,7},{7,6},{8,9},{9,8},{10,11... | collective-permute-start | bytes 393224 | tf_op jit(solution)/shard_map/ppermute | solution.py:274
  53.3 3.6 %collective-permute-start.12 = (f32[1,256]{1,0:T(1,128)S(1)}, f32[1,256]{1,0:T(1,128)S(1)}, u32[]{:S(2)}, u32[]{:S(2)}) collective-permute-start(f32[1,256]{1,0:T(1,128)S(1)} %fusion.2), channel_id=1, source_target_pairs={{0,16},{8,24},{16,0},{24,8},{32,48},{40,56},{48,32},{56,40},{64,80... | collective-permute-start | bytes 3080 | tf_op jit(solution)/shard_map/ppermute | solution.py:274
  53.4 18.2 %copy-start.1 = (f32[2048,256]{1,0:T(8,128)S(1)}, f32[2048,256]{1,0:T(8,128)}, u32[]{:S(2)}) copy-start(f32[2048,256]{1,0:T(8,128)} %get-tuple-element.22) | copy-start | bytes 6291460
  63.1 13.1 %collective-permute-start.14 = (f16[512,256]{1,0:T(8,128)(2,1)S(1)}, f16[512,256]{1,0:T(8,128)(2,1)S(1)}, u32[]{:S(2)}, u32[]{:S(2)}) collective-permute-start(f16[512,256]{1,0:T(8,128)(2,1)S(1)} %pad_add_fusion), channel_id=1, source_target_pairs={{0,2},{1,3},{2,4},{3,5},{4,6},{5,7},{6,0},{7,1},{8,10},{9,11},{10,... | collective-permute-start | bytes 786440 | tf_op jit(solution)/shard_map/ppermute | solution.py:274
  64.2 11.9 %collective-permute-start.13 = (f16[512,256]{1,0:T(8,128)(2,1)S(1)}, f16[512,256]{1,0:T(8,128)(2,1)S(1)}, u32[]{:S(2)}, u32[]{:S(2)}) collective-permute-start(f16[512,256]{1,0:T(8,128)(2,1)S(1)} %pad_add_fusion), channel_id=1, source_target_pairs={{0,6},{1,7},{2,0},{3,1},{4,2},{5,3},{6,4},{7,5},{8,14},{9,15},{10,... | collective-permute-start | bytes 786440 | tf_op jit(solution)/shard_map/ppermute | solution.py:274
  66.4 10.4 %collective-permute-start.15 = (f16[512,256]{1,0:T(8,128)(2,1)S(1)}, f16[512,256]{1,0:T(8,128)(2,1)S(1)}, u32[]{:S(2)}, u32[]{:S(2)}) collective-permute-start(f16[512,256]{1,0:T(8,128)(2,1)S(1)} %pad_add_fusion), channel_id=1, source_target_pairs={{0,4},{1,5},{2,6},{3,7},{4,0},{5,1},{6,2},{7,3},{8,12},{9,13},{10,... | collective-permute-start | bytes 786440 | tf_op jit(solution)/shard_map/ppermute | solution.py:274
  67.7 3.6 %collective-permute-start.17 = (f32[1,256]{1,0:T(1,128)S(1)}, f32[1,256]{1,0:T(1,128)S(1)}, u32[]{:S(2)}, u32[]{:S(2)}) collective-permute-start(f32[1,256]{1,0:T(1,128)S(1)} %add.205), channel_id=1, source_target_pairs={{0,32},{8,40},{16,48},{24,56},{32,0},{40,8},{48,16},{56,24},{64,96... | collective-permute-start | bytes 3080 | tf_op jit(solution)/shard_map/ppermute | solution.py:274
  69.1 7.8 %collective-permute-start.16 = (f16[512,256]{1,0:T(8,128)(2,1)S(1)}, f16[512,256]{1,0:T(8,128)(2,1)S(1)}, u32[]{:S(2)}, u32[]{:S(2)}) collective-permute-start(f16[512,256]{1,0:T(8,128)(2,1)S(1)} %add_convert_fusion.2), channel_id=1, source_target_pairs={{0,16},{8,24},{16,0},{24,8},{32,48},{40,56},{48,32},{56,40},{64,80... | collective-permute-start | bytes 786440 | tf_op jit(solution)/shard_map/ppermute | solution.py:274
  71.3 4.8 %collective-permute-start.18 = (f32[1,256]{1,0:T(1,128)S(1)}, f32[1,256]{1,0:T(1,128)S(1)}, u32[]{:S(2)}, u32[]{:S(2)}) collective-permute-start(f32[1,256]{1,0:T(1,128)S(1)} %add.235), channel_id=1, source_target_pairs={{0,96},{8,104},{16,112},{24,120},{32,64},{40,72},{48,80},{56,88},{... | collective-permute-start | bytes 3080 | tf_op jit(solution)/shard_map/ppermute | solution.py:274
  76.8 3.1 %copy-start.2 = (f32[2048,256]{1,0:T(8,128)}, f32[2048,256]{1,0:T(8,128)S(1)}, u32[]{:S(2)}) copy-start(f32[2048,256]{1,0:T(8,128)S(1)} %convert_dynamic-update-slice_fusion) | copy-start | bytes 6291460

commit v7 on v6

--- a/solution.py
+++ b/solution.py
@@ -374,7 +374,8 @@
         above = lax.dynamic_slice_in_dim(word_above, at, word_rows, 0)
         return (here + far) * WORD_SCALE + to_float(below) + to_float(above)
 
-    word_far = to_x_lo(to_half(word_half(1 - x_lo)))
+    word_mine, word_far = meet(word_half(x_lo), to_half(word_half(1 - x_lo)))
+    word_far = to_x_lo(word_far)
     doc_here = rows_around(jnp.where(x_hi == 0, doc_block, doc_far), 0, own_rows) + rows_around(
         jnp.where(x_hi == 0, doc_far, doc_block), own_rows, 0
     )
@@ -385,7 +386,7 @@
         at = (z + step) % N_Z * (N_X_HI * own_rows)
         doc_next = lax.dynamic_update_slice_in_dim(doc_next, to_float(value), at, 0)
     row_count = word_topics.shape[0] // n_docs
-    word_sums = (word_half(x_lo) + to_float(word_far)) / WORD_SCALE
+    word_sums = (word_mine + to_float(word_far)) / WORD_SCALE
     vocab_total = word_topics.shape[0] * n_vocab
     own_words = lax.dynamic_slice_in_dim(word_topics, docs_index * row_count, row_count, 0)
     word_scaled = own_words.astype(jnp.float32) * word_sums + prior_word

time: 79.8 us -> 77.7 us (0.974)
  waiting for transfers between devices: 25.3 us -> 17.9 us
  starting transfers between devices: 32.5 us -> 37.9 us
  Pallas kernels: 10.5 us -> 11.6 us
    ppermute x19, waiting for transfers between devices: 25.3 us -> 17.9 us  [moves(): lax.ppermute(value, axis, [(n, move(n) % size) for n in range(size)])]
    ppermute x19, starting transfers between devices: 32.5 us -> 37.9 us  [moves(): lax.ppermute(value, axis, [(n, move(n) % size) for n in range(size)])]
    pallas_call x1, Pallas kernels: 10.5 us -> 11.6 us  [run_tiles(): pl.pallas_call(tiles_kernel, out_shape=((doc_part,) * N_Z, (first_part, l...]
    div x1, other arithmetic: 3.06 us -> 2.1 us  [on_device(): word_next = vocab_total * word_scaled / (column + vocab_total * prior_word)]
  transfers between devices with their start and end apart: 19 -> 19, of which waited for: 9 -> 8; matrix products, arithmetic and copies ran while one was open for 8% -> 9% of each run, Pallas kernels for 0% -> 0%
where the time goes in v7:
time: 77.7 us; the launch traced here: 78.4 us
  starting transfers between devices  37.9 us (49%)
  waiting for transfers between devices  17.9 us (23%)
  Pallas kernels  11.6 us (15%)
  other arithmetic  9.41 us (12%)
  between operations  1.47 us (2%)
    ppermute x19, starting transfers between devices, moves(): lax.ppermute(value, axis, [(n, move(n) % size) for n in range(size)])  37.9 us
    ppermute x19, waiting for transfers between devices, moves(): lax.ppermute(value, axis, [(n, move(n) % size) for n in range(size)])  17.9 us
    pallas_call x1, Pallas kernels, run_tiles(): pl.pallas_call(tiles_kernel, out_shape=((doc_part,) * N_Z, (first_part, l...  11.6 us
    convert_element_type x7, other arithmetic, to_half(): return value.astype(jnp.float16)  5.62 us
    div x1, other arithmetic, on_device(): word_next = vocab_total * word_scaled / (column + vocab_total * prior_word)  2.1 us
  transfers between devices with their start and end apart: 19, of which 8 were waited for; matrix products, arithmetic and copies ran while one was open for 9% of the time, Pallas kernels for 0%

profile of v7, /device:TPU:0, one launch (start us, length us, event | category | flops | bytes accessed | tf_op | source)
XLA Modules:
  0.0 78.4 jit_solution(11630347334730917554)
XLA Ops:
  1.3 11.6 %tiles.1 = (f32[544,256]{1,0:T(8,128)S(1)}, f32[544,256]{1,0:T(8,128)S(1)}, f32[544,256]{1,0:T(8,128)S(1)}, f32[544,256]{1,0:T(8,128)S(1)}, f32[1024,256]{1,0:T(...) custom-call(s32[1,1,96]{2,1,0:T(1,128)} %pairs_hbm.1, ...), custom_call_target="tpu_custom_call" | custom-call | tf_op jit(solution)/shard_map/tiles/pallas_call | solution.py:233
  12.9 0.1 collective-permute-start.3
  13.0 0.5 collective-permute-start
  13.5 0.1 multiply_convert_fusion.1
  13.6 4.0 %collective-permute-start.6 = (f16[544,256]{1,0:T(8,128)(2,1)S(1)}, f16[544,256]{1,0:T(8,128)(2,1)S(1)}, u32[]{:S(2)}, u32[]{:S(2)}) collective-permute-start(f16[544,256]{1,0:T(8,128)(2,1)S(1)} %multiply_convert_fusion.1), channel_id=1, source_target_pairs={{0,4},{1,5},{2,6},{3,7},{4,0},{5,1},{6,2},{7,3},{8,12},{9,13},{10,... | collective-permute-start | bytes 835592 | tf_op jit(solution)/shard_map/ppermute | solution.py:274
  17.6 0.1 multiply_convert_fusion.2
  17.7 5.8 %collective-permute-start.5 = (f16[544,256]{1,0:T(8,128)(2,1)S(1)}, f16[544,256]{1,0:T(8,128)(2,1)S(1)}, u32[]{:S(2)}, u32[]{:S(2)}) collective-permute-start(f16[544,256]{1,0:T(8,128)(2,1)S(1)} %multiply_convert_fusion.2), channel_id=1, source_target_pairs={{0,6},{1,7},{2,0},{3,1},{4,2},{5,3},{6,4},{7,5},{8,14},{9,15},{10,... | collective-permute-start | bytes 835592 | tf_op jit(solution)/shard_map/ppermute | solution.py:274
  23.5 0.1 multiply_convert_fusion.3
  23.6 0.9 %collective-permute-start.4 = (f16[544,256]{1,0:T(8,128)(2,1)S(1)}, f16[544,256]{1,0:T(8,128)(2,1)S(1)}, u32[]{:S(2)}, u32[]{:S(2)}) collective-permute-start(f16[544,256]{1,0:T(8,128)(2,1)S(1)} %multiply_convert_fusion.3), channel_id=1, source_target_pairs={{0,2},{1,3},{2,4},{3,5},{4,6},{5,7},{6,0},{7,1},{8,10},{9,11},{10,... | collective-permute-start | bytes 835592 | tf_op jit(solution)/shard_map/ppermute | solution.py:274
  24.5 0.0 collective-permute-done
  24.5 0.2 multiply_convert_fusion
  24.7 0.1 fusion.3
  24.8 0.1 collective-permute-start.2
  24.9 0.0 collective-permute-done.6
  24.9 9.1 %collective-permute-start.1 = (f16[512,256]{1,0:T(8,128)(2,1)S(1)}, f16[512,256]{1,0:T(8,128)(2,1)S(1)}, u32[]{:S(2)}, u32[]{:S(2)}) collective-permute-start(f16[512,256]{1,0:T(8,128)(2,1)S(1)} %get-tuple-element.51), channel_id=1, source_target_pairs={{0,32},{8,40},{16,48},{24,56},{32,64},{40,72},{48,80},{56,88},{64,... | collective-permute-start | bytes 786440 | tf_op jit(solution)/shard_map/ppermute | solution.py:274
  34.0 3.2 %collective-permute-done.5 = f16[544,256]{1,0:T(8,128)(2,1)S(1)} collective-permute-done((f16[544,256]{1,0:T(8,128)(2,1)S(1)}, f16[544,256]{1,0:T(8,128)(2,1)S(1)}, u32[]{:S(2)}, u32[]{:S(2)}) %collective-permute-start.5) | collective-permute-done | bytes 278560 | tf_op jit(solution)/shard_map/ppermute | solution.py:274
  37.2 0.0 collective-permute-done.4
  37.2 0.0 collective-permute-done.2
  37.2 0.9 %collective-permute-done.1 = f16[512,256]{1,0:T(8,128)(2,1)S(1)} collective-permute-done((f16[512,256]{1,0:T(8,128)(2,1)S(1)}, f16[512,256]{1,0:T(8,128)(2,1)S(1)}, u32[]{:S(2)}, u32[]{:S(2)}) %collective-permute-start.1) | collective-permute-done | bytes 262176 | tf_op jit(solution)/shard_map/ppermute | solution.py:274
  38.2 0.0 copy-start
  38.2 0.0 collective-permute-done.3
  38.2 0.1 add_convert_fusion.3
  38.3 5.6 %collective-permute-start.9 = (f16[272,256]{1,0:T(8,128)(2,1)S(1)}, f16[272,256]{1,0:T(8,128)(2,1)S(1)}, u32[]{:S(2)}, u32[]{:S(2)}) collective-permute-start(f16[272,256]{1,0:T(8,128)(2,1)S(1)} %add_convert_fusion.3), channel_id=1, source_target_pairs={{0,1},{1,0},{2,3},{3,2},{4,5},{5,4},{6,7},{7,6},{8,9},{9,8},{10,11... | collective-permute-start | bytes 417800 | tf_op jit(solution)/shard_map/ppermute | solution.py:274
  43.8 0.0 copy-done
  43.8 2.6 %add_convert_fusion = (f16[1024,256]{1,0:T(8,128)(2,1)S(1)}, f16[1024,256]{1,0:T(8,128)(2,1)S(1)}) fusion(f32[3072,256]{1,0:T(8,128)} %collective-permute-done.3, f32[3072,256]{1,0:T(8,128)} %get-tuple-element.25, f16[512,256]{1,0:T(8,128)(2,1)S(1)} %collective-permute-done.2, f16[512,256]{1,0:T(8,128)(2,1)} %copy-done), kind=kLoop, calls=%fused_computation | loop fusion | flops 2621440 | bytes 5767168 | tf_op jit(solution)/shard_map/convert_element_type | solution.py:278
  46.4 1.0 %collective-permute-start.8 = (f16[1024,256]{1,0:T(8,128)(2,1)S(1)}, f16[1024,256]{1,0:T(8,128)(2,1)S(1)}, u32[]{:S(2)}, u32[]{:S(2)}) collective-permute-start(f16[1024,256]{1,0:T(8,128)(2,1)S(1)} %get-tuple-element.48), channel_id=1, source_target_pairs={{0,96},{8,104},{16,112},{24,120},{32,0},{40,8},{48,16},{56,24},{64... | collective-permute-start | bytes 1572872 | tf_op jit(solution)/shard_map/ppermute | solution.py:274
  47.5 1.1 %collective-permute-start.7 = (f16[1024,256]{1,0:T(8,128)(2,1)S(1)}, f16[1024,256]{1,0:T(8,128)(2,1)S(1)}, u32[]{:S(2)}, u32[]{:S(2)}) collective-permute-start(f16[1024,256]{1,0:T(8,128)(2,1)S(1)} %get-tuple-element.49), channel_id=1, source_target_pairs={{0,32},{8,40},{16,48},{24,56},{32,64},{40,72},{48,80},{56,88},{64,... | collective-permute-start | bytes 1572872 | tf_op jit(solution)/shard_map/ppermute | solution.py:274
  48.5 0.0 collective-permute-done.9
  48.5 0.1 add_multiply_fusion
  48.6 0.1 collective-permute-start.11
  48.7 1.0 %fusion.1 = f32[256]{0:T(256)S(1)} fusion(f32[272,256]{1,0:T(8,128)S(1)} %add_multiply_fusion, bf16[2048,256]{1,0:T(8,128)(2,1)} %doc_hbm.1, s32[]{:T(128)S(6)} %select_n.94), kind=kLoop, calls=%fused_computation.19 | loop fusion | flops 261888 | bytes 394244 | tf_op jit(solution)/shard_map/reduce_sum | solution.py:359
  49.8 1.0 %divide_convert_fusion = f16[256,256]{1,0:T(8,128)(2,1)S(1)} fusion(f32[272,256]{1,0:T(8,128)S(1)} %add_multiply_fusion, f32[256]{0:T(256)S(1)} %fusion.1, bf16[2048,256]{1,0:T(8,128)(2,1)} %doc_hbm.1, s32[]{:T(128)S(6)} %select_n.94), kind=kLoop, calls=%fused_computation.18 | loop fusion | flops 393216 | bytes 525316 | tf_op jit(solution)/shard_map/convert_element_type | solution.py:278
  50.8 2.0 %collective-permute-start.10 = (f16[256,256]{1,0:T(8,128)(2,1)S(1)}, f16[256,256]{1,0:T(8,128)(2,1)S(1)}, u32[]{:S(2)}, u32[]{:S(2)}) collective-permute-start(f16[256,256]{1,0:T(8,128)(2,1)S(1)} %divide_convert_fusion), channel_id=1, source_target_pairs={{0,1},{1,0},{2,3},{3,2},{4,5},{5,4},{6,7},{7,6},{8,9},{9,8},{10,11... | collective-permute-start | bytes 393224 | tf_op jit(solution)/shard_map/ppermute | solution.py:274
  52.8 0.0 collective-permute-done.11
  52.8 1.4 %collective-permute-start.12 = (f32[1,256]{1,0:T(1,128)S(1)}, f32[1,256]{1,0:T(1,128)S(1)}, u32[]{:S(2)}, u32[]{:S(2)}) collective-permute-start(f32[1,256]{1,0:T(1,128)S(1)} %fusion.2), channel_id=1, source_target_pairs={{0,16},{8,24},{16,0},{24,8},{32,48},{40,56},{48,32},{56,40},{64,80... | collective-permute-start | bytes 3080 | tf_op jit(solution)/shard_map/ppermute | solution.py:274
  54.2 3.9 %collective-permute-done.12 = f32[1,256]{1,0:T(1,128)S(1)} collective-permute-done((f32[1,256]{1,0:T(1,128)S(1)}, f32[1,256]{1,0:T(1,128)S(1)}, u32[]{:S(2)}, u32[]{:S(2)}) %collective-permute-start.12) | collective-permute-done | bytes 1056 | tf_op jit(solution)/shard_map/ppermute | solution.py:274
  58.1 0.2 collective-permute-done.10
  58.3 0.4 collective-permute-done.8
  58.7 3.1 %collective-permute-done.7 = f16[1024,256]{1,0:T(8,128)(2,1)S(1)} collective-permute-done((f16[1024,256]{1,0:T(8,128)(2,1)S(1)}, f16[1024,256]{1,0:T(8,128)(2,1)S(1)}, u32[]{:S(2)}, u32[]{:S(2)}) %collective-permute-start.7) | collective-permute-done | bytes 524320 | tf_op jit(solution)/shard_map/ppermute | solution.py:274
  61.8 0.1 broadcast_select_fusion.1
  61.9 0.1 pad_add_fusion
  61.9 0.0 copy-start.1
  61.9 3.6 %collective-permute-start.14 = (f16[512,256]{1,0:T(8,128)(2,1)S(1)}, f16[512,256]{1,0:T(8,128)(2,1)S(1)}, u32[]{:S(2)}, u32[]{:S(2)}) collective-permute-start(f16[512,256]{1,0:T(8,128)(2,1)S(1)} %pad_add_fusion), channel_id=1, source_target_pairs={{0,2},{1,3},{2,4},{3,5},{4,6},{5,7},{6,0},{7,1},{8,10},{9,11},{10,... | collective-permute-start | bytes 786440 | tf_op jit(solution)/shard_map/ppermute | solution.py:274
  65.5 0.1 collective-permute-start.13
  65.6 2.1 %collective-permute-start.15 = (f16[512,256]{1,0:T(8,128)(2,1)S(1)}, f16[512,256]{1,0:T(8,128)(2,1)S(1)}, u32[]{:S(2)}, u32[]{:S(2)}) collective-permute-start(f16[512,256]{1,0:T(8,128)(2,1)S(1)} %pad_add_fusion), channel_id=1, source_target_pairs={{0,4},{1,5},{2,6},{3,7},{4,0},{5,1},{6,2},{7,3},{8,12},{9,13},{10,... | collective-permute-start | bytes 786440 | tf_op jit(solution)/shard_map/ppermute | solution.py:274
  67.7 0.0 collective-permute-start.17
  67.7 1.7 %add_convert_fusion.2 = (f16[512,256]{1,0:T(8,128)(2,1)S(1)}, f32[512,256]{1,0:T(8,128)S(1)}) fusion(f32[3072,256]{1,0:T(8,128)} %collective-permute-done.3, s32[]{:T(128)S(6)} %select_n.113, f32[3072,256]{1,0:T(8,128)} %get-tuple-element.25, f16[1024,256]{1,0:T(8,128)(2,1)S(1)} %collective-permute-done.8, s32[]{:T(128)S(6)} %select_n.114, ...), kind=kLoop, calls=%fused_computation.7 | loop fusion | flops 1703936 | bytes 3932176 | tf_op jit(solution)/shard_map/convert_element_type | solution.py:278
  69.5 0.1 collective-permute-start.16
  69.6 1.7 %collective-permute-done.17 = f32[1,256]{1,0:T(1,128)S(1)} collective-permute-done((f32[1,256]{1,0:T(1,128)S(1)}, f32[1,256]{1,0:T(1,128)S(1)}, u32[]{:S(2)}, u32[]{:S(2)}) %collective-permute-start.17) | collective-permute-done | bytes 1056 | tf_op jit(solution)/shard_map/ppermute | solution.py:274
  71.3 0.3 collective-permute-start.18
  71.6 0.0 copy-done.1
  71.6 0.1 convert_dynamic-update-slice_fusion.3
  71.6 4.4 %collective-permute-done.18 = f32[1,256]{1,0:T(1,128)S(1)} collective-permute-done((f32[1,256]{1,0:T(1,128)S(1)}, f32[1,256]{1,0:T(1,128)S(1)}, u32[]{:S(2)}, u32[]{:S(2)}) %collective-permute-start.18) | collective-permute-done | bytes 1056 | tf_op jit(solution)/shard_map/ppermute | solution.py:274
  76.1 0.0 collective-permute-done.13
  76.1 0.1 convert_dynamic-update-slice_fusion.2
  76.1 0.0 collective-permute-done.14
  76.1 0.1 convert_dynamic-update-slice_fusion.1
  76.2 0.0 collective-permute-done.15
  76.2 0.1 convert_dynamic-update-slice_fusion
  76.3 0.0 copy-start.2
  76.3 0.0 collective-permute-done.16
  76.3 2.1 %multiply_divide_fusion = f32[512,256]{1,0:T(8,128)} fusion(f32[512,256]{1,0:T(8,128)S(1)} %get-tuple-element.43, f16[512,256]{1,0:T(8,128)(2,1)S(1)} %collective-permute-done.16, f32[256]{0:T(256)S(1)} %bitcast.7, bf16[8192,256]{1,0:T(8,128)(2,1)} %word_hbm.1, s32[]{:T(128)S(6)} %select_n.108), kind=kLoop, calls=%fused_computation.6 | loop fusion | flops 1048576 | bytes 1573892 | tf_op jit(solution)/shard_map/div | solution.py:393
  78.4 0.0 copy-done.2
  (5 shorter events, 0.0 us)
Async XLA Ops:
  12.9 25.2 %collective-permute-start.3 = (f32[3072,256]{1,0:T(8,128)}, f32[3072,256]{1,0:T(8,128)}, u32[]{:S(2)}, u32[]{:S(2)}) collective-permute-start(f32[3072,256]{1,0:T(8,128)} %get-tuple-element.28), channel_id=1, source_target_pairs={{0,8},{8,0},{16,24},{24,16},{32,40},{40,32},{48,56},{56,48},{64,72... | collective-permute-start | bytes 9437192 | tf_op jit(solution)/shard_map/ppermute | solution.py:274
  13.0 11.5 %collective-permute-start = (f32[1024,256]{1,0:T(8,128)S(1)}, f32[1024,256]{1,0:T(8,128)S(1)}, u32[]{:S(2)}, u32[]{:S(2)}) collective-permute-start(f32[1024,256]{1,0:T(8,128)S(1)} %get-tuple-element.27), channel_id=1, source_target_pairs={{0,8},{8,0},{16,24},{24,16},{32,40},{40,32},{48,56},{56,48},{64,72... | collective-permute-start | bytes 3145736 | tf_op jit(solution)/shard_map/ppermute | solution.py:274
  13.6 11.3 %collective-permute-start.6 = (f16[544,256]{1,0:T(8,128)(2,1)S(1)}, f16[544,256]{1,0:T(8,128)(2,1)S(1)}, u32[]{:S(2)}, u32[]{:S(2)}) collective-permute-start(f16[544,256]{1,0:T(8,128)(2,1)S(1)} %multiply_convert_fusion.1), channel_id=1, source_target_pairs={{0,4},{1,5},{2,6},{3,7},{4,0},{5,1},{6,2},{7,3},{8,12},{9,13},{10,... | collective-permute-start | bytes 835592 | tf_op jit(solution)/shard_map/ppermute | solution.py:274
  17.7 19.5 %collective-permute-start.5 = (f16[544,256]{1,0:T(8,128)(2,1)S(1)}, f16[544,256]{1,0:T(8,128)(2,1)S(1)}, u32[]{:S(2)}, u32[]{:S(2)}) collective-permute-start(f16[544,256]{1,0:T(8,128)(2,1)S(1)} %multiply_convert_fusion.2), channel_id=1, source_target_pairs={{0,6},{1,7},{2,0},{3,1},{4,2},{5,3},{6,4},{7,5},{8,14},{9,15},{10,... | collective-permute-start | bytes 835592 | tf_op jit(solution)/shard_map/ppermute | solution.py:274
  23.6 13.6 %collective-permute-start.4 = (f16[544,256]{1,0:T(8,128)(2,1)S(1)}, f16[544,256]{1,0:T(8,128)(2,1)S(1)}, u32[]{:S(2)}, u32[]{:S(2)}) collective-permute-start(f16[544,256]{1,0:T(8,128)(2,1)S(1)} %multiply_convert_fusion.3), channel_id=1, source_target_pairs={{0,2},{1,3},{2,4},{3,5},{4,6},{5,7},{6,0},{7,1},{8,10},{9,11},{10,... | collective-permute-start | bytes 835592 | tf_op jit(solution)/shard_map/ppermute | solution.py:274
  24.8 12.4 %collective-permute-start.2 = (f16[512,256]{1,0:T(8,128)(2,1)S(1)}, f16[512,256]{1,0:T(8,128)(2,1)S(1)}, u32[]{:S(2)}, u32[]{:S(2)}) collective-permute-start(f16[512,256]{1,0:T(8,128)(2,1)S(1)} %get-tuple-element.50), channel_id=1, source_target_pairs={{0,96},{8,104},{16,112},{24,120},{32,0},{40,8},{48,16},{56,24},{64... | collective-permute-start | bytes 786440 | tf_op jit(solution)/shard_map/ppermute | solution.py:274
  24.9 13.3 %collective-permute-start.1 = (f16[512,256]{1,0:T(8,128)(2,1)S(1)}, f16[512,256]{1,0:T(8,128)(2,1)S(1)}, u32[]{:S(2)}, u32[]{:S(2)}) collective-permute-start(f16[512,256]{1,0:T(8,128)(2,1)S(1)} %get-tuple-element.51), channel_id=1, source_target_pairs={{0,32},{8,40},{16,48},{24,56},{32,64},{40,72},{48,80},{56,88},{64,... | collective-permute-start | bytes 786440 | tf_op jit(solution)/shard_map/ppermute | solution.py:274
  38.2 5.7 %copy-start = (f16[512,256]{1,0:T(8,128)(2,1)}, f16[512,256]{1,0:T(8,128)(2,1)S(1)}, u32[]{:S(2)}) copy-start(f16[512,256]{1,0:T(8,128)(2,1)S(1)} %collective-permute-done.1) | copy-start | bytes 786436
  38.3 10.3 %collective-permute-start.9 = (f16[272,256]{1,0:T(8,128)(2,1)S(1)}, f16[272,256]{1,0:T(8,128)(2,1)S(1)}, u32[]{:S(2)}, u32[]{:S(2)}) collective-permute-start(f16[272,256]{1,0:T(8,128)(2,1)S(1)} %add_convert_fusion.3), channel_id=1, source_target_pairs={{0,1},{1,0},{2,3},{3,2},{4,5},{5,4},{6,7},{7,6},{8,9},{9,8},{10,11... | collective-permute-start | bytes 417800 | tf_op jit(solution)/shard_map/ppermute | solution.py:274
  46.4 12.3 %collective-permute-start.8 = (f16[1024,256]{1,0:T(8,128)(2,1)S(1)}, f16[1024,256]{1,0:T(8,128)(2,1)S(1)}, u32[]{:S(2)}, u32[]{:S(2)}) collective-permute-start(f16[1024,256]{1,0:T(8,128)(2,1)S(1)} %get-tuple-element.48), channel_id=1, source_target_pairs={{0,96},{8,104},{16,112},{24,120},{32,0},{40,8},{48,16},{56,24},{64... | collective-permute-start | bytes 1572872 | tf_op jit(solution)/shard_map/ppermute | solution.py:274
  47.5 14.3 %collective-permute-start.7 = (f16[1024,256]{1,0:T(8,128)(2,1)S(1)}, f16[1024,256]{1,0:T(8,128)(2,1)S(1)}, u32[]{:S(2)}, u32[]{:S(2)}) collective-permute-start(f16[1024,256]{1,0:T(8,128)(2,1)S(1)} %get-tuple-element.49), channel_id=1, source_target_pairs={{0,32},{8,40},{16,48},{24,56},{32,64},{40,72},{48,80},{56,88},{64,... | collective-permute-start | bytes 1572872 | tf_op jit(solution)/shard_map/ppermute | solution.py:274
  48.6 4.1 %collective-permute-start.11 = (f32[1,256]{1,0:T(1,128)S(1)}, f32[1,256]{1,0:T(1,128)S(1)}, u32[]{:S(2)}, u32[]{:S(2)}) collective-permute-start(f32[1,256]{1,0:T(1,128)S(1)} %slice_multiply_fusion.1), channel_id=1, source_target_pairs={{0,8},{8,0},{16,24},{24,16},{32,40},{40,32},{48,56},{56,48},{64,72... | collective-permute-start | bytes 3080 | tf_op jit(solution)/shard_map/ppermute | solution.py:274
  50.8 7.5 %collective-permute-start.10 = (f16[256,256]{1,0:T(8,128)(2,1)S(1)}, f16[256,256]{1,0:T(8,128)(2,1)S(1)}, u32[]{:S(2)}, u32[]{:S(2)}) collective-permute-start(f16[256,256]{1,0:T(8,128)(2,1)S(1)} %divide_convert_fusion), channel_id=1, source_target_pairs={{0,1},{1,0},{2,3},{3,2},{4,5},{5,4},{6,7},{7,6},{8,9},{9,8},{10,11... | collective-permute-start | bytes 393224 | tf_op jit(solution)/shard_map/ppermute | solution.py:274
  52.8 5.3 %collective-permute-start.12 = (f32[1,256]{1,0:T(1,128)S(1)}, f32[1,256]{1,0:T(1,128)S(1)}, u32[]{:S(2)}, u32[]{:S(2)}) collective-permute-start(f32[1,256]{1,0:T(1,128)S(1)} %fusion.2), channel_id=1, source_target_pairs={{0,16},{8,24},{16,0},{24,8},{32,48},{40,56},{48,32},{56,40},{64,80... | collective-permute-start | bytes 3080 | tf_op jit(solution)/shard_map/ppermute | solution.py:274
  61.9 9.6 %copy-start.1 = (f32[2048,256]{1,0:T(8,128)S(1)}, f32[2048,256]{1,0:T(8,128)}, u32[]{:S(2)}) copy-start(f32[2048,256]{1,0:T(8,128)} %get-tuple-element.24) | copy-start | bytes 6291460
  61.9 14.2 %collective-permute-start.14 = (f16[512,256]{1,0:T(8,128)(2,1)S(1)}, f16[512,256]{1,0:T(8,128)(2,1)S(1)}, u32[]{:S(2)}, u32[]{:S(2)}) collective-permute-start(f16[512,256]{1,0:T(8,128)(2,1)S(1)} %pad_add_fusion), channel_id=1, source_target_pairs={{0,2},{1,3},{2,4},{3,5},{4,6},{5,7},{6,0},{7,1},{8,10},{9,11},{10,... | collective-permute-start | bytes 786440 | tf_op jit(solution)/shard_map/ppermute | solution.py:274
  65.5 10.5 %collective-permute-start.13 = (f16[512,256]{1,0:T(8,128)(2,1)S(1)}, f16[512,256]{1,0:T(8,128)(2,1)S(1)}, u32[]{:S(2)}, u32[]{:S(2)}) collective-permute-start(f16[512,256]{1,0:T(8,128)(2,1)S(1)} %pad_add_fusion), channel_id=1, source_target_pairs={{0,6},{1,7},{2,0},{3,1},{4,2},{5,3},{6,4},{7,5},{8,14},{9,15},{10,... | collective-permute-start | bytes 786440 | tf_op jit(solution)/shard_map/ppermute | solution.py:274
  65.6 10.6 %collective-permute-start.15 = (f16[512,256]{1,0:T(8,128)(2,1)S(1)}, f16[512,256]{1,0:T(8,128)(2,1)S(1)}, u32[]{:S(2)}, u32[]{:S(2)}) collective-permute-start(f16[512,256]{1,0:T(8,128)(2,1)S(1)} %pad_add_fusion), channel_id=1, source_target_pairs={{0,4},{1,5},{2,6},{3,7},{4,0},{5,1},{6,2},{7,3},{8,12},{9,13},{10,... | collective-permute-start | bytes 786440 | tf_op jit(solution)/shard_map/ppermute | solution.py:274
  67.7 3.6 %collective-permute-start.17 = (f32[1,256]{1,0:T(1,128)S(1)}, f32[1,256]{1,0:T(1,128)S(1)}, u32[]{:S(2)}, u32[]{:S(2)}) collective-permute-start(f32[1,256]{1,0:T(1,128)S(1)} %add.205), channel_id=1, source_target_pairs={{0,32},{8,40},{16,48},{24,56},{32,0},{40,8},{48,16},{56,24},{64,96... | collective-permute-start | bytes 3080 | tf_op jit(solution)/shard_map/ppermute | solution.py:274
  69.5 6.9 %collective-permute-start.16 = (f16[512,256]{1,0:T(8,128)(2,1)S(1)}, f16[512,256]{1,0:T(8,128)(2,1)S(1)}, u32[]{:S(2)}, u32[]{:S(2)}) collective-permute-start(f16[512,256]{1,0:T(8,128)(2,1)S(1)} %get-tuple-element.44), channel_id=1, source_target_pairs={{0,16},{8,24},{16,0},{24,8},{32,48},{40,56},{48,32},{56,40},{64,80... | collective-permute-start | bytes 786440 | tf_op jit(solution)/shard_map/ppermute | solution.py:274
  71.3 4.8 %collective-permute-start.18 = (f32[1,256]{1,0:T(1,128)S(1)}, f32[1,256]{1,0:T(1,128)S(1)}, u32[]{:S(2)}, u32[]{:S(2)}) collective-permute-start(f32[1,256]{1,0:T(1,128)S(1)} %add.235), channel_id=1, source_target_pairs={{0,96},{8,104},{16,112},{24,120},{32,64},{40,72},{48,80},{56,88},{... | collective-permute-start | bytes 3080 | tf_op jit(solution)/shard_map/ppermute | solution.py:274
  76.3 2.1 %copy-start.2 = (f32[2048,256]{1,0:T(8,128)}, f32[2048,256]{1,0:T(8,128)S(1)}, u32[]{:S(2)}) copy-start(f32[2048,256]{1,0:T(8,128)S(1)} %convert_dynamic-update-slice_fusion) | copy-start | bytes 6291460
